TPU v7x, 32 devices: a whole 2x2x4 slice. The times are simulated.
32 devices in a mesh: shard: 8 (over z, x), ctx: 2 (over core), tp: 2 (over y).
Axes of the slice: x: 2, y: 2, z: 4, core: 2. Of those that a mesh axis runs over, the one named last changes fastest.
Arguments:
- tokens: bfloat16 [2, 8, 1024, 1280], P(None, 'shard', 'ctx'), may hold values from -6 to 6
- patch_meta: int32 [3, 2, 8, 1024], P(None, None, 'shard'), may hold values from -1 to 31, as said below
- attn_norm_gain: float32 [1280], replicated, may hold values from 0.5 to 1.5
- attn_norm_bias: float32 [1280], replicated, may hold values from -3 to 3
- qkv_weight: bfloat16 [3, 1280, 1280], P(None, 'shard', 'tp'), may hold values from -0.15625 to 0.15625
- qkv_bias: float32 [3, 1280], P(None, 'tp'), may hold values from -3 to 3
- proj_weight: bfloat16 [1280, 1280], P('tp', 'shard'), may hold values from -0.625 to 0.625
- proj_bias: float32 [1280], replicated, may hold values from -3 to 3
- mlp_norm_gain: float32 [1280], replicated, may hold values from 0.5 to 1.5
- mlp_norm_bias: float32 [1280], replicated, may hold values from -3 to 3
- fc1_weight: bfloat16 [1280, 5120], P('shard', 'tp'), may hold values from -0.15625 to 0.15625
- fc1_bias: float32 [5120], P('tp'), may hold values from -3 to 3
- fc2_weight: bfloat16 [5120, 1280], P('tp', 'shard'), may hold values from -0.078125 to 0.078125
- fc2_bias: float32 [1280], replicated, may hold values from -3 to 3
- cotangent: bfloat16 [2, 8, 1024, 1280], P(None, 'shard', 'ctx'), may hold values from -6 to 6
Outputs:
- block_output: bfloat16 [2, 8, 1024, 1280], P(None, 'shard', 'ctx')
- input_grad: float32 [2, 8, 1024, 1280], P(None, 'shard', 'ctx')
- grad_attn_norm_gain: float32 [1280], replicated
- grad_attn_norm_bias: float32 [1280], replicated
- grad_qkv_weight: float32 [3, 1280, 1280], P(None, 'shard', 'tp')
- grad_qkv_bias: float32 [3, 1280], P(None, 'tp')
- grad_proj_weight: float32 [1280, 1280], P('tp', 'shard')
- grad_proj_bias: float32 [1280], replicated
- grad_mlp_norm_gain: float32 [1280], replicated
- grad_mlp_norm_bias: float32 [1280], replicated
- grad_fc1_weight: float32 [1280, 5120], P('shard', 'tp')
- grad_fc1_bias: float32 [5120], P('tp')
- grad_fc2_weight: float32 [5120, 1280], P('tp', 'shard')
- grad_fc2_bias: float32 [1280], replicated
Inputs may be any that keep to these rules, and one draw needn't show every extreme that they name: patch_meta[0] holds each slot's picture id, counting up from 0 along a packed row, and -1 on padding slots, which lie only at a row's end; patch_meta[1] and patch_meta[2] hold the patch's row and column inside its picture (0 on padding). Pictures are rectangles of 10 to 32 patches a side filled row by row; only a row's last picture may have fewer picture rows. Fewer than 32 slots of a row are padding.
All inputs are finite; a program needn't handle non-finite values.
Results may differ from a plain program's by a relative error of at most 0.012.
Values may be sent and summed in bfloat16 or wider, within the bound.
A program may use at most 256 MiB of HBM per device.

v0:
```python
import math

import jax
import jax.numpy as jnp
from jax import lax
from jax.sharding import PartitionSpec as P

HDIM = 80


norm_epsilon = 1e-06
gelu_factor = 1.702
rope_base = 10000.0


def norm_stats(values):
    center = values - jnp.mean(values, -1, keepdims=True)
    spread = jnp.mean(center * center, -1, keepdims=True)
    inverse = lax.rsqrt(spread + norm_epsilon)
    return (center * inverse, inverse)


def norm_back(grad_out, normal, inverse, gain):
    scaled = grad_out * gain
    return inverse * (
        scaled
        - jnp.mean(scaled, -1, keepdims=True)
        - normal * jnp.mean(scaled * normal, -1, keepdims=True)
    )


def rope_tables(patch_row, patch_col, head_size):
    quarter = head_size // 4
    frequency = rope_base ** (-2.0 * jnp.arange(quarter, dtype=jnp.float32) / (head_size // 2))
    angles = jnp.concatenate(
        [
            patch_row.astype(jnp.float32)[:, None] * frequency[None, :],
            patch_col.astype(jnp.float32)[:, None] * frequency[None, :],
        ],
        axis=1,
    )
    angles = jnp.concatenate([angles, angles], axis=1)
    return (jnp.cos(angles)[:, None, :], jnp.sin(angles)[:, None, :])


def rotate_half(tensor):
    half_size = tensor.shape[-1] // 2
    return jnp.concatenate([-tensor[..., half_size:], tensor[..., :half_size]], axis=-1)


def apply_rope(tensor, cosine, sine_table):
    return tensor * cosine + rotate_half(tensor) * sine_table


def undo_rope(gradient, cosine, sine_table):
    return gradient * cosine - rotate_half(gradient * sine_table)


def split_heads(flat, batch, length, head_count):
    return (
        flat.reshape(batch, length, head_count, HDIM)
        .transpose(0, 2, 1, 3)
        .reshape(batch * head_count, length, HDIM)
    )


def join_heads(items, batch, length, head_count):
    return (
        items.reshape(batch, head_count, length, HDIM)
        .transpose(0, 2, 1, 3)
        .reshape(batch, length, head_count * HDIM)
    )


def masked_logits(query_head, key_head, query_ids, key_ids):
    logits = jnp.einsum("qd,kd->qk", query_head, key_head, preferred_element_type=jnp.float32) * (
        1.0 / math.sqrt(HDIM)
    )
    return jnp.where(query_ids[:, None] == key_ids[None, :], logits, -1e30)


def attend(packed):
    query_head, key_head, value_head, query_ids, key_ids = packed
    logits = masked_logits(query_head, key_head, query_ids, key_ids)
    peak = jnp.max(logits, -1, keepdims=True)
    exponent = jnp.exp(logits - peak)
    normalizer = jnp.sum(exponent, -1, keepdims=True)
    probs_low = (exponent / normalizer).astype(jnp.bfloat16)
    mixed_head = jnp.einsum("qk,kd->qd", probs_low, value_head, preferred_element_type=jnp.float32)
    return (mixed_head.astype(jnp.bfloat16), peak[:, 0] + jnp.log(normalizer[:, 0]))


def attend_back(packed):
    query_head, key_head, value_head, query_ids, key_ids, grad_head, log_total = packed
    score_scale = 1.0 / math.sqrt(HDIM)
    logits = masked_logits(query_head, key_head, query_ids, key_ids)
    probs = jnp.exp(logits - log_total[:, None])
    d_probs = jnp.einsum("qd,kd->qk", grad_head, value_head, preferred_element_type=jnp.float32)
    inner_sum = jnp.sum(probs * d_probs, -1, keepdims=True)
    d_logits = (probs * (d_probs - inner_sum)).astype(jnp.bfloat16)
    d_query = (
        jnp.einsum("qk,kd->qd", d_logits, key_head, preferred_element_type=jnp.float32)
        * score_scale
    )
    d_key = (
        jnp.einsum("qk,qd->kd", d_logits, query_head, preferred_element_type=jnp.float32)
        * score_scale
    )
    d_value = jnp.einsum(
        "qk,qd->kd", probs.astype(jnp.bfloat16), grad_head, preferred_element_type=jnp.float32
    )
    return (d_query, d_key, d_value)


def per_device(
    tokens,
    patch_meta,
    attn_norm_gain,
    attn_norm_bias,
    qkv_weight,
    qkv_bias,
    proj_weight,
    proj_bias,
    mlp_norm_gain,
    mlp_norm_bias,
    fc1_weight,
    fc1_bias,
    fc2_weight,
    fc2_bias,
    cotangent,
):
    local_len = tokens.shape[2]
    model_width = tokens.shape[3]
    full_len = patch_meta.shape[3]
    inner_width = qkv_weight.shape[2]
    ff_local = fc1_weight.shape[1]
    head_count = inner_width // HDIM
    offset = lax.axis_index("ctx") * local_len
    full_qkv, full_proj, full_first, full_second = (
        lax.all_gather(qkv_weight, "shard", axis=1, tiled=True),
        lax.all_gather(proj_weight, "shard", axis=1, tiled=True),
        lax.all_gather(fc1_weight, "shard", axis=0, tiled=True),
        lax.all_gather(fc2_weight, "shard", axis=1, tiled=True),
    )

    def one_micro(running, sample):
        tok_one, cot_one, meta_one = sample
        ids_all = meta_one[0]
        ids_own = lax.dynamic_slice_in_dim(ids_all, offset, local_len, 1)
        own_row = lax.dynamic_slice_in_dim(meta_one[1], offset, local_len, 1).reshape(local_len)
        own_col = lax.dynamic_slice_in_dim(meta_one[2], offset, local_len, 1).reshape(local_len)
        cosine, sine_table = rope_tables(own_row, own_col, HDIM)
        inputs = tok_one.reshape(local_len, model_width).astype(jnp.float32)
        normal_one, inverse_one = norm_stats(inputs)
        normed = (normal_one * attn_norm_gain + attn_norm_bias).astype(jnp.bfloat16)
        projected = (
            jnp.einsum("rd,cde->cre", normed, full_qkv, preferred_element_type=jnp.float32)
            + qkv_bias[:, None, :]
        )
        query = apply_rope(
            projected[0].reshape(local_len, head_count, HDIM), cosine, sine_table
        ).astype(jnp.bfloat16)
        key_part = apply_rope(
            projected[1].reshape(local_len, head_count, HDIM), cosine, sine_table
        ).astype(jnp.bfloat16)
        value_part = projected[2].astype(jnp.bfloat16)
        key_all, value_all = (
            lax.all_gather(key_part.reshape(1, local_len, inner_width), "ctx", axis=1, tiled=True),
            lax.all_gather(
                value_part.reshape(1, local_len, inner_width), "ctx", axis=1, tiled=True
            ),
        )
        query_items = split_heads(query, 1, local_len, head_count)
        key_items = split_heads(key_all, 1, full_len, head_count)
        value_items = split_heads(value_all, 1, full_len, head_count)
        query_ids = jnp.repeat(ids_own, head_count, axis=0)
        key_ids = jnp.repeat(ids_all, head_count, axis=0)
        mixed_items, log_totals = lax.map(
            attend, (query_items, key_items, value_items, query_ids, key_ids)
        )
        mixed = join_heads(mixed_items, 1, local_len, head_count).reshape(local_len, inner_width)
        attn_out = (
            lax.psum(jnp.dot(mixed, full_proj, preferred_element_type=jnp.float32), "tp")
            + proj_bias
        )
        hidden = inputs + attn_out
        normal_two, inverse_two = norm_stats(hidden)
        normed_two = (normal_two * mlp_norm_gain + mlp_norm_bias).astype(jnp.bfloat16)
        pre_act = jnp.dot(normed_two, full_first, preferred_element_type=jnp.float32) + fc1_bias
        sigmoid_part = jax.nn.sigmoid(gelu_factor * pre_act)
        activated = (pre_act * sigmoid_part).astype(jnp.bfloat16)
        mlp_out = (
            lax.psum(
                jnp.dot(activated, full_second, preferred_element_type=jnp.float32).astype(
                    jnp.bfloat16
                ),
                "tp",
            ).astype(jnp.float32)
            + fc2_bias
        )
        output_one = (hidden + mlp_out).astype(jnp.bfloat16).reshape(tok_one.shape)
        back_qkv, back_proj, back_first, back_second = (
            lax.all_gather(qkv_weight, "shard", axis=1, tiled=True),
            lax.all_gather(proj_weight, "shard", axis=1, tiled=True),
            lax.all_gather(fc1_weight, "shard", axis=0, tiled=True),
            lax.all_gather(fc2_weight, "shard", axis=1, tiled=True),
        )
        grad_low = cot_one.reshape(local_len, model_width)
        grad_out = grad_low.astype(jnp.float32)
        grad_second = jnp.einsum(
            "rf,rd->fd", activated, grad_low, preferred_element_type=jnp.float32
        )
        grad_second_bias = jnp.sum(grad_out, 0)
        d_act = jnp.einsum("rd,fd->rf", grad_low, back_second, preferred_element_type=jnp.float32)
        d_pre = (
            d_act * (sigmoid_part + gelu_factor * pre_act * sigmoid_part * (1.0 - sigmoid_part))
        ).astype(jnp.bfloat16)
        grad_first = jnp.einsum("rd,rf->df", normed_two, d_pre, preferred_element_type=jnp.float32)
        grad_first_bias = jnp.sum(d_pre.astype(jnp.float32), 0)
        d_norm_two = lax.psum(
            jnp.einsum("rf,df->rd", d_pre, back_first, preferred_element_type=jnp.float32), "tp"
        )
        grad_mlp_gain = jnp.sum(d_norm_two * normal_two, 0)
        grad_mlp_shift = jnp.sum(d_norm_two, 0)
        d_hidden = grad_out + norm_back(d_norm_two, normal_two, inverse_two, mlp_norm_gain)
        d_attn = d_hidden.astype(jnp.bfloat16)
        grad_proj_bias = jnp.sum(d_attn.astype(jnp.float32), 0)
        grad_proj = jnp.einsum("re,rd->ed", mixed, d_attn, preferred_element_type=jnp.float32)
        d_mixed = jnp.einsum(
            "rd,ed->re", d_attn, back_proj, preferred_element_type=jnp.float32
        ).astype(jnp.bfloat16)
        grad_items = split_heads(d_mixed, 1, local_len, head_count)
        d_query_items, d_key_items, d_value_items = lax.map(
            attend_back,
            (query_items, key_items, value_items, query_ids, key_ids, grad_items, log_totals),
        )
        d_key_all = join_heads(d_key_items, 1, full_len, head_count)
        d_value_all = join_heads(d_value_items, 1, full_len, head_count)
        d_key_own, d_value_own = (
            lax.psum_scatter(d_key_all, "ctx", scatter_dimension=1, tiled=True),
            lax.psum_scatter(d_value_all, "ctx", scatter_dimension=1, tiled=True),
        )
        d_query = join_heads(d_query_items, 1, local_len, head_count).reshape(
            local_len, head_count, HDIM
        )
        d_query_raw = undo_rope(d_query, cosine, sine_table).reshape(local_len, inner_width)
        d_key_raw = undo_rope(
            d_key_own.reshape(local_len, head_count, HDIM), cosine, sine_table
        ).reshape(local_len, inner_width)
        d_projected = jnp.stack(
            [d_query_raw, d_key_raw, d_value_own.reshape(local_len, inner_width)]
        ).astype(jnp.bfloat16)
        grad_qkv = jnp.einsum(
            "rd,cre->cde", normed, d_projected, preferred_element_type=jnp.float32
        )
        grad_qkv_shift = jnp.sum(d_projected.astype(jnp.float32), 1)
        d_normed = lax.psum(
            jnp.einsum("cre,cde->rd", d_projected, back_qkv, preferred_element_type=jnp.float32),
            "tp",
        )
        grad_attn_gain = jnp.sum(d_normed * normal_one, 0)
        grad_attn_shift = jnp.sum(d_normed, 0)
        input_one = (
            d_hidden + norm_back(d_normed, normal_one, inverse_one, attn_norm_gain)
        ).reshape(tok_one.shape)
        fresh = (
            grad_qkv,
            grad_proj,
            grad_first,
            grad_second,
            grad_attn_gain,
            grad_attn_shift,
            grad_qkv_shift,
            grad_proj_bias,
            grad_mlp_gain,
            grad_mlp_shift,
            grad_first_bias,
            grad_second_bias,
        )
        running = jax.tree.map(lambda earlier, latest: earlier + latest, running, fresh)
        return (running, (output_one, input_one))

    start_sums = (
        jnp.zeros((3, model_width, inner_width), jnp.float32),
        jnp.zeros((inner_width, model_width), jnp.float32),
        jnp.zeros((model_width, ff_local), jnp.float32),
        jnp.zeros((ff_local, model_width), jnp.float32),
        jnp.zeros((model_width,), jnp.float32),
        jnp.zeros((model_width,), jnp.float32),
        jnp.zeros((3, inner_width), jnp.float32),
        jnp.zeros((model_width,), jnp.float32),
        jnp.zeros((model_width,), jnp.float32),
        jnp.zeros((model_width,), jnp.float32),
        jnp.zeros((ff_local,), jnp.float32),
        jnp.zeros((model_width,), jnp.float32),
    )
    totals, (block_output, input_grad) = lax.scan(
        one_micro, start_sums, (tokens, cotangent, jnp.moveaxis(patch_meta, 1, 0))
    )
    small_sums = lax.psum(
        (totals[4], totals[5], totals[6], totals[7], totals[8], totals[9], totals[10], totals[11]),
        ("shard", "ctx"),
    )
    weight_grads = (totals[0], totals[1], totals[2], totals[3])
    weight_grads = (
        lax.psum_scatter(weight_grads[0], "shard", scatter_dimension=1, tiled=True),
        lax.psum_scatter(weight_grads[1], "shard", scatter_dimension=1, tiled=True),
        lax.psum_scatter(weight_grads[2], "shard", scatter_dimension=0, tiled=True),
        lax.psum_scatter(weight_grads[3], "shard", scatter_dimension=1, tiled=True),
    )
    weight_grads = lax.psum(
        (weight_grads[0], weight_grads[1], weight_grads[2], weight_grads[3]), "ctx"
    )
    return (
        block_output,
        input_grad,
        small_sums[0],
        small_sums[1],
        weight_grads[0],
        small_sums[2],
        weight_grads[1],
        small_sums[3],
        small_sums[4],
        small_sums[5],
        weight_grads[2],
        small_sums[6],
        weight_grads[3],
        small_sums[7],
    )


def solution(mesh):
    placed = (
        P(None, "shard", "ctx", None),
        P(None, None, "shard", None),
        P(),
        P(),
        P(None, "shard", "tp"),
        P(None, "tp"),
        P("tp", "shard"),
        P(),
        P(),
        P(),
        P("shard", "tp"),
        P("tp"),
        P("tp", "shard"),
        P(),
        P(None, "shard", "ctx", None),
    )
    return jax.shard_map(
        per_device,
        mesh=mesh,
        in_specs=placed,
        out_specs=(
            P(None, "shard", "ctx", None),
            P(None, "shard", "ctx", None),
            P(),
            P(),
            P(None, "shard", "tp"),
            P(None, "tp"),
            P("tp", "shard"),
            P(),
            P(),
            P(),
            P("shard", "tp"),
            P("tp"),
            P("tp", "shard"),
            P(),
        ),
        check_vma=False,
    )
```

profile of v0, /device:TPU:0, one launch (start us, length us, event | category | flops | bytes accessed | tf_op | source)
XLA Modules:
  0.0 2368.6 jit_solution(1720924637512056237)
XLA Ops:
  11.7 46.6 %all-gather.13.cloned.1.call-done = bf16[640,1280]{0,1:T(8,128)(2,1)} async-done(((bf16[640,160]{0,1:T(8,128)(2,1)}), bf16[640,1280]{0,1:T(8,128)(2,1)}) %all-gather.13.cloned.1.call-update) | async-done | bytes 1638416 | tf_op jit(solution)/shard_map/all_gather | solution.py:141
  61.9 99.7 %all-gather.17.cloned.1.call-done = bf16[2560,1280]{0,1:T(8,128)(2,1)} async-done(((bf16[2560,160]{0,1:T(8,128)(2,1)}), bf16[2560,1280]{0,1:T(8,128)(2,1)}) %all-gather.17.cloned.1.call-update) | async-done | bytes 6553616 | tf_op jit(solution)/shard_map/all_gather | solution.py:143
  171.2 73.1 %all-gather.11.cloned.1.call-done = bf16[3,1280,640]{2,1,0:T(8,128)(2,1)} async-done(((bf16[3,160,640]{2,1,0:T(8,128)(2,1)}), bf16[3,1280,640]{2,1,0:T(8,128)(2,1)}) %all-gather.11.cloned.1.call-update) | async-done | bytes 4915216 | tf_op jit(solution)/shard_map/all_gather | solution.py:140
  244.3 102.5 %all-gather.15.cloned.1.call-done = bf16[1280,2560]{1,0:T(8,128)(2,1)} async-done(((bf16[160,2560]{1,0:T(8,128)(2,1)}), bf16[1280,2560]{1,0:T(8,128)(2,1)}) %all-gather.15.cloned.1.call-update) | async-done | bytes 6553616 | tf_op jit(solution)/shard_map/all_gather | solution.py:142
  346.9 1259.4 %while.96 = (s32[]{:T(128)}, f32[3,1280,640]{1,2,0:T(8,128)}, f32[640,1280]{1,0:T(8,128)}, f32[1280,2560]{1,0:T(8,128)}, f32[2560,1280]{1,0:T(8,128)}, /*index=5...) while((s32[]{:T(128)}, f32[3,1280,640]{1,2,0:T(8,128)}, ...), condition=%wide.region_30.31_spmd.clone, body=%wide.region_0.30_spmd.clone.sunk | while | flops 30925250560 | bytes 610404544 | solution.py:297
  380.2 40.1 %while.97 = (s32[]{:T(128)}, bf16[8,512,80]{1,2,0:T(8,128)(2,1)S(1)}, f32[8,512]{1,0:T(8,128)}, s32[8,512]{1,0:T(8,128)S(1)}, s32[8,1024]{1,0:T(8,128)S(1)}, /*i...) while((s32[]{:T(128)}, ...), condition=%wide.region_6.6_spmd, body=%wide.region_3.5_spmd.sunk | while | flops 172531200 | bytes 7069817 | solution.py:178
  426.4 74.0 %all-reduce.10.cloned.1.call-done = f32[512,1280]{1,0:T(8,128)} async-done(((f32[512,1280]{1,0:T(8,128)}), f32[512,1280]{1,0:T(8,128)}) %all-reduce.10.cloned.1.call-update) | async-done | bytes 2621456 | tf_op jit(solution)/shard_map/while/body/eval_jaxpr/psum | solution.py:183
  511.8 18.7 all-gather.25.cloned.1.call-done
  530.5 11.5 convert_reduce_fusion.10
  542.1 90.7 %all-gather.27.cloned.1.call-done = bf16[1280,2560]{1,0:T(8,128)(2,1)} async-done(((bf16[160,2560]{1,0:T(8,128)(2,1)}), bf16[1280,2560]{1,0:T(8,128)(2,1)}) %all-gather.27.cloned.1.call-update) | async-done | bytes 6553616 | tf_op jit(solution)/shard_map/while/body/eval_jaxpr/all_gather | solution.py:205
  663.1 51.0 %all-reduce.12.cloned.1.call-done = f32[512,1280]{1,0:T(8,128)} async-done(((f32[512,1280]{1,0:T(8,128)}), f32[512,1280]{1,0:T(8,128)}) %all-reduce.12.cloned.1.call-update) | async-done | bytes 2621456 | tf_op jit(solution)/shard_map/while/body/eval_jaxpr/psum | solution.py:220
  725.7 75.7 %while.98 = (s32[]{:T(128)}, f32[8,512,80]{1,2,0:T(8,128)}, f32[8,1024,80]{1,2,0:T(8,128)}, f32[8,1024,80]{1,2,0:T(8,128)}, s32[8,512]{1,0:T(8,128)S(1)}, /*inde...) while((s32[]{:T(128)}, f32[8,512,80]{1,2,0:T(8,128)}, ...), condition=%wide.region_15.15_spmd, body=%wide.region_13.14_spmd.sunk | while | flops 424795648 | bytes 17794184 | solution.py:233
  803.0 12.0 convolution_add_fusion.8
  831.1 55.9 %all-gather.29.cloned.1.call-done = bf16[3,1280,640]{2,1,0:T(8,128)(2,1)} async-done(((bf16[3,160,640]{2,1,0:T(8,128)(2,1)}), bf16[3,1280,640]{2,1,0:T(8,128)(2,1)}) %all-gather.29.cloned.1.call-update) | async-done | bytes 4915216 | tf_op jit(solution)/shard_map/while/body/eval_jaxpr/all_gather | solution.py:203
  913.9 53.1 %all-reduce.14.cloned.1.call-done = f32[512,1280]{1,0:T(8,128)} async-done(((f32[512,1280]{1,0:T(8,128)}), f32[512,1280]{1,0:T(8,128)}) %all-reduce.14.cloned.1.call-update) | async-done | bytes 2621456 | tf_op jit(solution)/shard_map/while/body/eval_jaxpr/psum | solution.py:257
  1009.6 40.1 %while.97 = (s32[]{:T(128)}, bf16[8,512,80]{1,2,0:T(8,128)(2,1)S(1)}, f32[8,512]{1,0:T(8,128)}, s32[8,512]{1,0:T(8,128)S(1)}, s32[8,1024]{1,0:T(8,128)S(1)}, /*i...) while((s32[]{:T(128)}, ...), condition=%wide.region_6.6_spmd, body=%wide.region_3.5_spmd.sunk | while | flops 172531200 | bytes 7069817 | solution.py:178
  1055.8 74.0 %all-reduce.10.cloned.1.call-done = f32[512,1280]{1,0:T(8,128)} async-done(((f32[512,1280]{1,0:T(8,128)}), f32[512,1280]{1,0:T(8,128)}) %all-reduce.10.cloned.1.call-update) | async-done | bytes 2621456 | tf_op jit(solution)/shard_map/while/body/eval_jaxpr/psum | solution.py:183
  1141.2 19.1 all-gather.25.cloned.1.call-done
  1160.2 11.5 convert_reduce_fusion.10
  1171.8 90.8 %all-gather.27.cloned.1.call-done = bf16[1280,2560]{1,0:T(8,128)(2,1)} async-done(((bf16[160,2560]{1,0:T(8,128)(2,1)}), bf16[1280,2560]{1,0:T(8,128)(2,1)}) %all-gather.27.cloned.1.call-update) | async-done | bytes 6553616 | tf_op jit(solution)/shard_map/while/body/eval_jaxpr/all_gather | solution.py:205
  1282.9 61.1 %all-reduce.12.cloned.1.call-done = f32[512,1280]{1,0:T(8,128)} async-done(((f32[512,1280]{1,0:T(8,128)}), f32[512,1280]{1,0:T(8,128)}) %all-reduce.12.cloned.1.call-update) | async-done | bytes 2621456 | tf_op jit(solution)/shard_map/while/body/eval_jaxpr/psum | solution.py:220
  1355.7 75.8 %while.98 = (s32[]{:T(128)}, f32[8,512,80]{1,2,0:T(8,128)}, f32[8,1024,80]{1,2,0:T(8,128)}, f32[8,1024,80]{1,2,0:T(8,128)}, s32[8,512]{1,0:T(8,128)S(1)}, /*inde...) while((s32[]{:T(128)}, f32[8,512,80]{1,2,0:T(8,128)}, ...), condition=%wide.region_15.15_spmd, body=%wide.region_13.14_spmd.sunk | while | flops 424795648 | bytes 17794184 | solution.py:233
  1432.9 16.3 convolution_add_fusion.8
  1461.0 55.6 %all-gather.29.cloned.1.call-done = bf16[3,1280,640]{2,1,0:T(8,128)(2,1)} async-done(((bf16[3,160,640]{2,1,0:T(8,128)(2,1)}), bf16[3,1280,640]{2,1,0:T(8,128)(2,1)}) %all-gather.29.cloned.1.call-update) | async-done | bytes 4915216 | tf_op jit(solution)/shard_map/while/body/eval_jaxpr/all_gather | solution.py:203
  1524.0 11.9 convolution_add_fusion.7
  1548.0 48.6 %all-reduce.14.cloned.1.call-done = f32[512,1280]{1,0:T(8,128)} async-done(((f32[512,1280]{1,0:T(8,128)}), f32[512,1280]{1,0:T(8,128)}) %all-reduce.14.cloned.1.call-update) | async-done | bytes 2621456 | tf_op jit(solution)/shard_map/while/body/eval_jaxpr/psum | solution.py:257
  1623.1 14.0 copy.97
  1637.2 50.0 %reduce-scatter.9.cloned.1.call-done = f32[640,160]{0,1:T(8,128)} async-done(((f32[640,1280]{0,1:T(8,128)}), f32[640,160]{0,1:T(8,128)}) %reduce-scatter.9.cloned.1.call-update) | async-done | bytes 409616 | tf_op jit(solution)/shard_map/reduce_scatter | solution.py:307
  1687.2 171.9 %reduce-scatter.7.cloned.1.call-done = f32[3,160,640]{2,1,0:T(8,128)} async-done(((f32[3,1280,640]{2,1,0:T(8,128)}), f32[3,160,640]{2,1,0:T(8,128)}) %reduce-scatter.7.cloned.1.call-update) | async-done | bytes 1228816 | tf_op jit(solution)/shard_map/reduce_scatter | solution.py:306
  1859.1 217.8 %reduce-scatter.11.cloned.1.call-done = f32[160,2560]{1,0:T(8,128)} async-done(((f32[1280,2560]{1,0:T(8,128)}), f32[160,2560]{1,0:T(8,128)}) %reduce-scatter.11.cloned.1.call-update) | async-done | bytes 1638416 | tf_op jit(solution)/shard_map/reduce_scatter | solution.py:308
  2076.9 217.6 %reduce-scatter.13.cloned.1.call-done = f32[2560,160]{0,1:T(8,128)} async-done(((f32[2560,1280]{0,1:T(8,128)}), f32[2560,160]{0,1:T(8,128)}) %reduce-scatter.13.cloned.1.call-update) | async-done | bytes 1638416 | tf_op jit(solution)/shard_map/reduce_scatter | solution.py:309
  2294.7 61.0 %all-reduce = (f32[1280]{0:T(1024)}, f32[1280]{0:T(1024)}, f32[3,640]{1,0:T(4,128)}, f32[1280]{0:T(1024)}, f32[1280]{0:T(1024)}, /*index=5*/f32[1280]{0:T(1024)}, f32[2560]{0:T(1024)}, f32[1280]{0:T(1024)}) all-reduce(f32[1280]{0:T(1024)S(1)} %copy-done.55, ...), channel_id=1, replica_groups=mesh['shard'=8,'ctx'=2,'tp'=2] {'shard','ctx'}, use_global_device_ids=true, to_apply=%region_31.32 | all-reduce | flops 12160 | bytes 97280 | tf_op jit(solution)/shard_map/psum | solution.py:300
  (723 shorter events, 536.8 us)
Async XLA Ops:
  8.0 50.3 %all-gather.13.cloned.1.call-start = ((), (), s32[]{:S(2)}) async-start(), calls=%async_computation.7 | async-start | bytes 1843200 | tf_op jit(solution)/shard_map/all_gather | solution.py:141
  8.7 152.9 %all-gather.17.cloned.1.call-start = ((), (), s32[]{:S(2)}) async-start(), calls=%async_computation.9 | async-start | bytes 7372800 | tf_op jit(solution)/shard_map/all_gather | solution.py:143
  9.5 234.8 %all-gather.11.cloned.1.call-start = ((), (), s32[]{:S(2)}) async-start(), calls=%async_computation.6 | async-start | bytes 5529600 | tf_op jit(solution)/shard_map/all_gather | solution.py:140
  10.2 336.6 %all-gather.15.cloned.1.call-start = ((), (), s32[]{:S(2)}) async-start(), calls=%async_computation.8 | async-start | bytes 7372800 | tf_op jit(solution)/shard_map/all_gather | solution.py:142
  347.1 20.5 all-gather.21.cloned.1.call-start
  364.5 135.9 %all-reduce.10.cloned.1.call-start = ((), (), s32[]{:S(2)}) async-start(), calls=%async_computation.18 | async-start | bytes 5242880 | tf_op jit(solution)/shard_map/while/body/eval_jaxpr/psum | solution.py:183
  424.7 105.8 %all-gather.25.cloned.1.call-start = ((), (), s32[]{:S(2)}) async-start(), calls=%async_computation.19 | async-start | bytes 7372800 | tf_op jit(solution)/shard_map/while/body/eval_jaxpr/all_gather | solution.py:206
  425.3 207.4 %all-gather.27.cloned.1.call-start = ((), (), s32[]{:S(2)}) async-start(), calls=%async_computation.20 | async-start | bytes 7372800 | tf_op jit(solution)/shard_map/while/body/eval_jaxpr/all_gather | solution.py:205
  425.9 288.3 %all-reduce.12.cloned.1.call-start = ((), (), s32[]{:S(2)}) async-start(), calls=%async_computation.21 | async-start | bytes 5242880 | tf_op jit(solution)/shard_map/while/body/eval_jaxpr/psum | solution.py:220
  641.5 78.4 %all-gather.23.cloned.1.call-start = ((), (), s32[]{:S(2)}) async-start(), calls=%async_computation.17 | async-start | bytes 1843200 | tf_op jit(solution)/shard_map/while/body/eval_jaxpr/all_gather | solution.py:204
  642.1 173.0 %all-reduce.16.cloned.1.call-start = ((), (), s32[]{:S(2)}) async-start(), calls=%async_computation.26 | async-start | bytes 2621440 | tf_op jit(solution)/shard_map/while/body/eval_jaxpr/psum | solution.py:193
  652.8 165.0 %reduce-scatter.15.cloned.1.call-start = ((), (), s32[]{:S(2)}) async-start(), calls=%async_computation.22 | async-start | bytes 3932160 | tf_op jit(solution)/shard_map/while/body/eval_jaxpr/reduce_scatter | solution.py:241
  801.5 24.0 %reduce-scatter.17.cloned.1.call-start = ((), (), s32[]{:S(2)}) async-start(), calls=%async_computation.23 | async-start | bytes 3932160 | tf_op jit(solution)/shard_map/while/body/eval_jaxpr/reduce_scatter | solution.py:240
  802.2 84.8 %all-gather.29.cloned.1.call-start = ((), (), s32[]{:S(2)}) async-start(), calls=%async_computation.24 | async-start | bytes 5529600 | tf_op jit(solution)/shard_map/while/body/eval_jaxpr/all_gather | solution.py:203
  802.9 164.0 %all-reduce.14.cloned.1.call-start = ((), (), s32[]{:S(2)}) async-start(), calls=%async_computation.25 | async-start | bytes 5242880 | tf_op jit(solution)/shard_map/while/body/eval_jaxpr/psum | solution.py:257
  974.7 20.3 all-gather.21.cloned.1.call-start
  983.9 21.7 all-gather.19.cloned.1.call-start
  991.9 137.9 %all-reduce.10.cloned.1.call-start = ((), (), s32[]{:S(2)}) async-start(), calls=%async_computation.18 | async-start | bytes 5242880 | tf_op jit(solution)/shard_map/while/body/eval_jaxpr/psum | solution.py:183
  1054.1 106.1 %all-gather.25.cloned.1.call-start = ((), (), s32[]{:S(2)}) async-start(), calls=%async_computation.19 | async-start | bytes 7372800 | tf_op jit(solution)/shard_map/while/body/eval_jaxpr/all_gather | solution.py:206
  1054.9 207.7 %all-gather.27.cloned.1.call-start = ((), (), s32[]{:S(2)}) async-start(), calls=%async_computation.20 | async-start | bytes 7372800 | tf_op jit(solution)/shard_map/while/body/eval_jaxpr/all_gather | solution.py:205
  1055.6 288.4 %all-reduce.12.cloned.1.call-start = ((), (), s32[]{:S(2)}) async-start(), calls=%async_computation.21 | async-start | bytes 5242880 | tf_op jit(solution)/shard_map/while/body/eval_jaxpr/psum | solution.py:220
  1271.3 78.5 %all-gather.23.cloned.1.call-start = ((), (), s32[]{:S(2)}) async-start(), calls=%async_computation.17 | async-start | bytes 1843200 | tf_op jit(solution)/shard_map/while/body/eval_jaxpr/all_gather | solution.py:204
  1271.9 177.3 %all-reduce.16.cloned.1.call-start = ((), (), s32[]{:S(2)}) async-start(), calls=%async_computation.26 | async-start | bytes 2621440 | tf_op jit(solution)/shard_map/while/body/eval_jaxpr/psum | solution.py:193
  1282.7 169.3 %reduce-scatter.15.cloned.1.call-start = ((), (), s32[]{:S(2)}) async-start(), calls=%async_computation.22 | async-start | bytes 3932160 | tf_op jit(solution)/shard_map/while/body/eval_jaxpr/reduce_scatter | solution.py:241
  1431.5 23.9 %reduce-scatter.17.cloned.1.call-start = ((), (), s32[]{:S(2)}) async-start(), calls=%async_computation.23 | async-start | bytes 3932160 | tf_op jit(solution)/shard_map/while/body/eval_jaxpr/reduce_scatter | solution.py:240
  1432.2 84.4 %all-gather.29.cloned.1.call-start = ((), (), s32[]{:S(2)}) async-start(), calls=%async_computation.24 | async-start | bytes 5529600 | tf_op jit(solution)/shard_map/while/body/eval_jaxpr/all_gather | solution.py:203
  1432.8 163.7 %all-reduce.14.cloned.1.call-start = ((), (), s32[]{:S(2)}) async-start(), calls=%async_computation.25 | async-start | bytes 5242880 | tf_op jit(solution)/shard_map/while/body/eval_jaxpr/psum | solution.py:257
  1606.3 81.0 %reduce-scatter.9.cloned.1.call-start = ((), (), s32[]{:S(2)}) async-start(), calls=%async_computation.11 | async-start | bytes 3686400 | tf_op jit(solution)/shard_map/reduce_scatter | solution.py:307
  1611.0 248.1 %reduce-scatter.7.cloned.1.call-start = ((), (), s32[]{:S(2)}) async-start(), calls=%async_computation.10 | async-start | bytes 11059200 | tf_op jit(solution)/shard_map/reduce_scatter | solution.py:306
  1622.3 454.6 %reduce-scatter.11.cloned.1.call-start = ((), (), s32[]{:S(2)}) async-start(), calls=%async_computation.12 | async-start | bytes 14745600 | tf_op jit(solution)/shard_map/reduce_scatter | solution.py:308
  1623.0 671.5 %reduce-scatter.13.cloned.1.call-start = ((), (), s32[]{:S(2)}) async-start(), calls=%async_computation.13 | async-start | bytes 14745600 | tf_op jit(solution)/shard_map/reduce_scatter | solution.py:309
  1637.2 718.5 %all-reduce.8.cloned.1.call-start = ((), (), s32[]{:S(2)}) async-start(), calls=%async_computation.14 | async-start | bytes 9830400 | tf_op jit(solution)/shard_map/psum | solution.py:311
  (116 other events, 8389.8 us)
Sparse Core Ops, SparseCore 0:
  11.0 47.2 all-gather.12
  60.5 101.1 all-gather.16
  163.8 80.4 all-gather.10
  246.3 100.4 all-gather.14
  356.4 7.5 all-gather.20
  365.5 10.5 all-gather.18
  424.8 75.5 all-reduce.9
  641.6 72.5 all-reduce.11
  716.6 45.7 all-reduce.15
  801.6 10.0 reduce-scatter.14
  814.0 11.4 reduce-scatter.16
  894.4 72.5 all-reduce.13
  984.0 9.4 all-gather.20
  994.9 10.5 all-gather.18
  1054.2 75.5 all-reduce.9
  1271.5 72.5 all-reduce.11
  1346.3 45.7 all-reduce.15
  1431.6 9.8 reduce-scatter.14
  1443.9 11.4 reduce-scatter.16
  1524.0 72.5 all-reduce.13
  1611.1 76.1 reduce-scatter.8
  1691.3 167.7 reduce-scatter.6
  1863.2 213.6 reduce-scatter.10
  2080.8 213.6 reduce-scatter.12
  2297.6 28.9 all-reduce.7
Sparse Core Ops, SparseCore 1:
  427.4 103.1 all-gather.24
  532.6 100.1 all-gather.26
  644.1 42.9 all-gather.22
  805.2 81.8 all-gather.28
  1057.1 103.1 all-gather.24
  1162.4 100.1 all-gather.26
  1274.0 42.9 all-gather.22
  1434.9 81.6 all-gather.28
where the time goes:
time: 2380 us; the launch traced here: 2370 us
  waiting for transfers between devices  1700 us (71%)
  matrix products  374 us (16%)
  local copies, waits for them, and re-layouts  127 us (5%)
  other arithmetic  73.1 us (3%)
  blocking collectives  61 us (3%)
    reduce_scatter x1, waiting for transfers between devices, per_device(): lax.psum_scatter(weight_grads[2], 'shard', scatter_dimension=0, tiled=True)  218 us
    reduce_scatter x1, waiting for transfers between devices, per_device(): lax.psum_scatter(weight_grads[3], 'shard', scatter_dimension=1, tiled=True)  218 us
    all_gather x2, waiting for transfers between devices, one_micro(): lax.all_gather(fc1_weight, 'shard', axis=0, tiled=True)  181 us
    reduce_scatter x1, waiting for transfers between devices, per_device(): lax.psum_scatter(weight_grads[0], 'shard', scatter_dimension=1, tiled=True)  172 us
    psum x2, waiting for transfers between devices, one_micro(): lax.psum(jnp.dot(mixed, full_proj, preferred_element_type=jnp.float32), '...  148 us
    psum x2, waiting for transfers between devices, one_micro(): lax.psum(jnp.einsum('rf,df->rd', d_pre, back_first, preferred_element_typ...  112 us
    all_gather x2, waiting for transfers between devices, one_micro(): lax.all_gather(qkv_weight, 'shard', axis=1, tiled=True)  111 us
    all_gather x1, waiting for transfers between devices, per_device(): lax.all_gather(fc1_weight, 'shard', axis=0, tiled=True)  103 us
  transfers between devices with their start and end apart: 33, of which 24 were waited for; matrix products, arithmetic and copies ran while one was open for 17% of the time, Pallas kernels for 0%

commit v1 on v0

v1 whole, which is shorter than its diff:
```python
import functools
import math

import jax
import jax.numpy as jnp
from jax import lax
from jax.experimental import pallas as pl
from jax.experimental.pallas import tpu as pltpu
from jax.sharding import PartitionSpec as P

HDIM = 80
NORM_EPS = 1e-06
GELU = 1.702
ROPE_BASE = 10000.0
SCALE = 1.0 / math.sqrt(HDIM)
LOG2E = 1.0 / math.log(2.0)
NEG = -1e30
F32 = jnp.float32
BF16 = jnp.bfloat16
AXES = ("shard", "ctx", "tp")
QB = 256


def dg(left, right, dims, out=F32):
    return lax.dot_general(left, right, (dims, ((), ())), preferred_element_type=F32).astype(out)


def rope_rows(t, cosine, sine):
    half = t.shape[0] // 2
    first, second = t[:half], t[half:]
    return jnp.concatenate([first * cosine - second * sine, second * cosine + first * sine], axis=0)


def rope_rows_back(t, cosine, sine):
    half = t.shape[0] // 2
    first, second = t[:half], t[half:]
    return jnp.concatenate([first * cosine + second * sine, second * cosine - first * sine], axis=0)


def fill_bias(bias, idc_ref, idr_ref):
    @pl.when(pl.program_id(0) == 0)
    def _():
        bias[...] = jnp.where(idc_ref[...] == idr_ref[...], 0.0, NEG)


def attend_kernel(x_ref, cos_ref, sin_ref, idc_ref, idr_ref, low_ref, out_ref, outf_ref, lse_ref, bias):
    fill_bias(bias, idc_ref, idr_ref)
    cosine, sine = cos_ref[...], sin_ref[...]
    query = rope_rows(x_ref[0], cosine, sine).astype(BF16)
    key_f = rope_rows(x_ref[1], cosine, sine)
    value = x_ref[2].astype(BF16)
    low_ref[0] = query
    low_ref[1] = key_f.astype(BF16)
    low_ref[2] = value
    key_nat = key_f.T.astype(BF16)
    length = query.shape[1]
    factor = SCALE * LOG2E
    for start in range(0, length, QB):
        cols = slice(start, start + QB)
        logits = dg(key_nat, query[:, cols], ((1,), (0,))) + bias[:, cols]
        peak = jnp.max(logits, axis=0, keepdims=True)
        probs = jnp.exp2((logits - peak) * factor)
        total = jnp.sum(probs, axis=0, keepdims=True)
        mixed = dg(value, probs.astype(BF16), ((1,), (0,))) * (1.0 / total)
        out_ref[:, cols] = mixed.astype(BF16)
        outf_ref[:, cols] = mixed
        lse_ref[0, :, cols] = peak * factor + jnp.log2(total)


def attend(qkv, cosine, sine, ids):
    _, width, length = qkv.shape
    heads = width // HDIM
    half = HDIM // 2
    head = lambda h: (0, h, 0)
    whole = lambda h: (0, 0)
    return pl.pallas_call(
        attend_kernel,
        grid=(heads,),
        in_specs=[
            pl.BlockSpec((3, HDIM, length), head),
            pl.BlockSpec((half, length), whole),
            pl.BlockSpec((half, length), whole),
            pl.BlockSpec((length, 1), whole),
            pl.BlockSpec((1, length), whole),
        ],
        out_specs=[
            pl.BlockSpec((3, HDIM, length), head),
            pl.BlockSpec((HDIM, length), lambda h: (h, 0)),
            pl.BlockSpec((HDIM, length), lambda h: (h, 0)),
            pl.BlockSpec((1, 1, length), lambda h: (h, 0, 0)),
        ],
        out_shape=[
            jax.ShapeDtypeStruct((3, width, length), BF16),
            jax.ShapeDtypeStruct((width, length), BF16),
            jax.ShapeDtypeStruct((width, length), F32),
            jax.ShapeDtypeStruct((heads, 1, length), F32),
        ],
        scratch_shapes=[pltpu.VMEM((length, length), F32)],
        compiler_params=pltpu.CompilerParams(vmem_limit_bytes=48 << 20),
        cost_estimate=pl.CostEstimate(
            flops=4 * width * length * length,
            transcendentals=heads * length * length,
            bytes_accessed=26 * width * length,
        ),
        name="attend",
    )(qkv, cosine, sine, ids[:, None], ids[None, :])


def attend_back_kernel(
    low_ref, grad_ref, outf_ref, lse_ref, cos_ref, sin_ref, idc_ref, idr_ref, dproj_ref, bias, dq, dk, dv
):
    fill_bias(bias, idc_ref, idr_ref)
    cosine, sine = cos_ref[...], sin_ref[...]
    query, key = low_ref[0], low_ref[1]
    grad = grad_ref[...]
    grad_f = grad.astype(F32)
    delta = jnp.sum(grad_f * outf_ref[...], axis=0, keepdims=True)
    nat = lambda t: t.astype(F32).T.astype(BF16)
    query_nat, key_nat, value_nat, grad_nat = nat(query), nat(key), nat(low_ref[2]), nat(grad)
    lse = lse_ref[0]
    length = query.shape[1]
    factor = SCALE * LOG2E
    for start in range(0, length, QB):
        cols = slice(start, start + QB)
        logits = dg(key_nat, query[:, cols], ((1,), (0,)))
        probs = jnp.exp2(logits * factor + bias[:, cols] - lse[:, cols])
        d_probs = dg(value_nat, grad[:, cols], ((1,), (0,)))
        d_logits = (probs * (d_probs - delta[:, cols])).astype(BF16)
        part_v = dg(probs.astype(BF16), grad_nat[cols], ((1,), (0,)))
        part_k = dg(d_logits, query_nat[cols], ((1,), (0,)))
        dq[:, cols] = dg(key, d_logits, ((1,), (0,)))
        if start == 0:
            dv[...] = part_v
            dk[...] = part_k
        else:
            dv[...] += part_v
            dk[...] += part_k
    dproj_ref[0] = rope_rows_back(dq[...] * SCALE, cosine, sine).astype(BF16)
    dproj_ref[1] = rope_rows_back(dk[...].T * SCALE, cosine, sine).astype(BF16)
    dproj_ref[2] = dv[...].T.astype(BF16)


def attend_back(low, grad, outf, lse, cosine, sine, ids):
    _, width, length = low.shape
    heads = width // HDIM
    half = HDIM // 2
    head = lambda h: (0, h, 0)
    whole = lambda h: (0, 0)
    return pl.pallas_call(
        attend_back_kernel,
        grid=(heads,),
        in_specs=[
            pl.BlockSpec((3, HDIM, length), head),
            pl.BlockSpec((HDIM, length), lambda h: (h, 0)),
            pl.BlockSpec((HDIM, length), lambda h: (h, 0)),
            pl.BlockSpec((1, 1, length), lambda h: (h, 0, 0)),
            pl.BlockSpec((half, length), whole),
            pl.BlockSpec((half, length), whole),
            pl.BlockSpec((length, 1), whole),
            pl.BlockSpec((1, length), whole),
        ],
        out_specs=pl.BlockSpec((3, HDIM, length), head),
        out_shape=jax.ShapeDtypeStruct((3, width, length), BF16),
        scratch_shapes=[
            pltpu.VMEM((length, length), F32),
            pltpu.VMEM((HDIM, length), F32),
            pltpu.VMEM((length, HDIM), F32),
            pltpu.VMEM((length, HDIM), F32),
        ],
        compiler_params=pltpu.CompilerParams(vmem_limit_bytes=48 << 20),
        cost_estimate=pl.CostEstimate(
            flops=10 * width * length * length,
            transcendentals=heads * length * length,
            bytes_accessed=18 * width * length,
        ),
        name="attend_back",
    )(low, grad, outf, lse, cosine, sine, ids[:, None], ids[None, :])


def rope_tables(patch_row, patch_col):
    quarter = HDIM // 4
    frequency = ROPE_BASE ** (-2.0 * jnp.arange(quarter, dtype=F32) / (HDIM // 2))
    angles = jnp.concatenate(
        [
            frequency[:, None] * patch_row.astype(F32)[None, :],
            frequency[:, None] * patch_col.astype(F32)[None, :],
        ],
        axis=0,
    )
    return jnp.cos(angles), jnp.sin(angles)


def norm_stats(values):
    center = values - jnp.mean(values, -1, keepdims=True)
    spread = jnp.mean(center * center, -1, keepdims=True)
    inverse = lax.rsqrt(spread + NORM_EPS)
    return center * inverse, inverse


def norm_back(grad_out, normal, inverse, gain):
    scaled = grad_out * gain
    return inverse * (
        scaled
        - jnp.mean(scaled, -1, keepdims=True)
        - normal * jnp.mean(scaled * normal, -1, keepdims=True)
    )


class Links:
    def __init__(self, shards):
        self.shards = shards
        self.lines = shards // 2
        self.s = lax.axis_index("shard")
        self.c = lax.axis_index("ctx")
        self.y = lax.axis_index("tp")
        self.line = self.s // 2
        self.side = self.s % 2
        self.diag = self.c == self.y

    def send(self, value, target, where=lambda c, y: True):
        flat = lambda s, c, y: (s * 2 + c) * 2 + y
        pairs = []
        for s in range(self.shards):
            for c in range(2):
                for y in range(2):
                    if where(c, y):
                        pairs.append((flat(s, c, y), flat(*target(s, c, y))))
        return lax.ppermute(value, AXES, pairs)

    def core(self, value):
        return self.send(value, lambda s, c, y: (s, 1 - c, y))

    def across(self, value, where=lambda c, y: True):
        return self.send(value, lambda s, c, y: (s, c, 1 - y), where)

    def beside(self, value, where=lambda c, y: True):
        return self.send(value, lambda s, c, y: (s ^ 1, c, y), where)

    def along(self, value, step, where=lambda c, y: True):
        lines = self.lines
        return self.send(value, lambda s, c, y: (((s // 2 + step) % lines) * 2 + s % 2, c, y), where)

    def gather(self, block, where=lambda c, y: True):
        near = [block] + [self.along(block, k, where) for k in range(1, self.lines)]
        far = [self.beside(piece, where) for piece in near]
        return near, far

    def place(self, near, far):
        full = jnp.zeros((self.shards,) + near[0].shape, near[0].dtype)
        for k in range(self.lines):
            row = ((self.line - k) % self.lines) * 2
            full = lax.dynamic_update_index_in_dim(full, near[k], row + self.side, 0)
            full = lax.dynamic_update_index_in_dim(full, far[k], row + 1 - self.side, 0)
        return full

    def scatter(self, blocks, where=lambda c, y: True):
        pick = lambda t, i, d: lax.dynamic_index_in_dim(t, i, d, False)
        other = pick(blocks, 1 - self.side, 1)
        mine = pick(blocks, self.side, 1).astype(F32) + self.beside(other, where).astype(F32)
        low = mine.astype(BF16)
        total = pick(mine, self.line, 0)
        for k in range(1, self.lines):
            piece = pick(low, (self.line + k) % self.lines, 0)
            total = total + self.along(piece, k, where).astype(F32)
        return total


def on_diag(c, y):
    return c == y


def off_diag(c, y):
    return c != y


def per_device(
    tokens,
    patch_meta,
    attn_norm_gain,
    attn_norm_bias,
    qkv_weight,
    qkv_bias,
    proj_weight,
    proj_bias,
    mlp_norm_gain,
    mlp_norm_bias,
    fc1_weight,
    fc1_bias,
    fc2_weight,
    fc2_bias,
    cotangent,
    *,
    shards,
):
    net = Links(shards)
    c, y = net.c, net.y
    local = tokens.shape[2]
    width = tokens.shape[3]
    full = patch_meta.shape[3]
    inner = qkv_weight.shape[2]
    rows = width // shards
    quarter = fc1_weight.shape[1] // 2
    pick = lambda t, i, d=0: lax.dynamic_index_in_dim(t, i, d, False)
    mine_or = lambda own, other: jnp.where(net.diag, own, other)

    def both(own, other, index):
        return jnp.where(index == 0, jnp.stack([own, other]), jnp.stack([other, own]))

    attn_block = jnp.concatenate([qkv_weight, proj_weight.T[None]], axis=0)
    early = attn_block[3:]
    early_peer = net.across(early, on_diag)
    late_near, late_far = net.gather(attn_block[:3], on_diag)
    early_near, early_far = net.gather(mine_or(early, early_peer))
    late_near_peer = [net.across(p, on_diag) for p in late_near]
    late_far_peer = [net.across(p, on_diag) for p in late_far]
    late_near = [mine_or(p, q) for p, q in zip(late_near, late_near_peer)]
    late_far = [mine_or(p, q) for p, q in zip(late_far, late_far_peer)]
    qkv_full = jnp.moveaxis(net.place(late_near, late_far), 0, 1).reshape(3, width, inner)
    proj_full = net.place(early_near, early_far).reshape(width, inner)

    fc1_block = lax.dynamic_slice_in_dim(fc1_weight, c * quarter, quarter, 1)
    fc2_block = lax.dynamic_slice_in_dim(fc2_weight, c * quarter, quarter, 0).T
    fc1_full = net.place(*net.gather(fc1_block)).reshape(width, quarter)
    fc2_full = net.place(*net.gather(fc2_block)).reshape(width, quarter)
    bias_qkv = mine_or(qkv_bias, net.across(qkv_bias, on_diag))
    bias_fc1 = lax.dynamic_slice_in_dim(fc1_bias, c * quarter, quarter, 0)

    inputs = pick(tokens, y).reshape(local, width).astype(F32)
    normal_one, inverse_one = norm_stats(inputs)
    normed_own = (normal_one * attn_norm_gain + attn_norm_bias).astype(BF16)
    normed = both(normed_own, net.core(normed_own), c).reshape(full, width)
    meta = pick(patch_meta, y, 1).reshape(3, full)
    ids = meta[0]
    cosine, sine = rope_tables(meta[1], meta[2])
    qkv = (
        jnp.einsum("cde,rd->cer", qkv_full, normed, preferred_element_type=F32)
        + bias_qkv[:, :, None]
    )
    low, mixed, mixed_f, lse = attend(qkv, cosine, sine, ids)
    attn_part = dg(mixed, proj_full, ((0,), (1,))).reshape(2, local, width)
    attn_own = pick(attn_part, c) + net.core(pick(attn_part, 1 - c))
    hidden = inputs + attn_own + proj_bias

    normal_two, inverse_two = norm_stats(hidden)
    two_own = (normal_two * mlp_norm_gain + mlp_norm_bias).astype(BF16)
    two_peer = net.across(two_own)
    two = [
        jnp.concatenate([two_own, net.core(two_own)]),
        jnp.concatenate([two_peer, net.core(two_peer)]),
    ]
    grad_out = cotangent.reshape(2, local, width)
    grad_out_sib = net.core(grad_out)
    dy_own = pick(grad_out, y)
    dy = [jnp.concatenate([pick(grad_out, m), pick(grad_out_sib, m)]) for m in (y, 1 - y)]

    acts, d_pres, d_twos = [], [], []
    for part, dy_part in zip(two, dy):
        pre = dg(part, fc1_full, ((1,), (0,))) + bias_fc1
        sig = jax.nn.sigmoid(GELU * pre)
        acts.append((pre * sig).astype(BF16))
        d_act = dg(dy_part, fc2_full, ((1,), (0,)))
        d_pre = (d_act * (sig + GELU * pre * sig * (1.0 - sig))).astype(BF16)
        d_pres.append(d_pre)
        d_twos.append(dg(d_pre, fc1_full, ((1,), (1,))))

    def reduce_slots(parts):
        own, other = parts
        other = other[:local] + net.core(other[local:].astype(BF16)).astype(F32)
        from_peer = net.across(other.astype(BF16)).astype(F32)
        own = own[:local] + net.core(own[local:].astype(BF16)).astype(F32)
        return own + from_peer

    d_two = reduce_slots(d_twos)
    mlp_out = reduce_slots([dg(a, fc2_full, ((1,), (1,))) for a in acts])
    out_own = (hidden + mlp_out + fc2_bias).astype(BF16)
    block_output = both(out_own, net.across(out_own), y)

    def weight_sum(lefts, rights):
        total = sum(dg(l, r, ((0,), (0,))) for l, r in zip(lefts, rights))
        return total.astype(BF16).reshape(net.lines, 2, rows, quarter)

    def all_hidden(block):
        return both(block, net.core(block), c)

    grad_fc2 = all_hidden(net.scatter(weight_sum(dy, acts)))
    grad_fc1 = all_hidden(net.scatter(weight_sum(two, d_pres)))
    grad_fc1 = jnp.moveaxis(grad_fc1, 0, 1).reshape(rows, 2 * quarter)
    grad_fc2 = jnp.moveaxis(grad_fc2, 1, 2).reshape(2 * quarter, rows)

    d_hidden = dy_own.astype(F32) + norm_back(d_two, normal_two, inverse_two, mlp_norm_gain)
    d_attn_own = d_hidden.astype(BF16)
    d_attn = both(d_attn_own, net.core(d_attn_own), c).reshape(full, width)
    grad_proj_part = dg(d_attn, mixed, ((0,), (1,)), BF16)
    d_mixed = dg(proj_full, d_attn, ((0,), (1,)), BF16)
    d_proj = attend_back(low, d_mixed, mixed_f, lse, cosine, sine, ids)
    grad_qkv_part = jnp.einsum("cer,rd->cde", d_proj, normed, preferred_element_type=F32).astype(BF16)
    d_one_part = jnp.einsum("cer,cde->rd", d_proj, qkv_full, preferred_element_type=F32)
    d_one_part = d_one_part.reshape(2, local, width)
    d_one = pick(d_one_part, c) + net.core(pick(d_one_part, 1 - c))
    grad_in = d_hidden + norm_back(d_one, normal_one, inverse_one, attn_norm_gain)
    grad_in = grad_in.astype(BF16)
    input_grad = both(grad_in, net.across(grad_in), y).astype(F32)

    proj_plane = net.scatter(grad_proj_part.reshape(net.lines, 2, rows, inner))
    proj_sum = proj_plane + net.across(proj_plane.astype(BF16), off_diag).astype(F32)
    qkv_pair = grad_qkv_part.astype(F32) + net.across(grad_qkv_part, off_diag).astype(F32)
    qkv_pair = jnp.moveaxis(qkv_pair.astype(BF16).reshape(3, net.lines, 2, rows, inner), 0, 2)
    qkv_sum = net.scatter(qkv_pair, on_diag)
    attn_sum = jnp.concatenate([qkv_sum, proj_sum[None]])
    attn_sum = mine_or(attn_sum, net.send(attn_sum, lambda s, c, y: (s, 1 - c, y), on_diag))
    grad_qkv, grad_proj = attn_sum[:3], attn_sum[3].T

    sums = lambda t: jnp.sum(t.astype(F32), axis=0)
    qkv_shift = jnp.sum(d_proj.astype(F32), axis=2)
    fc1_shift = sum(sums(d) for d in d_pres)
    zero_qkv, zero_fc1 = jnp.zeros_like(qkv_shift), jnp.zeros_like(fc1_shift)
    small = jnp.concatenate(
        [
            sums(d_one * normal_one),
            sums(d_one),
            sums(d_attn_own),
            sums(d_two * normal_two),
            sums(d_two),
            sums(dy_own),
            jnp.where(c == 0, qkv_shift, zero_qkv).reshape(-1),
            jnp.where(c == 1, qkv_shift, zero_qkv).reshape(-1),
        ]
        + [jnp.where((y == i) & (c == j), fc1_shift, zero_fc1) for i in range(2) for j in range(2)]
    )
    small = lax.psum(small, AXES)
    vec = lambda i: small[i * width : (i + 1) * width]
    at = 6 * width
    qkv_shifts = small[at : at + 6 * inner].reshape(2, 3, inner)
    fc1_shifts = small[at + 6 * inner :].reshape(2, 2 * quarter)
    out_shape = tokens.shape
    return (
        block_output.reshape(out_shape),
        input_grad.reshape(out_shape),
        vec(0),
        vec(1),
        grad_qkv,
        pick(qkv_shifts, y),
        grad_proj,
        vec(2),
        vec(3),
        vec(4),
        grad_fc1,
        pick(fc1_shifts, y),
        grad_fc2,
        vec(5),
    )


def solution(mesh):
    slots = P(None, "shard", "ctx", None)
    placed = (
        slots,
        P(None, None, "shard", None),
        P(),
        P(),
        P(None, "shard", "tp"),
        P(None, "tp"),
        P("tp", "shard"),
        P(),
        P(),
        P(),
        P("shard", "tp"),
        P("tp"),
        P("tp", "shard"),
        P(),
        slots,
    )
    return jax.shard_map(
        functools.partial(per_device, shards=mesh.shape["shard"]),
        mesh=mesh,
        in_specs=placed,
        out_specs=(
            slots,
            slots,
            P(),
            P(),
            P(None, "shard", "tp"),
            P(None, "tp"),
            P("tp", "shard"),
            P(),
            P(),
            P(),
            P("shard", "tp"),
            P("tp"),
            P("tp", "shard"),
            P(),
        ),
        check_vma=False,
    )
```

time: 2380 us -> 751 us (0.32)
  waiting for transfers between devices: 1700 us -> 307 us
  matrix products: 374 us -> 116 us
  starting transfers between devices: 12.5 us -> 134 us
  local copies, waits for them, and re-layouts: 127 us -> 56.9 us
  blocking collectives: 61 us -> 0 us
  Pallas kernels: 0 us -> 52.7 us
    reduce_scatter x8 -> x0, waiting for transfers between devices: 664 us -> none  [the longest x1 218 us: per_device(): lax.psum_scatter(weight_grads[2], 'shard', scatter_dimension=0, tiled=True)]
    all_gather x16 -> x0, waiting for transfers between devices: 664 us -> none  [the longest x2 181 us: one_micro(): lax.all_gather(fc1_weight, 'shard', axis=0, tiled=True)]
    dot_general x136 -> x18, matrix products: 374 us -> 116 us  [the longest x15 92.4 us: dg(): lax.dot_general(left, right, (dims, ((), ())), preferred_element_type=F32)]
    psum x9 -> x1, waiting for transfers between devices: 362 us -> 113 us  [per_device(): small = lax.psum(small, AXES)]
    ppermute x0 -> x75, waiting for transfers between devices: none -> 193 us  [send(): return lax.ppermute(value, AXES, pairs)]
    ppermute x0 -> x75, starting transfers between devices: none -> 134 us  [send(): return lax.ppermute(value, AXES, pairs)]
    psum x1 -> x0, blocking collectives: 61 us -> none  [per_device(): lax.psum((totals[4], totals[5], totals[6], totals[7], totals[8], totals[9...]
    while x197 -> x0, local copies, waits for them, and re-layouts: 55.3 us -> none  [the longest x3 29.8 us: per_device(): lax.scan(one_micro, start_sums, (tokens, cotangent, jnp.moveaxis(patch_me...]
  transfers between devices with their start and end apart: 33 -> 76, of which waited for: 24 -> 30; matrix products, arithmetic and copies ran while one was open for 17% -> 30% of each run, Pallas kernels for 0% -> 7%
where the time goes in v1:
time: 751 us; the launch traced here: 740 us
  waiting for transfers between devices  307 us (41%)
  starting transfers between devices  134 us (18%)
  matrix products  116 us (15%)
  other arithmetic  57.9 us (8%)
  local copies, waits for them, and re-layouts  56.9 us (8%)
  Pallas kernels  52.7 us (7%)
  between operations  16.4 us (2%)
    ppermute x75, waiting for transfers between devices, send(): return lax.ppermute(value, AXES, pairs)  193 us
    ppermute x75, starting transfers between devices, send(): return lax.ppermute(value, AXES, pairs)  134 us
    psum x1, waiting for transfers between devices, per_device(): small = lax.psum(small, AXES)  113 us
    dot_general x15, matrix products, dg(): lax.dot_general(left, right, (dims, ((), ())), preferred_element_type=F32)  92.4 us
    pallas_call x1, Pallas kernels, attend(): pl.pallas_call(attend_kernel, grid=(heads,), in_specs=[pl.BlockSpec((3, H...  26.8 us
    pallas_call x1, Pallas kernels, attend_back(): pl.pallas_call(attend_back_kernel, grid=(heads,), in_specs=[pl.BlockSpec(...  25.9 us
  transfers between devices with their start and end apart: 76, of which 30 were waited for; matrix products, arithmetic and copies ran while one was open for 30% of the time, Pallas kernels for 7%

profile of v1, /device:TPU:0, one launch (start us, length us, event | category | flops | bytes accessed | tf_op | source)
XLA Modules:
  0.0 740.3 jit_solution(11486878493275513776)
XLA Ops:
  52.4 6.6 collective-permute-done.28
  88.5 7.9 %collective-permute-start.2 = (bf16[3,160,640]{2,1,0:T(8,128)(2,1)S(1)}, bf16[3,160,640]{2,1,0:T(8,128)(2,1)S(1)}, u32[]{:S(2)}, u32[]{:S(2)}) collective-permute-start(bf16[3,160,640]{2,1,0:T(8,128)(2,1)S(1)} %collective-permute-done.1), channel_id=1, source_target_pairs={{0,1},{3,2},{4,5},{7,6},{8,9},{11,10},{12,13},{15,14},{16,17},{19,... | collective-permute-start | bytes 1843208 | tf_op jit(solution)/shard_map/ppermute | solution.py:228
  149.7 9.5 %collective-permute-done.30 = bf16[160,1280]{1,0:T(8,128)(2,1)} collective-permute-done((bf16[160,1280]{1,0:T(8,128)(2,1)}, bf16[160,1280]{1,0:T(8,128)(2,1)}, u32[]{:S(2)}, u32[]{:S(2)}) %collective-permute-start.30) | collective-permute-done | bytes 409632 | tf_op jit(solution)/shard_map/ppermute | solution.py:228
  159.2 9.1 %collective-permute-start.32 = (bf16[160,1280]{1,0:T(8,128)(2,1)}, bf16[160,1280]{1,0:T(8,128)(2,1)}, u32[]{:S(2)}, u32[]{:S(2)}) collective-permute-start(bf16[160,1280]{1,0:T(8,128)(2,1)} %get-tuple-element.50), channel_id=1, source_target_pairs={{0,24},{1,25},{2,26},{3,27},{4,28},{5,29},{6,30},{7,31},{8,0},{9,1... | collective-permute-start | bytes 1228808 | tf_op jit(solution)/shard_map/ppermute | solution.py:228
  170.4 8.2 %broadcast_add_fusion.x_ref = f32[3,640,1024]{2,1,0:T(8,128)} fusion(f32[3,640]{1,0:T(4,128)S(1)} %broadcast_select_fusion.4, bf16[3,1280,640]{2,1,0:T(8,128)(2,1)S(1)} %bitcast.334, bf16[1024,1280,1]{1,0,2:T(8,128)(2,1)S(1)} %bitcast.350), kind=kOutput, calls=%fused_computation.20 | convolution fusion | flops 5035130880 | bytes 15408640 | tf_op jit(solution)/shard_map/cde,rd->cer/dot_general | solution.py:336
  178.6 26.8 %attend.1 = (bf16[3,640,1024]{2,1,0:T(8,128)(2,1)}, bf16[640,1024]{1,0:T(8,128)(2,1)S(1)}, f32[640,1024]{1,0:T(8,128)S(1)}, f32[8,1,1024]{2,1,0:T(1,128)S(1)}) custom-call(f32[3,640,1024]{2,1,0:T(8,128)} %broadcast_add_fusion.x_ref, f32[40,1024]{1,0:T(8,128)S(1)} %get-tuple-element.69.cos_ref, f32[40,1024]{1,0:T(8,128)S(1)} %get-tuple-element.68.sin_ref, ...), custom_call_target="tpu_custom_call" | custom-call | flops 2684354560 | bytes 17039360 | tf_op jit(solution)/shard_map/attend/pallas_call | solution.py:76
  221.2 8.4 %collective-permute-done.36 = bf16[160,1280]{1,0:T(8,128)(2,1)S(1)} collective-permute-done((bf16[160,1280]{1,0:T(8,128)(2,1)}, bf16[160,1280]{1,0:T(8,128)(2,1)S(1)}, u32[]{:S(2)}, u32[]{:S(2)}) %collective-permute-start.36) | collective-permute-done | bytes 409632 | tf_op jit(solution)/shard_map/ppermute | solution.py:228
  231.0 16.2 %collective-permute-done.38 = bf16[160,1280]{1,0:T(8,128)(2,1)S(1)} collective-permute-done((bf16[160,1280]{1,0:T(8,128)(2,1)}, bf16[160,1280]{1,0:T(8,128)(2,1)S(1)}, u32[]{:S(2)}, u32[]{:S(2)}) %collective-permute-start.38) | collective-permute-done | bytes 409632 | tf_op jit(solution)/shard_map/ppermute | solution.py:228
  257.4 8.2 %fusion.38 = f32[1024,1280]{1,0:T(8,128)} fusion(bf16[1280,1280]{1,0:T(8,128)(2,1)} %bitcast.51, bf16[512,1280]{1,0:T(8,128)(2,1)S(1)} %collective-permute-done.26, bf16[512,1280]{1,0:T(8,128)(2,1)S(1)} %add_convert_fusion.1), kind=kOutput, calls=%fused_computation.90 | convolution fusion | flops 3360686080 | bytes 11141120 | tf_op jit(solution)/shard_map/dot_general | solution.py:25
  265.6 6.2 fusion.62
  273.2 9.1 %convert_reduce_fusion.2 = (f32[1280]{0:T(1024)}, bf16[1024,1280]{1,0:T(8,128)(2,1)S(1)}) fusion(f32[1024,1280]{1,0:T(8,128)} %fusion.38, f32[1280]{0:T(1024)S(1)} %dynamic_slice.138, bf16[1280,1280]{1,0:T(8,128)(2,1)S(1)} %bitcast.340, bf16[512,1280]{1,0:T(8,128)(2,1)S(1)} %get-tuple-element.54, bf16[512,1280]{1,0:T(8,128)(2,1)S(1)} %get-tuple-element.41), kind=kOutput, calls=%fused_computation.7 | convolution fusion | flops 3377724160 | bytes 13772800 | tf_op jit(solution)/shard_map/dot_general | solution.py:25
  292.9 5.7 fusion.37
  298.7 6.4 fusion.73
  305.2 6.9 convert_reduce_fusion.1
  312.1 6.5 fusion.36
  318.7 6.6 fusion.63
  326.5 8.2 %fusion.1 = bf16[1280,1280]{1,0:T(8,128)(2,1)S(1)} fusion(f32[1280,1280]{1,0:T(8,128)} %fusion.36, bf16[512,1280]{1,0:T(8,128)(2,1)S(1)} %get-tuple-element.54, bf16[512,1280]{1,0:T(8,128)(2,1)S(1)} %get-tuple-element.41, f32[1024,1280]{1,0:T(8,128)} %fusion.38, f32[1280]{0:T(1024)S(1)} %dynamic_slice.138), kind=kOutput, calls=%fused_computation.5 | convolution fusion | flops 3373137920 | bytes 17699840 | tf_op jit(solution)/shard_map/dot_general | solution.py:25
  336.4 5.7 fusion.75
  343.8 6.6 fusion
  357.0 16.6 %collective-permute-done.70 = bf16[4,160,1280]{2,1,0:T(8,128)(2,1)} collective-permute-done((bf16[4,160,1280]{2,1,0:T(8,128)(2,1)S(1)}, bf16[4,160,1280]{2,1,0:T(8,128)(2,1)}, u32[]{:S(2)}, u32[]{:S(2)}) %collective-permute-start.70) | collective-permute-done | bytes 1638432 | tf_op jit(solution)/shard_map/ppermute | solution.py:228
  377.4 7.0 collective-permute-done.50
  387.8 23.5 %collective-permute-done.45 = bf16[512,1280]{1,0:T(8,128)(2,1)S(1)} collective-permute-done((bf16[512,1280]{1,0:T(8,128)(2,1)}, bf16[512,1280]{1,0:T(8,128)(2,1)S(1)}, u32[]{:S(2)}, u32[]{:S(2)}) %collective-permute-start.45) | collective-permute-done | bytes 1310752 | tf_op jit(solution)/shard_map/ppermute | solution.py:228
  425.7 25.9 %attend_back.1 = bf16[3,640,1024]{2,1,0:T(8,128)(2,1)} custom-call(bf16[3,640,1024]{2,1,0:T(8,128)(2,1)} %get-tuple-element.19.low_ref, bf16[640,1024]{1,0:T(8,128)(2,1)S(1)} %convolution_convert_fusion.2.grad_ref, f32[640,1024]{1,0:T(8,128)S(1)} %copy-done.3, f32[8,1,1024]{2,1,0:T(1,128)S(1)} %get-tuple-element.21.lse_ref, ...), custom_call_target="tpu_custom_call" | custom-call | flops 6710886400 | bytes 11796480 | tf_op jit(solution)/shard_map/attend_back/pallas_call | solution.py:149
  451.6 9.5 %fusion.2 = bf16[3,1280,640]{2,1,0:T(8,128)(2,1)} fusion(bf16[1024,1280,1]{1,0,2:T(8,128)(2,1)S(1)} %bitcast.351, bf16[3,640,1024]{2,1,0:T(8,128)(2,1)} %attend_back.1), kind=kOutput, calls=%fused_computation.17 | convolution fusion | flops 5035622400 | bytes 11468800 | tf_op jit(solution)/shard_map/cer,rd->cde/dot_general | solution.py:396
  482.7 5.7 convolution_bitcast_fusion
  492.1 9.2 %collective-permute-done.59 = bf16[4,160,640]{2,1,0:T(8,128)(2,1)S(1)} collective-permute-done((bf16[4,160,640]{2,1,0:T(8,128)(2,1)S(1)}, bf16[4,160,640]{2,1,0:T(8,128)(2,1)S(1)}, u32[]{:S(2)}, u32[]{:S(2)}) %collective-permute-start.59) | collective-permute-done | bytes 819232 | tf_op jit(solution)/shard_map/ppermute | solution.py:228
  514.1 8.9 %collective-permute-done.61 = bf16[160,640]{1,0:T(8,128)(2,1)S(1)} collective-permute-done((bf16[160,640]{1,0:T(8,128)(2,1)S(1)}, bf16[160,640]{1,0:T(8,128)(2,1)S(1)}, u32[]{:S(2)}, u32[]{:S(2)}) %collective-permute-start.61) | collective-permute-done | bytes 204832 | tf_op jit(solution)/shard_map/ppermute | solution.py:228
  536.9 12.9 %collective-permute-done.63 = bf16[160,640]{1,0:T(8,128)(2,1)S(1)} collective-permute-done((bf16[160,640]{1,0:T(8,128)(2,1)S(1)}, bf16[160,640]{1,0:T(8,128)(2,1)S(1)}, u32[]{:S(2)}, u32[]{:S(2)}) %collective-permute-start.63) | collective-permute-done | bytes 204832 | tf_op jit(solution)/shard_map/ppermute | solution.py:228
  554.4 10.7 %collective-permute-done.55 = bf16[4,3,160,640]{3,2,0,1:T(8,128)(2,1)S(1)} collective-permute-done((bf16[4,3,160,640]{3,2,0,1:T(8,128)(2,1)S(1)}, bf16[4,3,160,640]{3,2,0,1:T(8,128)(2,1)S(1)}, u32[]{:S(2)}, u32[]{:S(2)}) %collective-permute-start.55) | collective-permute-done | bytes 2457632 | tf_op jit(solution)/shard_map/ppermute | solution.py:228
  580.2 6.4 collective-permute-done.58
  586.6 13.2 %collective-permute-done.57 = bf16[3,160,640]{2,1,0:T(8,128)(2,1)S(1)} collective-permute-done((bf16[3,160,640]{2,1,0:T(8,128)(2,1)S(1)}, bf16[3,160,640]{2,1,0:T(8,128)(2,1)S(1)}, u32[]{:S(2)}, u32[]{:S(2)}) %collective-permute-start.57) | collective-permute-done | bytes 614432 | tf_op jit(solution)/shard_map/ppermute | solution.py:228
  608.8 113.4 %all-reduce.2.cloned.1.call-done = f32[16640]{0:T(1024)} async-done(((f32[16640]{0:T(1024)}), f32[16640]{0:T(1024)}) %all-reduce.2.cloned.1.call-update) | async-done | bytes 66576 | tf_op jit(solution)/shard_map/psum | solution.py:430
  (383 shorter events, 292.2 us)
Async XLA Ops:
  7.2 715.0 %all-reduce.2.cloned.1.call-start = ((), (), s32[]{:S(2)}) async-start(), calls=%async_computation | async-start | bytes 139264 | tf_op jit(solution)/shard_map/psum | solution.py:430
  9.2 59.7 %collective-permute-start.35 = (bf16[160,1280]{1,0:T(8,128)(2,1)}, bf16[160,1280]{1,0:T(8,128)(2,1)}, u32[]{:S(2)}, u32[]{:S(2)}) collective-permute-start(bf16[160,1280]{1,0:T(8,128)(2,1)} %dynamic-slice_bitcast_fusion.19), channel_id=1, source_target_pairs={{0,8},{1,9},{2,10},{3,11},{4,12},{5,13},{6,14},{7,15},{8,16},{9,17... | collective-permute-start | bytes 1228808 | tf_op jit(solution)/shard_map/ppermute | solution.py:228
  12.2 36.8 %collective-permute-start.34 = (bf16[160,1280]{1,0:T(8,128)(2,1)}, bf16[160,1280]{1,0:T(8,128)(2,1)}, u32[]{:S(2)}, u32[]{:S(2)}) collective-permute-start(bf16[160,1280]{1,0:T(8,128)(2,1)} %dynamic-slice_bitcast_fusion.19), channel_id=1, source_target_pairs={{0,4},{1,5},{2,6},{3,7},{4,0},{5,1},{6,2},{7,3},{8,12},{9,13},{10,... | collective-permute-start | bytes 1228808 | tf_op jit(solution)/shard_map/ppermute | solution.py:228
  19.1 81.5 %collective-permute-start.3 = (bf16[3,160,640]{2,1,0:T(8,128)(2,1)}, bf16[3,160,640]{2,1,0:T(8,128)(2,1)}, u32[]{:S(2)}, u32[]{:S(2)}) collective-permute-start(bf16[3,160,640]{2,1,0:T(8,128)(2,1)} %param.19), channel_id=1, source_target_pairs={{0,8},{3,11},{4,12},{7,15},{8,16},{11,19},{12,20},{15,23},{16,24},... | collective-permute-start | bytes 1843208 | tf_op jit(solution)/shard_map/ppermute | solution.py:228
  39.3 48.5 %collective-permute-start.1 = (bf16[3,160,640]{2,1,0:T(8,128)(2,1)S(1)}, bf16[3,160,640]{2,1,0:T(8,128)(2,1)S(1)}, u32[]{:S(2)}, u32[]{:S(2)}) collective-permute-start(bf16[3,160,640]{2,1,0:T(8,128)(2,1)S(1)} %copy-done.25), channel_id=1, source_target_pairs={{0,4},{3,7},{4,0},{7,3},{8,12},{11,15},{12,8},{15,11},{16,20},{19,... | collective-permute-start | bytes 1843208 | tf_op jit(solution)/shard_map/ppermute | solution.py:228
  46.8 51.0 %collective-permute-start = (bf16[3,160,640]{2,1,0:T(8,128)(2,1)S(1)}, bf16[3,160,640]{2,1,0:T(8,128)(2,1)S(1)}, u32[]{:S(2)}, u32[]{:S(2)}) collective-permute-start(bf16[3,160,640]{2,1,0:T(8,128)(2,1)S(1)} %copy-done.25), channel_id=1, source_target_pairs={{0,1},{3,2},{4,5},{7,6},{8,9},{11,10},{12,13},{15,14},{16,17},{19,... | collective-permute-start | bytes 1843208 | tf_op jit(solution)/shard_map/ppermute | solution.py:228
  97.8 33.8 %collective-permute-start.15 = (bf16[512,1280]{1,0:T(8,128)(2,1)S(1)}, bf16[512,1280]{1,0:T(8,128)(2,1)S(1)}, u32[]{:S(2)}, u32[]{:S(2)}) collective-permute-start(bf16[512,1280]{1,0:T(8,128)(2,1)S(1)} %copy-done.21), channel_id=1, source_target_pairs={{0,2},{1,3},{2,0},{3,1},{4,6},{5,7},{6,4},{7,5},{8,10},{9,11},{10,... | collective-permute-start | bytes 3932168 | tf_op jit(solution)/shard_map/ppermute | solution.py:228
  117.2 101.9 %collective-permute-start.37 = (bf16[160,1280]{1,0:T(8,128)(2,1)}, bf16[160,1280]{1,0:T(8,128)(2,1)}, u32[]{:S(2)}, u32[]{:S(2)}) collective-permute-start(bf16[160,1280]{1,0:T(8,128)(2,1)} %dynamic-slice_bitcast_fusion.19), channel_id=1, source_target_pairs={{0,16},{1,17},{2,18},{3,19},{4,20},{5,21},{6,22},{7,23},{8,24},{9,... | collective-permute-start | bytes 1228808 | tf_op jit(solution)/shard_map/ppermute | solution.py:228
  133.6 34.7 %collective-permute-start.12 = (bf16[3,160,640]{2,1,0:T(8,128)(2,1)S(1)}, bf16[3,160,640]{2,1,0:T(8,128)(2,1)S(1)}, u32[]{:S(2)}, u32[]{:S(2)}) collective-permute-start(bf16[3,160,640]{2,1,0:T(8,128)(2,1)S(1)} %collective-permute-done.11), channel_id=1, source_target_pairs={{0,1},{3,2},{4,5},{7,6},{8,9},{11,10},{12,13},{15,14},{16,17},{19,... | collective-permute-start | bytes 1843208 | tf_op jit(solution)/shard_map/ppermute | solution.py:228
  146.7 74.1 %collective-permute-start.39 = (bf16[160,1280]{1,0:T(8,128)(2,1)}, bf16[160,1280]{1,0:T(8,128)(2,1)}, u32[]{:S(2)}, u32[]{:S(2)}) collective-permute-start(bf16[160,1280]{1,0:T(8,128)(2,1)} %dynamic-slice_bitcast_fusion.19), channel_id=1, source_target_pairs={{0,24},{1,25},{2,26},{3,27},{4,28},{5,29},{6,30},{7,31},{8,0},{9,1... | collective-permute-start | bytes 1228808 | tf_op jit(solution)/shard_map/ppermute | solution.py:228
  159.2 57.9 %collective-permute-start.32 = (bf16[160,1280]{1,0:T(8,128)(2,1)}, bf16[160,1280]{1,0:T(8,128)(2,1)}, u32[]{:S(2)}, u32[]{:S(2)}) collective-permute-start(bf16[160,1280]{1,0:T(8,128)(2,1)} %get-tuple-element.50), channel_id=1, source_target_pairs={{0,24},{1,25},{2,26},{3,27},{4,28},{5,29},{6,30},{7,31},{8,0},{9,1... | collective-permute-start | bytes 1228808 | tf_op jit(solution)/shard_map/ppermute | solution.py:228
  168.2 46.5 %collective-permute-start.31 = (bf16[160,1280]{1,0:T(8,128)(2,1)}, bf16[160,1280]{1,0:T(8,128)(2,1)}, u32[]{:S(2)}, u32[]{:S(2)}) collective-permute-start(bf16[160,1280]{1,0:T(8,128)(2,1)} %collective-permute-done.30), channel_id=1, source_target_pairs={{0,4},{1,5},{2,6},{3,7},{4,0},{5,1},{6,2},{7,3},{8,12},{9,13},{10,... | collective-permute-start | bytes 1228808 | tf_op jit(solution)/shard_map/ppermute | solution.py:228
  212.7 34.5 %collective-permute-start.25 = (f32[512,1280]{1,0:T(8,128)S(1)}, f32[512,1280]{1,0:T(8,128)S(1)}, u32[]{:S(2)}, u32[]{:S(2)}) collective-permute-start(f32[512,1280]{1,0:T(8,128)S(1)} %dynamic-slice_bitcast_fusion.1), channel_id=1, source_target_pairs={{0,2},{1,3},{2,0},{3,1},{4,6},{5,7},{6,4},{7,5},{8,10},{9,11},{10,... | collective-permute-start | bytes 7864328 | tf_op jit(solution)/shard_map/ppermute | solution.py:228
  214.8 40.2 %collective-permute-start.47 = (bf16[2,512,1280]{2,1,0:T(8,128)(2,1)S(1)}, bf16[2,512,1280]{2,1,0:T(8,128)(2,1)S(1)}, u32[]{:S(2)}, u32[]{:S(2)}) collective-permute-start(bf16[2,512,1280]{2,1,0:T(8,128)(2,1)S(1)} %bitcast.349), channel_id=1, source_target_pairs={{0,2},{1,3},{2,0},{3,1},{4,6},{5,7},{6,4},{7,5},{8,10},{9,11},{10,... | collective-permute-start | bytes 7864328 | tf_op jit(solution)/shard_map/ppermute | solution.py:228
  273.2 114.5 %collective-permute-start.41 = (bf16[512,1280]{1,0:T(8,128)(2,1)}, bf16[512,1280]{1,0:T(8,128)(2,1)S(1)}, u32[]{:S(2)}, u32[]{:S(2)}) collective-permute-start(bf16[512,1280]{1,0:T(8,128)(2,1)} %slice.138), channel_id=1, source_target_pairs={{0,2},{1,3},{2,0},{3,1},{4,6},{5,7},{6,4},{7,5},{8,10},{9,11},{10,... | collective-permute-start | bytes 3932168 | tf_op jit(solution)/shard_map/ppermute | solution.py:228
  292.3 85.0 %collective-permute-start.48 = (bf16[512,1280]{1,0:T(8,128)(2,1)}, bf16[512,1280]{1,0:T(8,128)(2,1)}, u32[]{:S(2)}, u32[]{:S(2)}) collective-permute-start(bf16[512,1280]{1,0:T(8,128)(2,1)} %slice.136), channel_id=1, source_target_pairs={{0,2},{1,3},{2,0},{3,1},{4,6},{5,7},{6,4},{7,5},{8,10},{9,11},{10,... | collective-permute-start | bytes 3932168 | tf_op jit(solution)/shard_map/ppermute | solution.py:228
  334.8 38.8 %collective-permute-start.70 = (bf16[4,160,1280]{2,1,0:T(8,128)(2,1)S(1)}, bf16[4,160,1280]{2,1,0:T(8,128)(2,1)}, u32[]{:S(2)}, u32[]{:S(2)}) collective-permute-start(bf16[4,160,1280]{2,1,0:T(8,128)(2,1)S(1)} %dynamic-slice_bitcast_fusion.3), channel_id=1, source_target_pairs={{0,4},{1,5},{2,6},{3,7},{4,0},{5,1},{6,2},{7,3},{8,12},{9,13},{10,... | collective-permute-start | bytes 4915208 | tf_op jit(solution)/shard_map/ppermute | solution.py:228
  350.5 64.2 %collective-permute-start.65 = (bf16[4,160,1280]{2,1,0:T(8,128)(2,1)S(1)}, bf16[4,160,1280]{2,1,0:T(8,128)(2,1)}, u32[]{:S(2)}, u32[]{:S(2)}) collective-permute-start(bf16[4,160,1280]{2,1,0:T(8,128)(2,1)S(1)} %dynamic-slice_bitcast_fusion.4), channel_id=1, source_target_pairs={{0,4},{1,5},{2,6},{3,7},{4,0},{5,1},{6,2},{7,3},{8,12},{9,13},{10,... | collective-permute-start | bytes 4915208 | tf_op jit(solution)/shard_map/ppermute | solution.py:228
  373.6 37.8 %collective-permute-start.45 = (bf16[512,1280]{1,0:T(8,128)(2,1)}, bf16[512,1280]{1,0:T(8,128)(2,1)S(1)}, u32[]{:S(2)}, u32[]{:S(2)}) collective-permute-start(bf16[512,1280]{1,0:T(8,128)(2,1)} %fusion.30), channel_id=1, source_target_pairs={{0,1},{1,0},{2,3},{3,2},{4,5},{5,4},{6,7},{7,6},{8,9},{9,8},{10,11... | collective-permute-start | bytes 3932168 | tf_op jit(solution)/shard_map/ppermute | solution.py:228
  377.3 39.5 %collective-permute-start.71 = (bf16[160,1280]{1,0:T(8,128)(2,1)S(1)}, bf16[160,1280]{1,0:T(8,128)(2,1)S(1)}, u32[]{:S(2)}, u32[]{:S(2)}) collective-permute-start(bf16[160,1280]{1,0:T(8,128)(2,1)S(1)} %get-tuple-element.59), channel_id=1, source_target_pairs={{0,8},{1,9},{2,10},{3,11},{4,12},{5,13},{6,14},{7,15},{8,16},{9,17... | collective-permute-start | bytes 1228808 | tf_op jit(solution)/shard_map/ppermute | solution.py:228
  384.4 36.2 %collective-permute-start.73 = (bf16[160,1280]{1,0:T(8,128)(2,1)S(1)}, bf16[160,1280]{1,0:T(8,128)(2,1)S(1)}, u32[]{:S(2)}, u32[]{:S(2)}) collective-permute-start(bf16[160,1280]{1,0:T(8,128)(2,1)S(1)} %get-tuple-element.60), channel_id=1, source_target_pairs={{0,24},{1,25},{2,26},{3,27},{4,28},{5,29},{6,30},{7,31},{8,0},{9,1... | collective-permute-start | bytes 1228808 | tf_op jit(solution)/shard_map/ppermute | solution.py:228
  387.7 32.9 %collective-permute-start.72 = (bf16[160,1280]{1,0:T(8,128)(2,1)S(1)}, bf16[160,1280]{1,0:T(8,128)(2,1)S(1)}, u32[]{:S(2)}, u32[]{:S(2)}) collective-permute-start(bf16[160,1280]{1,0:T(8,128)(2,1)S(1)} %get-tuple-element.61), channel_id=1, source_target_pairs={{0,16},{1,17},{2,18},{3,19},{4,20},{5,21},{6,22},{7,23},{8,24},{9,... | collective-permute-start | bytes 1228808 | tf_op jit(solution)/shard_map/ppermute | solution.py:228
  416.7 45.7 %collective-permute-start.66 = (bf16[160,1280]{1,0:T(8,128)(2,1)S(1)}, bf16[160,1280]{1,0:T(8,128)(2,1)S(1)}, u32[]{:S(2)}, u32[]{:S(2)}) collective-permute-start(bf16[160,1280]{1,0:T(8,128)(2,1)S(1)} %get-tuple-element.62), channel_id=1, source_target_pairs={{0,8},{1,9},{2,10},{3,11},{4,12},{5,13},{6,14},{7,15},{8,16},{9,17... | collective-permute-start | bytes 1228808 | tf_op jit(solution)/shard_map/ppermute | solution.py:228
  416.8 45.6 %collective-permute-start.68 = (bf16[160,1280]{1,0:T(8,128)(2,1)S(1)}, bf16[160,1280]{1,0:T(8,128)(2,1)S(1)}, u32[]{:S(2)}, u32[]{:S(2)}) collective-permute-start(bf16[160,1280]{1,0:T(8,128)(2,1)S(1)} %get-tuple-element.63), channel_id=1, source_target_pairs={{0,24},{1,25},{2,26},{3,27},{4,28},{5,29},{6,30},{7,31},{8,0},{9,1... | collective-permute-start | bytes 1228808 | tf_op jit(solution)/shard_map/ppermute | solution.py:228
  420.6 41.9 %collective-permute-start.67 = (bf16[160,1280]{1,0:T(8,128)(2,1)S(1)}, bf16[160,1280]{1,0:T(8,128)(2,1)S(1)}, u32[]{:S(2)}, u32[]{:S(2)}) collective-permute-start(bf16[160,1280]{1,0:T(8,128)(2,1)S(1)} %get-tuple-element.64), channel_id=1, source_target_pairs={{0,16},{1,17},{2,18},{3,19},{4,20},{5,21},{6,22},{7,23},{8,24},{9,... | collective-permute-start | bytes 1228808 | tf_op jit(solution)/shard_map/ppermute | solution.py:228
  420.8 47.9 %collective-permute-start.74 = (f32[160,1280]{1,0:T(8,128)S(1)}, f32[160,1280]{1,0:T(8,128)S(1)}, u32[]{:S(2)}, u32[]{:S(2)}) collective-permute-start(f32[160,1280]{1,0:T(8,128)S(1)} %fusion.42), channel_id=1, source_target_pairs={{0,2},{1,3},{2,0},{3,1},{4,6},{5,7},{6,4},{7,5},{8,10},{9,11},{10,... | collective-permute-start | bytes 2457608 | tf_op jit(solution)/shard_map/ppermute | solution.py:228
  461.2 66.8 %collective-permute-start.54 = (bf16[3,1280,640]{2,1,0:T(8,128)(2,1)}, bf16[3,1280,640]{2,1,0:T(8,128)(2,1)}, u32[]{:S(2)}, u32[]{:S(2)}) collective-permute-start(bf16[3,1280,640]{2,1,0:T(8,128)(2,1)} %fusion.2), channel_id=1, source_target_pairs={{1,0},{2,3},{5,4},{6,7},{9,8},{10,11},{13,12},{14,15},{17,16},{18,... | collective-permute-start | bytes 14745608 | tf_op jit(solution)/shard_map/ppermute | solution.py:228
  491.5 58.4 %collective-permute-start.52 = (f32[512,1280]{1,0:T(8,128)}, f32[512,1280]{1,0:T(8,128)}, u32[]{:S(2)}, u32[]{:S(2)}) collective-permute-start(f32[512,1280]{1,0:T(8,128)} %dynamic-slice_bitcast_fusion), channel_id=1, source_target_pairs={{0,2},{1,3},{2,0},{3,1},{4,6},{5,7},{6,4},{7,5},{8,10},{9,11},{10,... | collective-permute-start | bytes 7864328 | tf_op jit(solution)/shard_map/ppermute | solution.py:228
  511.6 92.8 %collective-permute-start.46 = (bf16[512,1280]{1,0:T(8,128)(2,1)}, bf16[512,1280]{1,0:T(8,128)(2,1)}, u32[]{:S(2)}, u32[]{:S(2)}) collective-permute-start(bf16[512,1280]{1,0:T(8,128)(2,1)} %get-tuple-element.53), channel_id=1, source_target_pairs={{0,1},{1,0},{2,3},{3,2},{4,5},{5,4},{6,7},{7,6},{8,9},{9,8},{10,11... | collective-permute-start | bytes 3932168 | tf_op jit(solution)/shard_map/ppermute | solution.py:228
  533.2 31.9 %collective-permute-start.55 = (bf16[4,3,160,640]{3,2,0,1:T(8,128)(2,1)S(1)}, bf16[4,3,160,640]{3,2,0,1:T(8,128)(2,1)S(1)}, u32[]{:S(2)}, u32[]{:S(2)}) collective-permute-start(bf16[4,3,160,640]{3,2,0,1:T(8,128)(2,1)S(1)} %dynamic-slice_bitcast_fusion.2), channel_id=1, source_target_pairs={{0,4},{3,7},{4,0},{7,3},{8,12},{11,15},{12,8},{15,11},{16,20},{19,... | collective-permute-start | bytes 7372808 | tf_op jit(solution)/shard_map/ppermute | solution.py:228
  554.3 172.1 %collective-permute-start.53 = (bf16[512,1280]{1,0:T(8,128)(2,1)S(1)}, bf16[512,1280]{1,0:T(8,128)(2,1)}, u32[]{:S(2)}, u32[]{:S(2)}) collective-permute-start(bf16[512,1280]{1,0:T(8,128)(2,1)S(1)} %fusion.19), channel_id=1, source_target_pairs={{0,1},{1,0},{2,3},{3,2},{4,5},{5,4},{6,7},{7,6},{8,9},{9,8},{10,11... | collective-permute-start | bytes 3932168 | tf_op jit(solution)/shard_map/ppermute | solution.py:228
  601.3 129.7 %collective-permute-start.64 = (f32[4,160,640]{2,1,0:T(8,128)}, f32[4,160,640]{2,1,0:T(8,128)}, u32[]{:S(2)}, u32[]{:S(2)}) collective-permute-start(f32[4,160,640]{2,1,0:T(8,128)} %pad_maximum_fusion.9), channel_id=1, source_target_pairs={{0,2},{3,1},{4,6},{7,5},{8,10},{11,9},{12,14},{15,13},{16,18},{19,... | collective-permute-start | bytes 4915208 | tf_op jit(solution)/shard_map/ppermute | solution.py:228
  (96 other events, 1320.1 us)
Sparse Core Ops, SparseCore 0:
  604.6 117.6 all-reduce.1

commit v2 on v1

--- a/solution.py
+++ b/solution.py
@@ -190,6 +190,224 @@
     return jnp.cos(angles), jnp.sin(angles)
 
 
+MESH = pl.DeviceIdType.MESH
+
+
+def remote(src, dst, send_sem, recv_sem, device):
+    return pltpu.make_async_remote_copy(
+        src_ref=src,
+        dst_ref=dst,
+        send_sem=send_sem,
+        recv_sem=recv_sem,
+        device_id=device,
+        device_id_type=MESH,
+    )
+
+
+class Place:
+    def __init__(self, lines):
+        self.lines = lines
+        self.s = lax.axis_index("shard")
+        self.c = lax.axis_index("ctx")
+        self.y = lax.axis_index("tp")
+        self.line = self.s // 2
+        self.side = lax.rem(self.s, 2)
+        self.sib = (self.s, 1 - self.c, self.y)
+        self.peer = (self.s, self.c, 1 - self.y)
+        self.beside = (self.line * 2 + 1 - self.side, self.c, self.y)
+
+    def ahead(self, k):
+        return (lax.rem(self.line + k, self.lines) * 2 + self.side, self.c, self.y)
+
+    def source(self, k):
+        return lax.rem(self.line + self.lines - k, self.lines) * 2
+
+    def greet(self):
+        barrier = pltpu.get_barrier_semaphore()
+        others = [self.sib, self.peer, self.beside] + [self.ahead(k) for k in range(1, self.lines)]
+        for other in others:
+            pl.semaphore_signal(barrier, inc=1, device_id=other, device_id_type=MESH)
+        pl.semaphore_wait(barrier, len(others))
+
+
+def norm_rows(values):
+    center = values - jnp.mean(values, -1, keepdims=True)
+    spread = jnp.mean(center * center, -1, keepdims=True)
+    return center * lax.rsqrt(spread + NORM_EPS)
+
+
+def collect_kernel(
+    lines, pieces, block, tok, gain, shift, dy, qb,
+    out, normed, dy_sib, qb_out,
+    norm_buf, own_sem, zs, zr, xs, xr, ys, yr, ms, mr,
+):
+    at = Place(lines)
+    diag = at.c == at.y
+
+    def part(p, s):
+        j, first, count, _ = pieces[p]
+        return out.at[j, s, :, pl.ds(first, count)]
+
+    def own(p):
+        j, first, count, _ = pieces[p]
+        return block.at[j, :, pl.ds(first, count)]
+
+    def z_copy(p, k, src):
+        return remote(src, part(p, at.s), zs.at[p, k], zr.at[p, k], at.ahead(k))
+
+    def x_copy(p, k, src):
+        return remote(src, part(p, at.source(k) + at.side), xs.at[p, k], xr.at[p, k], at.beside)
+
+    def y_copy(p, i, src, s):
+        return remote(src, part(p, s), ys.at[p, i], yr.at[p, i], at.peer)
+
+    def near(k):
+        return at.source(k) + at.side
+
+    def far(k):
+        return at.source(k) + 1 - at.side
+
+    def z_wait(p, k):
+        z_copy(p, k, part(p, near(k))).wait_recv()
+
+    def x_wait(p, k):
+        x_copy(p, k, part(p, far(k))).wait_recv()
+
+    def y_wait(p, i, s):
+        y_copy(p, i, part(p, s), s).wait_recv()
+
+    late = [p for p in range(len(pieces)) if pieces[p][3]]
+    early = [p for p in range(len(pieces)) if not pieces[p][3]]
+    order = late + early
+    at.greet()
+
+    own_copy = pltpu.make_async_copy(block, out.at[:, at.s], own_sem.at[0])
+    bias_copy = pltpu.make_async_copy(qb, qb_out, own_sem.at[1])
+
+    @pl.when(diag)
+    def _():
+        own_copy.start()
+        bias_copy.start()
+        remote(qb, qb_out, ms.at[0], mr.at[0], at.peer).start()
+        for p in early:
+            y_copy(p, 0, own(p), at.s).start()
+        for p in order:
+            for k in range(1, lines):
+                z_copy(p, k, own(p)).start()
+            x_copy(p, 0, own(p)).start()
+            if p in late:
+                y_copy(p, 0, own(p), at.s).start()
+
+    dy_copy = remote(dy, dy_sib, ms.at[1], mr.at[1], at.sib)
+    dy_copy.start()
+    norm_buf[...] = (norm_rows(tok[...].astype(F32)) * gain[...] + shift[...]).astype(BF16)
+    norm_copy = remote(norm_buf, normed.at[at.c], ms.at[2], mr.at[2], at.sib)
+    norm_copy.start()
+    norm_keep = pltpu.make_async_copy(norm_buf, normed.at[at.c], own_sem.at[2])
+    norm_keep.start()
+
+    @pl.when(diag)
+    def _():
+        for step in range(len(order) + 1):
+            if step < len(order):
+                p = order[step]
+                for k in range(1, lines):
+                    z_wait(p, k)
+                    x_copy(p, k, part(p, near(k))).start()
+                    if p in late:
+                        y_copy(p, k, part(p, near(k)), near(k)).start()
+            if step > 0:
+                p = order[step - 1]
+                for k in range(lines):
+                    x_wait(p, k)
+                    if p in late:
+                        y_copy(p, lines + k, part(p, far(k)), far(k)).start()
+        own_copy.wait()
+        bias_copy.wait()
+        remote(qb, qb_out, ms.at[0], mr.at[0], at.peer).wait_send()
+        for p in order:
+            for k in range(1, lines):
+                z_copy(p, k, own(p)).wait_send()
+            for k in range(lines):
+                x_copy(p, k, part(p, near(k))).wait_send()
+            y_copy(p, 0, own(p), at.s).wait_send()
+            if p in late:
+                for k in range(1, lines):
+                    y_copy(p, k, part(p, near(k)), near(k)).wait_send()
+                for k in range(lines):
+                    y_copy(p, lines + k, part(p, far(k)), far(k)).wait_send()
+
+    @pl.when(jnp.logical_not(diag))
+    def _():
+        for p in early:
+            y_wait(p, 0, at.s)
+            for k in range(1, lines):
+                z_copy(p, k, part(p, at.s)).start()
+            x_copy(p, 0, part(p, at.s)).start()
+        for step in range(len(early) + 1):
+            if step < len(early):
+                p = early[step]
+                for k in range(1, lines):
+                    z_wait(p, k)
+                    x_copy(p, k, part(p, near(k))).start()
+            if step > 0:
+                for k in range(lines):
+                    x_wait(early[step - 1], k)
+        for p in early:
+            for k in range(1, lines):
+                z_copy(p, k, part(p, at.s)).wait_send()
+            for k in range(lines):
+                x_copy(p, k, part(p, near(k))).wait_send()
+        remote(qb, qb_out, ms.at[0], mr.at[0], at.peer).wait_recv()
+        for p in late:
+            for k in range(lines):
+                y_wait(p, k, near(k))
+                y_wait(p, lines + k, far(k))
+
+    dy_copy.wait()
+    norm_copy.wait_send()
+    remote(norm_buf, normed.at[1 - at.c], ms.at[2], mr.at[2], at.sib).wait_recv()
+    norm_keep.wait()
+
+
+def collect(lines, block, tok, gain, shift, dy, qb):
+    groups, rows, inner = block.shape
+    local, width = tok.shape
+    cut = (inner * 3 // 5) // 128 * 128
+    pieces = [(0, 0, inner, True), (1, 0, inner, True), (2, 0, cut, True), (2, cut, inner - cut, False), (3, 0, inner, False)]
+    n = len(pieces)
+    anywhere = pl.BlockSpec(memory_space=pl.ANY)
+    vmem = pl.BlockSpec(memory_space=pltpu.VMEM)
+    dma = pltpu.SemaphoreType.DMA
+    return pl.pallas_call(
+        functools.partial(collect_kernel, lines, pieces),
+        in_specs=[anywhere, vmem, vmem, vmem, anywhere, anywhere],
+        out_specs=[anywhere] * 4,
+        out_shape=[
+            jax.ShapeDtypeStruct((groups, 2 * lines, rows, inner), BF16),
+            jax.ShapeDtypeStruct((2, local, width), BF16),
+            jax.ShapeDtypeStruct(dy.shape, BF16),
+            jax.ShapeDtypeStruct(qb.shape, F32),
+        ],
+        scratch_shapes=[
+            pltpu.VMEM((local, width), BF16),
+            dma((3,)),
+            dma((n, lines)),
+            dma((n, lines)),
+            dma((n, lines)),
+            dma((n, lines)),
+            dma((n, 2 * lines)),
+            dma((n, 2 * lines)),
+            dma((3,)),
+            dma((3,)),
+        ],
+        compiler_params=pltpu.CompilerParams(
+            collective_id=0, has_side_effects=True, vmem_limit_bytes=24 << 20
+        ),
+        name="collect",
+    )(block, tok, gain[None], shift[None], dy, qb)
+
+
 def norm_stats(values):
     center = values - jnp.mean(values, -1, keepdims=True)
     spread = jnp.mean(center * center, -1, keepdims=True)
@@ -307,28 +525,28 @@
         return jnp.where(index == 0, jnp.stack([own, other]), jnp.stack([other, own]))
 
     attn_block = jnp.concatenate([qkv_weight, proj_weight.T[None]], axis=0)
-    early = attn_block[3:]
-    early_peer = net.across(early, on_diag)
-    late_near, late_far = net.gather(attn_block[:3], on_diag)
-    early_near, early_far = net.gather(mine_or(early, early_peer))
-    late_near_peer = [net.across(p, on_diag) for p in late_near]
-    late_far_peer = [net.across(p, on_diag) for p in late_far]
-    late_near = [mine_or(p, q) for p, q in zip(late_near, late_near_peer)]
-    late_far = [mine_or(p, q) for p, q in zip(late_far, late_far_peer)]
-    qkv_full = jnp.moveaxis(net.place(late_near, late_far), 0, 1).reshape(3, width, inner)
-    proj_full = net.place(early_near, early_far).reshape(width, inner)
-
-    fc1_block = lax.dynamic_slice_in_dim(fc1_weight, c * quarter, quarter, 1)
-    fc2_block = lax.dynamic_slice_in_dim(fc2_weight, c * quarter, quarter, 0).T
-    fc1_full = net.place(*net.gather(fc1_block)).reshape(width, quarter)
-    fc2_full = net.place(*net.gather(fc2_block)).reshape(width, quarter)
-    bias_qkv = mine_or(qkv_bias, net.across(qkv_bias, on_diag))
+    grad_out = cotangent.reshape(2, local, width)
+    tok = pick(tokens, y).reshape(local, width)
+    attn_full, normed, grad_out_sib, bias_qkv = collect(
+        net.lines, attn_block, tok, attn_norm_gain, attn_norm_bias, grad_out, qkv_bias
+    )
+    normed = normed.reshape(full, width)
+    qkv_full = attn_full[:3].reshape(3, width, inner)
+    proj_full = attn_full[3].reshape(width, inner)
+
+    fc_block = jnp.stack(
+        [
+            lax.dynamic_slice_in_dim(fc1_weight, c * quarter, quarter, 1),
+            lax.dynamic_slice_in_dim(fc2_weight, c * quarter, quarter, 0).T,
+        ]
+    )
+    fc_block, _ = lax.optimization_barrier((fc_block, bias_qkv))
+    fc_full = net.place(*net.gather(fc_block))
+    fc1_full, fc2_full = [fc_full[:, i].reshape(width, quarter) for i in range(2)]
     bias_fc1 = lax.dynamic_slice_in_dim(fc1_bias, c * quarter, quarter, 0)
 
-    inputs = pick(tokens, y).reshape(local, width).astype(F32)
+    inputs = tok.astype(F32)
     normal_one, inverse_one = norm_stats(inputs)
-    normed_own = (normal_one * attn_norm_gain + attn_norm_bias).astype(BF16)
-    normed = both(normed_own, net.core(normed_own), c).reshape(full, width)
     meta = pick(patch_meta, y, 1).reshape(3, full)
     ids = meta[0]
     cosine, sine = rope_tables(meta[1], meta[2])
@@ -348,8 +566,6 @@
         jnp.concatenate([two_own, net.core(two_own)]),
         jnp.concatenate([two_peer, net.core(two_peer)]),
     ]
-    grad_out = cotangent.reshape(2, local, width)
-    grad_out_sib = net.core(grad_out)
     dy_own = pick(grad_out, y)
     dy = [jnp.concatenate([pick(grad_out, m), pick(grad_out_sib, m)]) for m in (y, 1 - y)]
 

time: 751 us -> 722 us (0.961)
  starting transfers between devices: 134 us -> 56.5 us
  Pallas kernels: 52.7 us -> 130 us
  waiting for transfers between devices: 307 us -> 267 us
  local copies, waits for them, and re-layouts: 56.9 us -> 66.4 us
    ppermute x75 -> x42, starting transfers between devices: 134 us -> 56.4 us  [send(): return lax.ppermute(value, AXES, pairs)]
    pallas_call x0 -> x1, Pallas kernels: none -> 76.9 us  [collect(): pl.pallas_call(functools.partial(collect_kernel, lines, pieces), in_specs...]
    ppermute x75 -> x42, waiting for transfers between devices: 193 us -> 148 us  [send(): return lax.ppermute(value, AXES, pairs)]
    unnamed x115 -> x141, local copies, waits for them, and re-layouts: 7.8 us -> 17.3 us
    dynamic_update_slice x12 -> x4, local copies, waits for them, and re-layouts: 8.97 us -> 1.39 us  [place(): full = lax.dynamic_update_index_in_dim(full, far[k], row + 1 - self.side, 0)]
  transfers between devices with their start and end apart: 76 -> 43, of which waited for: 30 -> 14; matrix products, arithmetic and copies ran while one was open for 30% -> 31% of each run, Pallas kernels for 7% -> 7%
where the time goes in v2:
time: 722 us; the launch traced here: 710 us
  waiting for transfers between devices  267 us (37%)
  Pallas kernels  130 us (18%)
  matrix products  118 us (16%)
  local copies, waits for them, and re-layouts  66.4 us (9%)
  other arithmetic  57.6 us (8%)
  starting transfers between devices  56.5 us (8%)
  between operations  15.7 us (2%)
    ppermute x42, waiting for transfers between devices, send(): return lax.ppermute(value, AXES, pairs)  148 us
    psum x1, waiting for transfers between devices, per_device(): small = lax.psum(small, AXES)  119 us
    dot_general x15, matrix products, dg(): lax.dot_general(left, right, (dims, ((), ())), preferred_element_type=F32)  91.8 us
    pallas_call x1, Pallas kernels, collect(): pl.pallas_call(functools.partial(collect_kernel, lines, pieces), in_specs...  76.9 us
    ppermute x42, starting transfers between devices, send(): return lax.ppermute(value, AXES, pairs)  56.4 us
    pallas_call x1, Pallas kernels, attend(): pl.pallas_call(attend_kernel, grid=(heads,), in_specs=[pl.BlockSpec((3, H...  26.9 us
    pallas_call x1, Pallas kernels, attend_back(): pl.pallas_call(attend_back_kernel, grid=(heads,), in_specs=[pl.BlockSpec(...  25.8 us
    unnamed x141, local copies, waits for them, and re-layouts  17.3 us
  transfers between devices with their start and end apart: 43, of which 14 were waited for; matrix products, arithmetic and copies ran while one was open for 31% of the time, Pallas kernels for 7%

profile of v2, /device:TPU:0, one launch (start us, length us, event | category | flops | bytes accessed | tf_op | source)
XLA Modules:
  0.0 710.4 jit_solution(10691603435134697900)
XLA Ops:
  15.7 76.9 %collect.1 = (bf16[4,8,160,640]{3,2,1,0:T(8,128)(2,1)S(1)}, bf16[2,512,1280]{2,1,0:T(8,128)(2,1)S(1)}, bf16[2,512,1280]{2,1,0:T(8,128)(2,1)S(1)}, f32[3,640]{1,0:T(4,128)S(1)}) custom-call(bf16[4,160,640]{2,1,0:T(8,128)(2,1)S(1)} %pad_maximum_fusion.10.block, bf16[512,1280]{1,0:T(8,128)(2,1)S(1)} %get-tuple-element.57.tok, ...), custom_call_target="tpu_custom_call" | custom-call | tf_op jit(solution)/shard_map/collect/pallas_call | solution.py:382
  107.8 11.0 %broadcast_add_fusion.x_ref = f32[3,640,1024]{2,1,0:T(8,128)} fusion(f32[3,640]{1,0:T(4,128)S(1)} %get-tuple-element.25, bf16[3,1280,640]{2,1,0:T(8,128)(2,1)} %bitcast.228, bf16[1024,1280,1]{1,0,2:T(8,128)(2,1)} %bitcast.216), kind=kOutput, calls=%fused_computation.20 | convolution fusion | flops 5035130880 | bytes 15408640 | tf_op jit(solution)/shard_map/cde,rd->cer/dot_general | solution.py:554
  118.7 26.9 %attend.1 = (bf16[3,640,1024]{2,1,0:T(8,128)(2,1)}, bf16[640,1024]{1,0:T(8,128)(2,1)S(1)}, f32[640,1024]{1,0:T(8,128)S(1)}, f32[8,1,1024]{2,1,0:T(1,128)S(1)}) custom-call(f32[3,640,1024]{2,1,0:T(8,128)} %broadcast_add_fusion.x_ref, f32[40,1024]{1,0:T(8,128)S(1)} %get-tuple-element.80.cos_ref, f32[40,1024]{1,0:T(8,128)S(1)} %get-tuple-element.79.sin_ref, ...), custom_call_target="tpu_custom_call" | custom-call | flops 2684354560 | bytes 17039360 | tf_op jit(solution)/shard_map/attend/pallas_call | solution.py:76
  148.8 6.4 fusion.63
  174.4 16.3 %collective-permute-done.4 = bf16[2,160,1280]{2,1,0:T(8,128)(2,1)S(1)} collective-permute-done((bf16[2,160,1280]{2,1,0:T(8,128)(2,1)}, bf16[2,160,1280]{2,1,0:T(8,128)(2,1)S(1)}, u32[]{:S(2)}, u32[]{:S(2)}) %collective-permute-start.4) | collective-permute-done | bytes 819232 | tf_op jit(solution)/shard_map/ppermute | solution.py:446
  192.0 16.3 %collective-permute-done.6 = bf16[2,160,1280]{2,1,0:T(8,128)(2,1)S(1)} collective-permute-done((bf16[2,160,1280]{2,1,0:T(8,128)(2,1)}, bf16[2,160,1280]{2,1,0:T(8,128)(2,1)S(1)}, u32[]{:S(2)}, u32[]{:S(2)}) %collective-permute-start.6) | collective-permute-done | bytes 819232 | tf_op jit(solution)/shard_map/ppermute | solution.py:446
  215.2 10.2 %collective-permute-done.8 = bf16[2,160,1280]{2,1,0:T(8,128)(2,1)S(1)} collective-permute-done((bf16[2,160,1280]{2,1,0:T(8,128)(2,1)}, bf16[2,160,1280]{2,1,0:T(8,128)(2,1)S(1)}, u32[]{:S(2)}, u32[]{:S(2)}) %collective-permute-start.8) | collective-permute-done | bytes 819232 | tf_op jit(solution)/shard_map/ppermute | solution.py:446
  228.4 5.3 fusion.28
  233.8 14.8 %fusion.52 = f32[1024,1280]{1,0:T(8,128)S(1)} fusion(bf16[1280,1280]{1,0:T(8,128)(2,1)S(1)} %bitcast.237, f32[1024,1280]{1,0:T(8,128)S(1)} %fusion.28, f32[1280]{0:T(1024)S(1)} %dynamic_slice.139), kind=kOutput, calls=%fused_computation.180 | convolution fusion | flops 3364618240 | bytes 13767680 | tf_op jit(solution)/shard_map/dot_general | solution.py:25
  250.9 6.6 convert_reduce_fusion.2
  262.9 7.7 %fusion.27 = f32[1280,1280]{1,0:T(8,128)} fusion(bf16[1024,1280]{1,0:T(8,128)(2,1)S(1)} %get-tuple-element.96, bf16[512,1280]{1,0:T(8,128)(2,1)S(1)} %copy-done.52, bf16[512,1280]{1,0:T(8,128)(2,1)} %add_convert_fusion.1), kind=kOutput, calls=%fused_computation.78 | convolution fusion | flops 3360686080 | bytes 11796480 | tf_op jit(solution)/shard_map/dot_general | solution.py:25
  270.6 6.6 fusion.26
  280.9 6.3 fusion.53
  287.3 7.6 %convert_reduce_fusion.1 = (f32[1280]{0:T(1024)}, bf16[1024,1280]{1,0:T(8,128)(2,1)}) fusion(f32[1024,1280]{1,0:T(8,128)S(1)} %fusion.64, f32[1280]{0:T(1024)S(1)} %dynamic_slice.139, bf16[1280,1280]{1,0:T(8,128)(2,1)S(1)} %bitcast.240, bf16[512,1280]{1,0:T(8,128)(2,1)S(1)} %copy-done.29, bf16[512,1280]{1,0:T(8,128)(2,1)S(1)} %copy-done.28), kind=kOutput, calls=%fused_computation.6 | convolution fusion | flops 3377724160 | bytes 13772800 | tf_op jit(solution)/shard_map/dot_general | solution.py:25
  294.9 8.2 %fusion.1 = bf16[1280,1280]{1,0:T(8,128)(2,1)S(1)} fusion(f32[1280,1280]{1,0:T(8,128)} %fusion.26, bf16[512,1280]{1,0:T(8,128)(2,1)S(1)} %copy-done.29, bf16[512,1280]{1,0:T(8,128)(2,1)S(1)} %copy-done.28, f32[1024,1280]{1,0:T(8,128)} %copy-done.53, f32[1280]{0:T(1024)S(1)} %dynamic_slice.139), kind=kOutput, calls=%fused_computation.5 | convolution fusion | flops 3373137920 | bytes 17699840 | tf_op jit(solution)/shard_map/dot_general | solution.py:25
  312.2 7.3 %fusion = bf16[1280,1280]{1,0:T(8,128)(2,1)S(1)} fusion(f32[1280,1280]{1,0:T(8,128)} %fusion.27, bf16[1024,1280]{1,0:T(8,128)(2,1)S(1)} %copy-done.34, bf16[1024,1280]{1,0:T(8,128)(2,1)} %get-tuple-element.98), kind=kOutput, calls=%fused_computation.4 | convolution fusion | flops 3358720000 | bytes 15073280 | tf_op jit(solution)/shard_map/dot_general | solution.py:25
  325.4 16.5 %collective-permute-done.37 = bf16[4,160,1280]{2,1,0:T(8,128)(2,1)S(1)} collective-permute-done((bf16[4,160,1280]{2,1,0:T(8,128)(2,1)S(1)}, bf16[4,160,1280]{2,1,0:T(8,128)(2,1)S(1)}, u32[]{:S(2)}, u32[]{:S(2)}) %collective-permute-start.37) | collective-permute-done | bytes 1638432 | tf_op jit(solution)/shard_map/ppermute | solution.py:446
  344.5 10.8 %collective-permute-done.17 = bf16[512,1280]{1,0:T(8,128)(2,1)S(1)} collective-permute-done((bf16[512,1280]{1,0:T(8,128)(2,1)S(1)}, bf16[512,1280]{1,0:T(8,128)(2,1)S(1)}, u32[]{:S(2)}, u32[]{:S(2)}) %collective-permute-start.17) | collective-permute-done | bytes 1310752 | tf_op jit(solution)/shard_map/ppermute | solution.py:446
  364.1 18.4 %collective-permute-done.13 = bf16[512,1280]{1,0:T(8,128)(2,1)S(1)} collective-permute-done((bf16[512,1280]{1,0:T(8,128)(2,1)S(1)}, bf16[512,1280]{1,0:T(8,128)(2,1)S(1)}, u32[]{:S(2)}, u32[]{:S(2)}) %collective-permute-start.13) | collective-permute-done | bytes 1310752 | tf_op jit(solution)/shard_map/ppermute | solution.py:446
  398.2 25.8 %attend_back.1 = bf16[3,640,1024]{2,1,0:T(8,128)(2,1)} custom-call(bf16[3,640,1024]{2,1,0:T(8,128)(2,1)} %get-tuple-element.29.low_ref, bf16[640,1024]{1,0:T(8,128)(2,1)S(1)} %convolution_convert_fusion.2.grad_ref, f32[640,1024]{1,0:T(8,128)S(1)} %copy-done.14, f32[8,1,1024]{2,1,0:T(1,128)S(1)} %get-tuple-element.31.lse_ref, ...), custom_call_target="tpu_custom_call" | custom-call | flops 6710886400 | bytes 11796480 | tf_op jit(solution)/shard_map/attend_back/pallas_call | solution.py:149
  424.0 9.4 %fusion.2 = bf16[3,1280,640]{2,1,0:T(8,128)(2,1)} fusion(bf16[1024,1280,1]{1,0,2:T(8,128)(2,1)S(1)} %bitcast.217, bf16[3,640,1024]{2,1,0:T(8,128)(2,1)} %attend_back.1), kind=kOutput, calls=%fused_computation.17 | convolution fusion | flops 5035622400 | bytes 11468800 | tf_op jit(solution)/shard_map/cer,rd->cde/dot_general | solution.py:612
  456.3 5.7 convolution_bitcast_fusion
  465.7 10.2 %collective-permute-done.26 = bf16[4,160,640]{2,1,0:T(8,128)(2,1)S(1)} collective-permute-done((bf16[4,160,640]{2,1,0:T(8,128)(2,1)S(1)}, bf16[4,160,640]{2,1,0:T(8,128)(2,1)S(1)}, u32[]{:S(2)}, u32[]{:S(2)}) %collective-permute-start.26) | collective-permute-done | bytes 819232 | tf_op jit(solution)/shard_map/ppermute | solution.py:446
  482.7 5.7 collective-permute-done.27
  490.4 5.2 collective-permute-done.28
  498.3 5.0 add_convert_fusion
  506.3 15.9 %collective-permute-done.30 = bf16[160,640]{1,0:T(8,128)(2,1)S(1)} collective-permute-done((bf16[160,640]{1,0:T(8,128)(2,1)S(1)}, bf16[160,640]{1,0:T(8,128)(2,1)S(1)}, u32[]{:S(2)}, u32[]{:S(2)}) %collective-permute-start.30) | collective-permute-done | bytes 204832 | tf_op jit(solution)/shard_map/ppermute | solution.py:446
  528.8 6.8 collective-permute-done.22
  536.7 5.9 collective-permute-start.23
  551.6 13.0 %collective-permute-done.24 = bf16[3,160,640]{2,1,0:T(8,128)(2,1)S(1)} collective-permute-done((bf16[3,160,640]{2,1,0:T(8,128)(2,1)S(1)}, bf16[3,160,640]{2,1,0:T(8,128)(2,1)S(1)}, u32[]{:S(2)}, u32[]{:S(2)}) %collective-permute-start.24) | collective-permute-done | bytes 614432 | tf_op jit(solution)/shard_map/ppermute | solution.py:446
  572.7 118.7 %all-reduce.2.cloned.1.call-done = f32[16640]{0:T(1024)} async-done(((f32[16640]{0:T(1024)}), f32[16640]{0:T(1024)}) %all-reduce.2.cloned.1.call-update) | async-done | bytes 66576 | tf_op jit(solution)/shard_map/psum | solution.py:646
  695.6 5.4 fusion.25
  (321 shorter events, 181.8 us)
Async XLA Ops:
  7.2 684.2 %all-reduce.2.cloned.1.call-start = ((), (), s32[]{:S(2)}) async-start(), calls=%async_computation | async-start | bytes 139264 | tf_op jit(solution)/shard_map/psum | solution.py:646
  95.6 76.4 %collective-permute-start.2 = (bf16[2,160,1280]{2,1,0:T(8,128)(2,1)}, bf16[2,160,1280]{2,1,0:T(8,128)(2,1)}, u32[]{:S(2)}, u32[]{:S(2)}) collective-permute-start(bf16[2,160,1280]{2,1,0:T(8,128)(2,1)} %pad_maximum_fusion.11), channel_id=1, source_target_pairs={{0,4},{1,5},{2,6},{3,7},{4,0},{5,1},{6,2},{7,3},{8,12},{9,13},{10,... | collective-permute-start | bytes 2457608 | tf_op jit(solution)/shard_map/ppermute | solution.py:446
  97.1 72.3 %collective-permute-start.3 = (bf16[2,160,1280]{2,1,0:T(8,128)(2,1)}, bf16[2,160,1280]{2,1,0:T(8,128)(2,1)}, u32[]{:S(2)}, u32[]{:S(2)}) collective-permute-start(bf16[2,160,1280]{2,1,0:T(8,128)(2,1)} %pad_maximum_fusion.11), channel_id=1, source_target_pairs={{0,8},{1,9},{2,10},{3,11},{4,12},{5,13},{6,14},{7,15},{8,16},{9,17... | collective-permute-start | bytes 2457608 | tf_op jit(solution)/shard_map/ppermute | solution.py:446
  98.3 71.7 %collective-permute-start.5 = (bf16[2,160,1280]{2,1,0:T(8,128)(2,1)}, bf16[2,160,1280]{2,1,0:T(8,128)(2,1)}, u32[]{:S(2)}, u32[]{:S(2)}) collective-permute-start(bf16[2,160,1280]{2,1,0:T(8,128)(2,1)} %pad_maximum_fusion.11), channel_id=1, source_target_pairs={{0,16},{1,17},{2,18},{3,19},{4,20},{5,21},{6,22},{7,23},{8,24},{9,... | collective-permute-start | bytes 2457608 | tf_op jit(solution)/shard_map/ppermute | solution.py:446
  102.8 68.7 %collective-permute-start.7 = (bf16[2,160,1280]{2,1,0:T(8,128)(2,1)}, bf16[2,160,1280]{2,1,0:T(8,128)(2,1)}, u32[]{:S(2)}, u32[]{:S(2)}) collective-permute-start(bf16[2,160,1280]{2,1,0:T(8,128)(2,1)} %pad_maximum_fusion.11), channel_id=1, source_target_pairs={{0,24},{1,25},{2,26},{3,27},{4,28},{5,29},{6,30},{7,31},{8,0},{9,1... | collective-permute-start | bytes 2457608 | tf_op jit(solution)/shard_map/ppermute | solution.py:446
  158.7 50.9 %collective-permute-start = (f32[512,1280]{1,0:T(8,128)}, f32[512,1280]{1,0:T(8,128)}, u32[]{:S(2)}, u32[]{:S(2)}) collective-permute-start(f32[512,1280]{1,0:T(8,128)} %dynamic-slice_bitcast_fusion.1), channel_id=1, source_target_pairs={{0,2},{1,3},{2,0},{3,1},{4,6},{5,7},{6,4},{7,5},{8,10},{9,11},{10,... | collective-permute-start | bytes 7864328 | tf_op jit(solution)/shard_map/ppermute | solution.py:446
  169.4 21.3 %collective-permute-start.4 = (bf16[2,160,1280]{2,1,0:T(8,128)(2,1)}, bf16[2,160,1280]{2,1,0:T(8,128)(2,1)S(1)}, u32[]{:S(2)}, u32[]{:S(2)}) collective-permute-start(bf16[2,160,1280]{2,1,0:T(8,128)(2,1)} %collective-permute-done.3), channel_id=1, source_target_pairs={{0,4},{1,5},{2,6},{3,7},{4,0},{5,1},{6,2},{7,3},{8,12},{9,13},{10,... | collective-permute-start | bytes 2457608 | tf_op jit(solution)/shard_map/ppermute | solution.py:446
  170.0 38.3 %collective-permute-start.6 = (bf16[2,160,1280]{2,1,0:T(8,128)(2,1)}, bf16[2,160,1280]{2,1,0:T(8,128)(2,1)S(1)}, u32[]{:S(2)}, u32[]{:S(2)}) collective-permute-start(bf16[2,160,1280]{2,1,0:T(8,128)(2,1)} %collective-permute-done.5), channel_id=1, source_target_pairs={{0,4},{1,5},{2,6},{3,7},{4,0},{5,1},{6,2},{7,3},{8,12},{9,13},{10,... | collective-permute-start | bytes 2457608 | tf_op jit(solution)/shard_map/ppermute | solution.py:446
  171.5 53.9 %collective-permute-start.8 = (bf16[2,160,1280]{2,1,0:T(8,128)(2,1)}, bf16[2,160,1280]{2,1,0:T(8,128)(2,1)S(1)}, u32[]{:S(2)}, u32[]{:S(2)}) collective-permute-start(bf16[2,160,1280]{2,1,0:T(8,128)(2,1)} %collective-permute-done.7), channel_id=1, source_target_pairs={{0,4},{1,5},{2,6},{3,7},{4,0},{5,1},{6,2},{7,3},{8,12},{9,13},{10,... | collective-permute-start | bytes 2457608 | tf_op jit(solution)/shard_map/ppermute | solution.py:446
  225.9 44.6 %collective-permute-start.10 = (bf16[512,1280]{1,0:T(8,128)(2,1)}, bf16[512,1280]{1,0:T(8,128)(2,1)S(1)}, u32[]{:S(2)}, u32[]{:S(2)}) collective-permute-start(bf16[512,1280]{1,0:T(8,128)(2,1)} %add_convert_fusion.1), channel_id=1, source_target_pairs={{0,1},{1,0},{2,3},{3,2},{4,5},{5,4},{6,7},{7,6},{8,9},{9,8},{10,11... | collective-permute-start | bytes 3932168 | tf_op jit(solution)/shard_map/ppermute | solution.py:446
  249.9 111.3 %collective-permute-start.9 = (bf16[512,1280]{1,0:T(8,128)(2,1)}, bf16[512,1280]{1,0:T(8,128)(2,1)}, u32[]{:S(2)}, u32[]{:S(2)}) collective-permute-start(bf16[512,1280]{1,0:T(8,128)(2,1)} %slice.156), channel_id=1, source_target_pairs={{0,2},{1,3},{2,0},{3,1},{4,6},{5,7},{6,4},{7,5},{8,10},{9,11},{10,... | collective-permute-start | bytes 3932168 | tf_op jit(solution)/shard_map/ppermute | solution.py:446
  262.3 80.2 %collective-permute-start.15 = (bf16[512,1280]{1,0:T(8,128)(2,1)}, bf16[512,1280]{1,0:T(8,128)(2,1)}, u32[]{:S(2)}, u32[]{:S(2)}) collective-permute-start(bf16[512,1280]{1,0:T(8,128)(2,1)} %slice.154), channel_id=1, source_target_pairs={{0,2},{1,3},{2,0},{3,1},{4,6},{5,7},{6,4},{7,5},{8,10},{9,11},{10,... | collective-permute-start | bytes 3932168 | tf_op jit(solution)/shard_map/ppermute | solution.py:446
  303.2 38.7 %collective-permute-start.37 = (bf16[4,160,1280]{2,1,0:T(8,128)(2,1)S(1)}, bf16[4,160,1280]{2,1,0:T(8,128)(2,1)S(1)}, u32[]{:S(2)}, u32[]{:S(2)}) collective-permute-start(bf16[4,160,1280]{2,1,0:T(8,128)(2,1)S(1)} %dynamic-slice_bitcast_fusion.3), channel_id=1, source_target_pairs={{0,4},{1,5},{2,6},{3,7},{4,0},{5,1},{6,2},{7,3},{8,12},{9,13},{10,... | collective-permute-start | bytes 4915208 | tf_op jit(solution)/shard_map/ppermute | solution.py:446
  319.6 66.7 %collective-permute-start.32 = (bf16[4,160,1280]{2,1,0:T(8,128)(2,1)S(1)}, bf16[4,160,1280]{2,1,0:T(8,128)(2,1)}, u32[]{:S(2)}, u32[]{:S(2)}) collective-permute-start(bf16[4,160,1280]{2,1,0:T(8,128)(2,1)S(1)} %dynamic-slice_bitcast_fusion.4), channel_id=1, source_target_pairs={{0,4},{1,5},{2,6},{3,7},{4,0},{5,1},{6,2},{7,3},{8,12},{9,13},{10,... | collective-permute-start | bytes 4915208 | tf_op jit(solution)/shard_map/ppermute | solution.py:446
  323.7 31.6 %collective-permute-start.17 = (bf16[512,1280]{1,0:T(8,128)(2,1)S(1)}, bf16[512,1280]{1,0:T(8,128)(2,1)S(1)}, u32[]{:S(2)}, u32[]{:S(2)}) collective-permute-start(bf16[512,1280]{1,0:T(8,128)(2,1)S(1)} %fusion.18), channel_id=1, source_target_pairs={{0,1},{1,0},{2,3},{3,2},{4,5},{5,4},{6,7},{7,6},{8,9},{9,8},{10,11... | collective-permute-start | bytes 3932168 | tf_op jit(solution)/shard_map/ppermute | solution.py:446
  341.9 40.6 %collective-permute-start.13 = (bf16[512,1280]{1,0:T(8,128)(2,1)S(1)}, bf16[512,1280]{1,0:T(8,128)(2,1)S(1)}, u32[]{:S(2)}, u32[]{:S(2)}) collective-permute-start(bf16[512,1280]{1,0:T(8,128)(2,1)S(1)} %fusion.20), channel_id=1, source_target_pairs={{0,1},{1,0},{2,3},{3,2},{4,5},{5,4},{6,7},{7,6},{8,9},{9,8},{10,11... | collective-permute-start | bytes 3932168 | tf_op jit(solution)/shard_map/ppermute | solution.py:446
  342.5 48.9 %collective-permute-start.38 = (bf16[160,1280]{1,0:T(8,128)(2,1)S(1)}, bf16[160,1280]{1,0:T(8,128)(2,1)S(1)}, u32[]{:S(2)}, u32[]{:S(2)}) collective-permute-start(bf16[160,1280]{1,0:T(8,128)(2,1)S(1)} %get-tuple-element.69), channel_id=1, source_target_pairs={{0,8},{1,9},{2,10},{3,11},{4,12},{5,13},{6,14},{7,15},{8,16},{9,17... | collective-permute-start | bytes 1228808 | tf_op jit(solution)/shard_map/ppermute | solution.py:446
  356.4 34.9 %collective-permute-start.39 = (bf16[160,1280]{1,0:T(8,128)(2,1)S(1)}, bf16[160,1280]{1,0:T(8,128)(2,1)S(1)}, u32[]{:S(2)}, u32[]{:S(2)}) collective-permute-start(bf16[160,1280]{1,0:T(8,128)(2,1)S(1)} %get-tuple-element.71), channel_id=1, source_target_pairs={{0,16},{1,17},{2,18},{3,19},{4,20},{5,21},{6,22},{7,23},{8,24},{9,... | collective-permute-start | bytes 1228808 | tf_op jit(solution)/shard_map/ppermute | solution.py:446
  361.2 32.5 %collective-permute-start.40 = (bf16[160,1280]{1,0:T(8,128)(2,1)S(1)}, bf16[160,1280]{1,0:T(8,128)(2,1)S(1)}, u32[]{:S(2)}, u32[]{:S(2)}) collective-permute-start(bf16[160,1280]{1,0:T(8,128)(2,1)S(1)} %get-tuple-element.70), channel_id=1, source_target_pairs={{0,24},{1,25},{2,26},{3,27},{4,28},{5,29},{6,30},{7,31},{8,0},{9,1... | collective-permute-start | bytes 1228808 | tf_op jit(solution)/shard_map/ppermute | solution.py:446
  389.3 45.6 %collective-permute-start.33 = (bf16[160,1280]{1,0:T(8,128)(2,1)}, bf16[160,1280]{1,0:T(8,128)(2,1)}, u32[]{:S(2)}, u32[]{:S(2)}) collective-permute-start(bf16[160,1280]{1,0:T(8,128)(2,1)} %get-tuple-element.72), channel_id=1, source_target_pairs={{0,8},{1,9},{2,10},{3,11},{4,12},{5,13},{6,14},{7,15},{8,16},{9,17... | collective-permute-start | bytes 1228808 | tf_op jit(solution)/shard_map/ppermute | solution.py:446
  391.3 43.6 %collective-permute-start.34 = (bf16[160,1280]{1,0:T(8,128)(2,1)}, bf16[160,1280]{1,0:T(8,128)(2,1)}, u32[]{:S(2)}, u32[]{:S(2)}) collective-permute-start(bf16[160,1280]{1,0:T(8,128)(2,1)} %get-tuple-element.74), channel_id=1, source_target_pairs={{0,16},{1,17},{2,18},{3,19},{4,20},{5,21},{6,22},{7,23},{8,24},{9,... | collective-permute-start | bytes 1228808 | tf_op jit(solution)/shard_map/ppermute | solution.py:446
  391.3 43.6 %collective-permute-start.35 = (bf16[160,1280]{1,0:T(8,128)(2,1)}, bf16[160,1280]{1,0:T(8,128)(2,1)}, u32[]{:S(2)}, u32[]{:S(2)}) collective-permute-start(bf16[160,1280]{1,0:T(8,128)(2,1)} %get-tuple-element.73), channel_id=1, source_target_pairs={{0,24},{1,25},{2,26},{3,27},{4,28},{5,29},{6,30},{7,31},{8,0},{9,1... | collective-permute-start | bytes 1228808 | tf_op jit(solution)/shard_map/ppermute | solution.py:446
  394.8 47.3 %collective-permute-start.41 = (f32[160,1280]{1,0:T(8,128)}, f32[160,1280]{1,0:T(8,128)}, u32[]{:S(2)}, u32[]{:S(2)}) collective-permute-start(f32[160,1280]{1,0:T(8,128)} %fusion.32), channel_id=1, source_target_pairs={{0,2},{1,3},{2,0},{3,1},{4,6},{5,7},{6,4},{7,5},{8,10},{9,11},{10,... | collective-permute-start | bytes 2457608 | tf_op jit(solution)/shard_map/ppermute | solution.py:446
  433.4 64.9 %collective-permute-start.21 = (bf16[3,1280,640]{2,1,0:T(8,128)(2,1)}, bf16[3,1280,640]{2,1,0:T(8,128)(2,1)}, u32[]{:S(2)}, u32[]{:S(2)}) collective-permute-start(bf16[3,1280,640]{2,1,0:T(8,128)(2,1)} %fusion.2), channel_id=1, source_target_pairs={{1,0},{2,3},{5,4},{6,7},{9,8},{10,11},{13,12},{14,15},{17,16},{18,... | collective-permute-start | bytes 14745608 | tf_op jit(solution)/shard_map/ppermute | solution.py:446
  455.6 20.3 %collective-permute-start.26 = (bf16[4,160,640]{2,1,0:T(8,128)(2,1)S(1)}, bf16[4,160,640]{2,1,0:T(8,128)(2,1)S(1)}, u32[]{:S(2)}, u32[]{:S(2)}) collective-permute-start(bf16[4,160,640]{2,1,0:T(8,128)(2,1)S(1)} %dynamic-slice_bitcast_fusion.10), channel_id=1, source_target_pairs={{0,4},{1,5},{2,6},{3,7},{4,0},{5,1},{6,2},{7,3},{8,12},{9,13},{10,... | collective-permute-start | bytes 2457608 | tf_op jit(solution)/shard_map/ppermute | solution.py:446
  465.1 58.3 %collective-permute-start.19 = (f32[512,1280]{1,0:T(8,128)}, f32[512,1280]{1,0:T(8,128)}, u32[]{:S(2)}, u32[]{:S(2)}) collective-permute-start(f32[512,1280]{1,0:T(8,128)} %dynamic-slice_bitcast_fusion), channel_id=1, source_target_pairs={{0,2},{1,3},{2,0},{3,1},{4,6},{5,7},{6,4},{7,5},{8,10},{9,11},{10,... | collective-permute-start | bytes 7864328 | tf_op jit(solution)/shard_map/ppermute | solution.py:446
  488.4 80.9 %collective-permute-start.14 = (bf16[512,1280]{1,0:T(8,128)(2,1)}, bf16[512,1280]{1,0:T(8,128)(2,1)}, u32[]{:S(2)}, u32[]{:S(2)}) collective-permute-start(bf16[512,1280]{1,0:T(8,128)(2,1)} %get-tuple-element.63), channel_id=1, source_target_pairs={{0,1},{1,0},{2,3},{3,2},{4,5},{5,4},{6,7},{7,6},{8,9},{9,8},{10,11... | collective-permute-start | bytes 3932168 | tf_op jit(solution)/shard_map/ppermute | solution.py:446
  496.9 25.3 %collective-permute-start.30 = (bf16[160,640]{1,0:T(8,128)(2,1)S(1)}, bf16[160,640]{1,0:T(8,128)(2,1)S(1)}, u32[]{:S(2)}, u32[]{:S(2)}) collective-permute-start(bf16[160,640]{1,0:T(8,128)(2,1)S(1)} %fusion.41), channel_id=1, source_target_pairs={{1,0},{2,3},{5,4},{6,7},{9,8},{10,11},{13,12},{14,15},{17,16},{18,... | collective-permute-start | bytes 614408 | tf_op jit(solution)/shard_map/ppermute | solution.py:446
  503.7 31.9 %collective-permute-start.22 = (bf16[4,3,160,640]{3,2,0,1:T(8,128)(2,1)S(1)}, bf16[4,3,160,640]{3,2,0,1:T(8,128)(2,1)S(1)}, u32[]{:S(2)}, u32[]{:S(2)}) collective-permute-start(bf16[4,3,160,640]{3,2,0,1:T(8,128)(2,1)S(1)} %dynamic-slice_bitcast_fusion.2), channel_id=1, source_target_pairs={{0,4},{3,7},{4,0},{7,3},{8,12},{11,15},{12,8},{15,11},{16,20},{19,... | collective-permute-start | bytes 7372808 | tf_op jit(solution)/shard_map/ppermute | solution.py:446
  528.7 166.9 %collective-permute-start.20 = (bf16[512,1280]{1,0:T(8,128)(2,1)}, bf16[512,1280]{1,0:T(8,128)(2,1)}, u32[]{:S(2)}, u32[]{:S(2)}) collective-permute-start(bf16[512,1280]{1,0:T(8,128)(2,1)} %fusion.14), channel_id=1, source_target_pairs={{0,1},{1,0},{2,3},{3,2},{4,5},{5,4},{6,7},{7,6},{8,9},{9,8},{10,11... | collective-permute-start | bytes 3932168 | tf_op jit(solution)/shard_map/ppermute | solution.py:446
  542.5 22.1 %collective-permute-start.24 = (bf16[3,160,640]{2,1,0:T(8,128)(2,1)S(1)}, bf16[3,160,640]{2,1,0:T(8,128)(2,1)S(1)}, u32[]{:S(2)}, u32[]{:S(2)}) collective-permute-start(bf16[3,160,640]{2,1,0:T(8,128)(2,1)S(1)} %get-tuple-element.68), channel_id=1, source_target_pairs={{0,16},{3,19},{4,20},{7,23},{8,24},{11,27},{12,28},{15,31},{16,0},... | collective-permute-start | bytes 1843208 | tf_op jit(solution)/shard_map/ppermute | solution.py:446
  566.2 134.9 %collective-permute-start.31 = (f32[4,160,640]{2,1,0:T(8,128)}, f32[4,160,640]{2,1,0:T(8,128)}, u32[]{:S(2)}, u32[]{:S(2)}) collective-permute-start(f32[4,160,640]{2,1,0:T(8,128)} %pad_maximum_fusion.9), channel_id=1, source_target_pairs={{0,2},{3,1},{4,6},{7,5},{8,10},{11,9},{12,14},{15,13},{16,18},{19,... | collective-permute-start | bytes 4915208 | tf_op jit(solution)/shard_map/ppermute | solution.py:446
  (76 other events, 1136.6 us)
Sparse Core Ops, SparseCore 0:
  569.4 121.9 all-reduce.1

commit v3 on v2

--- a/solution.py
+++ b/solution.py
@@ -19,6 +19,8 @@
 BF16 = jnp.bfloat16
 AXES = ("shard", "ctx", "tp")
 QB = 256
+AHEAD = 1
+FIRST = 8
 
 
 def dg(left, right, dims, out=F32):
@@ -291,12 +293,9 @@
         remote(qb, qb_out, ms.at[0], mr.at[0], at.peer).start()
         for p in early:
             y_copy(p, 0, own(p), at.s).start()
-        for p in order:
+        for p in order[:AHEAD]:
             for k in range(1, lines):
                 z_copy(p, k, own(p)).start()
-            x_copy(p, 0, own(p)).start()
-            if p in late:
-                y_copy(p, 0, own(p), at.s).start()
 
     dy_copy = remote(dy, dy_sib, ms.at[1], mr.at[1], at.sib)
     dy_copy.start()
@@ -311,6 +310,12 @@
         for step in range(len(order) + 1):
             if step < len(order):
                 p = order[step]
+                if step + AHEAD < len(order):
+                    for k in range(1, lines):
+                        z_copy(order[step + AHEAD], k, own(order[step + AHEAD])).start()
+                x_copy(p, 0, own(p)).start()
+                if p in late:
+                    y_copy(p, 0, own(p), at.s).start()
                 for k in range(1, lines):
                     z_wait(p, k)
                     x_copy(p, k, part(p, near(k))).start()
@@ -374,7 +379,7 @@
     groups, rows, inner = block.shape
     local, width = tok.shape
     cut = (inner * 3 // 5) // 128 * 128
-    pieces = [(0, 0, inner, True), (1, 0, inner, True), (2, 0, cut, True), (2, cut, inner - cut, False), (3, 0, inner, False)]
+    pieces = [(j, f, n, i < 5) for i, (j, f, n) in enumerate((j, f, n) for j in range(4) for f, n in ((0, cut), (cut, inner - cut)))]
     n = len(pieces)
     anywhere = pl.BlockSpec(memory_space=pl.ANY)
     vmem = pl.BlockSpec(memory_space=pltpu.VMEM)
@@ -408,6 +413,535 @@
     )(block, tok, gain[None], shift[None], dy, qb)
 
 
+class Scatter:
+    def __init__(self, at, src, xbuf, zbuf, zin, xs, xr, zs, zr):
+        self.at, self.src, self.xbuf, self.zbuf, self.zin = at, src, xbuf, zbuf, zin
+        self.xs, self.xr, self.zs, self.zr = xs, xr, zs, zr
+
+    def x_copy(self):
+        return remote(self.src.at[:, 1 - self.at.side], self.xbuf, self.xs, self.xr, self.at.beside)
+
+    def z_copy(self, k):
+        row = lax.rem(self.at.line + k, self.at.lines)
+        return remote(self.zbuf.at[row], self.zin.at[k], self.zs.at[k], self.zr.at[k], self.at.ahead(k))
+
+    def start(self):
+        self.x_copy().start()
+
+    def middle(self):
+        self.x_copy().wait_recv()
+        for row in range(self.at.lines):
+            total = self.src[row, self.at.side].astype(F32) + self.xbuf[row].astype(F32)
+            self.zbuf[row] = total.astype(BF16)
+        for k in range(1, self.at.lines):
+            self.z_copy(k).start()
+
+    def finish(self):
+        total = self.src[self.at.line, self.at.side].astype(F32) + self.xbuf[self.at.line].astype(F32)
+        for k in range(1, self.at.lines):
+            self.z_copy(k).wait_recv()
+            total += self.zin[k].astype(F32)
+        return total
+
+    def drain(self):
+        self.x_copy().wait_send()
+        for k in range(1, self.at.lines):
+            self.z_copy(k).wait_send()
+
+
+def flow(units, ahead, begin, done):
+    count = len(units)
+    for i in range(min(ahead, count)):
+        begin(i)
+    for step in range(count + 1):
+        if step < count:
+            if step + ahead < count:
+                begin(step + ahead)
+            units[step].middle()
+        if step > 0:
+            done(step - 1, units[step - 1].finish())
+
+
+def settle_kernel(
+    lines, pieces, fc_cols, attn, fc, grad_in, vec,
+    attn_out, fc_out, grad_peer, vec_out,
+    ax, az, ai, ay, al, fx, fz, fi, vbuf, vin,
+    axs, axr, azs, azr, ays, ayr, fxs, fxr, fzs, fzr, cs, cr, fs, fr, vs, vr, ms, mr,
+):
+    at = Place(lines)
+    diag = at.c == at.y
+    rows = attn.shape[3]
+    first = [p for p in range(len(pieces)) if pieces[p][3]]
+    last = [p for p in range(len(pieces)) if not pieces[p][3]]
+
+    def cut(ref, p):
+        _, start, count, _ = pieces[p]
+        return ref.at[..., pl.ds(start, count)]
+
+    def attn_unit(p, src):
+        j = pieces[p][0]
+        return Scatter(
+            at, src, cut(ax.at[j], p), cut(az.at[j], p), cut(ai.at[j], p),
+            axs.at[p], axr.at[p], azs.at[p], azr.at[p],
+        )
+
+    def pair_copy(p, half):
+        side = (1 - at.side, at.side)[half]
+        j = pieces[p][0]
+        return remote(
+            cut(attn.at[j, :, side], p), cut(ay.at[j, :, side], p), ays.at[p, half], ayr.at[p, half], at.peer
+        )
+
+    def last_copy(p):
+        j = pieces[p][0]
+        here = cut(al.at[j, 0], p)
+        return remote(here, cut(al.at[j, 1], p), ays.at[p, 0], ayr.at[p, 0], at.peer)
+
+    def attn_share(p):
+        here = cut(attn_out.at[pieces[p][0]], p)
+        return remote(here, here, cs.at[p], cr.at[p], at.sib)
+
+    wide = fc_cols[0][2]
+    fc_units = [
+        Scatter(
+            at, fc.at[m, :, :, :, pl.ds(start, wide)], fx.at[i], fz.at[i], fi.at[i],
+            fxs.at[i], fxr.at[i], fzs.at[i], fzr.at[i],
+        )
+        for i, (m, start, _) in enumerate(fc_cols)
+    ]
+
+    def fc_share(i):
+        m, start, _ = fc_cols[i]
+        here = fc_out.at[at.c, m, :, pl.ds(start, wide)]
+        return remote(here, here, fs.at[i], fr.at[i], at.sib)
+
+    def fc_arrive(i):
+        m, start, _ = fc_cols[i]
+        there = fc_out.at[1 - at.c, m, :, pl.ds(start, wide)]
+        return remote(there, there, fs.at[i], fr.at[i], at.sib)
+
+    def fc_done(i, total):
+        m, start, _ = fc_cols[i]
+        fc_out[at.c, m, :, start : start + wide] = total
+        fc_share(i).start()
+
+    at.greet()
+
+    @pl.when(jnp.logical_not(diag))
+    def _():
+        for p in first:
+            for half in range(2):
+                pair_copy(p, half).start()
+
+    grad_copy = remote(grad_in, grad_peer, ms, mr, at.peer)
+    grad_copy.start()
+
+    def small_copy(stage, src, device):
+        return remote(src, vin.at[stage], vs.at[stage], vr.at[stage], device)
+
+    steps = [at.sib, at.peer, at.beside]
+
+    def small_start(stage):
+        small_copy(stage, vec if stage == 0 else vbuf.at[stage - 1], steps[stage]).start()
+
+    def small_add(stage):
+        small_copy(stage, vbuf.at[0], steps[stage]).wait_recv()
+        before = vec[...] if stage == 0 else vbuf[stage - 1]
+        vbuf[stage] = before + vin[stage]
+
+    def line_copy(k):
+        return remote(vbuf.at[2], vin.at[3 + at.line], vs.at[2 + k], vr.at[2 + k], at.ahead(k))
+
+    def line_wait(k):
+        remote(
+            vbuf.at[2], vin.at[3 + at.source(k) // 2], vs.at[2 + k], vr.at[2 + k], at.ahead(k)
+        ).wait_recv()
+
+    small_start(0)
+    small_add(0)
+    small_start(1)
+    flow(fc_units, 1, lambda i: fc_units[i].start(), fc_done)
+    small_add(1)
+    small_start(2)
+
+    @pl.when(diag)
+    def _():
+        units = [attn_unit(p, cut(attn.at[pieces[p][0]], p)) for p in last]
+        units += [attn_unit(p, cut(ay.at[pieces[p][0]], p)) for p in first]
+        order = last + first
+
+        def begin(i):
+            p = order[i]
+            if p in first:
+                j, start, count, _ = pieces[p]
+                for half in range(2):
+                    pair_copy(p, half).wait_recv()
+                for row in range(lines):
+                    for side in range(2):
+                        both = cut(attn.at[j, row, side], p)[...].astype(F32)
+                        both = both + cut(ay.at[j, row, side], p)[...].astype(F32)
+                        ay[j, row, side, :, start : start + count] = both.astype(BF16)
+            units[i].start()
+
+        def done(i, total):
+            p = order[i]
+            j, start, count, _ = pieces[p]
+            if p in last:
+                last_copy(p).wait_recv()
+                total = total + cut(al.at[j, 1], p)[...].astype(F32)
+            attn_out[j, :, start : start + count] = total
+            attn_share(p).start()
+
+        flow(units, 1, begin, done)
+        for unit in units:
+            unit.drain()
+        for p in order:
+            attn_share(p).wait_send()
+
+    @pl.when(jnp.logical_not(diag))
+    def _():
+        units = [attn_unit(p, cut(attn.at[pieces[p][0]], p)) for p in last]
+
+        def done(i, total):
+            j, start, count, _ = pieces[last[i]]
+            al[j, 0, :, start : start + count] = total.astype(BF16)
+            last_copy(last[i]).start()
+
+        flow(units, 1, lambda i: units[i].start(), done)
+        for unit in units:
+            unit.drain()
+        for p in last:
+            last_copy(p).wait_send()
+        for p in first:
+            for half in range(2):
+                pair_copy(p, half).wait_send()
+        for p in first + last:
+            attn_share(p).wait_recv()
+
+    small_add(2)
+    for k in range(1, lines):
+        line_copy(k).start()
+    vin[3 + at.line] = vbuf[2]
+    for k in range(1, lines):
+        line_wait(k)
+    total = vin[3]
+    for row in range(1, lines):
+        total = total + vin[3 + row]
+    vec_out[...] = total
+    small_copy(0, vec, at.sib).wait_send()
+    small_copy(1, vbuf.at[0], at.peer).wait_send()
+    small_copy(2, vbuf.at[1], at.beside).wait_send()
+    for k in range(1, lines):
+        line_copy(k).wait_send()
+    for i, unit in enumerate(fc_units):
+        unit.drain()
+        fc_share(i).wait_send()
+        fc_arrive(i).wait_recv()
+    grad_copy.wait()
+
+
+def settle(lines, attn, fc, grad_in, vec):
+    groups, _, _, rows, inner = attn.shape
+    mats, quarter = fc.shape[0], fc.shape[4]
+    cut = (inner * 3 // 5) // 128 * 128
+    columns = ((0, cut), (cut, inner - cut))
+    pieces = [(j, f, n, 2 * j + i < FIRST) for j in range(groups) for i, (f, n) in enumerate(columns)]
+    wide = quarter // 2 // 128 * 128
+    fc_cols = [(m, f, wide) for m in range(mats) for f in (0, wide)]
+    n, fn = len(pieces), len(fc_cols)
+    anywhere = pl.BlockSpec(memory_space=pl.ANY)
+    vmem = pl.BlockSpec(memory_space=pltpu.VMEM)
+    dma = pltpu.SemaphoreType.DMA
+    stage = (groups, lines, rows, inner)
+    fstage = (fn, lines, rows, wide)
+    return pl.pallas_call(
+        functools.partial(settle_kernel, lines, pieces, fc_cols),
+        in_specs=[vmem, vmem, anywhere, vmem],
+        out_specs=[vmem, vmem, anywhere, vmem],
+        out_shape=[
+            jax.ShapeDtypeStruct((groups, rows, inner), F32),
+            jax.ShapeDtypeStruct((2, mats, rows, quarter), F32),
+            jax.ShapeDtypeStruct(grad_in.shape, BF16),
+            jax.ShapeDtypeStruct(vec.shape, F32),
+        ],
+        scratch_shapes=[
+            pltpu.VMEM(stage, BF16),
+            pltpu.VMEM(stage, BF16),
+            pltpu.VMEM(stage, BF16),
+            pltpu.VMEM(attn.shape, BF16),
+            pltpu.VMEM((groups, 2, rows, inner), BF16),
+            pltpu.VMEM(fstage, BF16),
+            pltpu.VMEM(fstage, BF16),
+            pltpu.VMEM(fstage, BF16),
+            pltpu.VMEM((3,) + vec.shape, F32),
+            pltpu.VMEM((3 + lines,) + vec.shape, F32),
+            dma((n,)), dma((n,)), dma((n, lines)), dma((n, lines)), dma((n, 2)), dma((n, 2)),
+            dma((fn,)), dma((fn,)), dma((fn, lines)), dma((fn, lines)),
+            dma((n,)), dma((n,)), dma((fn,)), dma((fn,)), dma((2 + lines,)), dma((2 + lines,)),
+            dma, dma,
+        ],
+        compiler_params=pltpu.CompilerParams(
+            collective_id=1, has_side_effects=True, vmem_limit_bytes=60 << 20
+        ),
+        name="settle",
+    )(attn, fc, grad_in, vec)
+
+
+TILE = 256
+
+
+def feed_kernel(
+    lines, part, tok, proj_bias, gain, shift, b1, b2, w1_in, w2_in, dy_in, dy_sib,
+    d_attn, d_hid, base, mlp_other, g1, g2, vec,
+    w1, w2, two, dy, act, dpre, hid, part_in, sbuf, rbuf, mbuf, ybuf, yin, acc, low_tile, grad_tile, out_low,
+    loads, ps, pr, ns, nr, ss, sr, ts, tr, ys, yr, os, dos, dor, gs,
+):
+    at = Place(lines)
+    c, y = at.c, at.y
+    local = tok.shape[0]
+    tiles = local // TILE
+
+    def rows(g, q):
+        return pl.ds((g * tiles + q) * TILE, TILE)
+
+    def group(g):
+        return pl.ds(g * local, local)
+
+    def near_rows(q):
+        return pl.ds(q * TILE, TILE)
+
+    copies = [
+        pltpu.make_async_copy(w1_in, w1, loads.at[0]),
+        pltpu.make_async_copy(w2_in, w2, loads.at[1]),
+        pltpu.make_async_copy(dy_in.at[y], dy.at[group(0)], loads.at[2]),
+        pltpu.make_async_copy(dy_sib.at[y], dy.at[group(1)], loads.at[3]),
+        pltpu.make_async_copy(dy_in.at[1 - y], dy.at[group(2)], loads.at[4]),
+        pltpu.make_async_copy(dy_sib.at[1 - y], dy.at[group(3)], loads.at[5]),
+    ]
+    for copy in copies:
+        copy.start()
+    at.greet()
+    part_copy = remote(part.at[1 - c], part_in, ps, pr, at.sib)
+    part_copy.start()
+
+    def two_sib(q):
+        return remote(two.at[rows(0, q)], two.at[rows(1, q)], ns.at[0, q], nr.at[0, q], at.sib)
+
+    def two_peer(q):
+        return remote(two.at[rows(0, q)], two.at[rows(2, q)], ns.at[1, q], nr.at[1, q], at.peer)
+
+    def two_pass(q):
+        return remote(two.at[rows(2, q)], two.at[rows(3, q)], ns.at[2, q], nr.at[2, q], at.sib)
+
+    part_copy.wait_recv()
+    for q in range(tiles):
+        r = near_rows(q)
+        value = tok[r].astype(F32) + part[c, r].astype(F32) + part_in[r].astype(F32) + proj_bias[...]
+        hid[r] = value
+        two[rows(0, q)] = (norm_rows(value) * gain[...] + shift[...]).astype(BF16)
+        two_peer(q).start()
+        two_sib(q).start()
+
+    def first_layer(start, count):
+        def body(i, carry):
+            r = pl.ds(pl.multiple_of((start + i) * TILE, TILE), TILE)
+            pre = dg(two[r], w1[...], ((1,), (0,))) + b1[...]
+            sig = jax.nn.sigmoid(GELU * pre)
+            act[r] = (pre * sig).astype(BF16)
+            dpre[r] = (sig + GELU * pre * sig * (1.0 - sig)).astype(BF16)
+            return carry
+
+        lax.fori_loop(0, count, body, 0)
+
+    copies[0].wait()
+    first_layer(0, tiles)
+    for q in range(tiles):
+        two_sib(q).wait_recv()
+    first_layer(tiles, tiles)
+    for q in range(tiles):
+        two_peer(q).wait_recv()
+        two_pass(q).start()
+        first_layer(2 * tiles + q, 1)
+    for q in range(tiles):
+        two_pass(q).wait_recv()
+    first_layer(3 * tiles, tiles)
+    for copy in copies[1:]:
+        copy.wait()
+
+    shift_sum = jnp.zeros((1, b1.shape[1]), F32)
+
+    def to_norm(g, q):
+        r = rows(g, q)
+        low = (dg(dy[r], w2[...], ((1,), (0,))) * dpre[r].astype(F32)).astype(BF16)
+        dpre[r] = low
+        return dg(low, w1[...], ((1,), (1,))), jnp.sum(low.astype(F32), axis=0, keepdims=True)
+
+    def swap(kind, q):
+        r = near_rows(q)
+        return remote(sbuf.at[kind, r], rbuf.at[kind, r], ss.at[kind, q], sr.at[kind, q], at.sib)
+
+    def y_copy(q):
+        r = near_rows(q)
+        return remote(ybuf.at[r], yin.at[r], ys.at[q], yr.at[q], at.peer)
+
+    for kind in range(2):
+        for q in range(tiles):
+            r = near_rows(q)
+            value, total = to_norm(3 - 2 * kind, q)
+            sbuf[kind, r] = value.astype(BF16)
+            shift_sum += total
+            swap(kind, q).start()
+            value, total = to_norm(2 - 2 * kind, q)
+            shift_sum += total
+            swap(kind, q).wait_recv()
+            value += rbuf[kind, r].astype(F32)
+            if kind == 0:
+                ybuf[r] = value.astype(BF16)
+                y_copy(q).start()
+            else:
+                acc[r] = value
+
+    def weight_grad(left, right, out, sem):
+        count = out.shape[0] // TILE
+
+        def copy(i):
+            slot = lax.rem(i, 2)
+            where = pl.ds(pl.multiple_of(i * TILE, TILE), TILE)
+            return pltpu.make_async_copy(grad_tile.at[slot], out.at[where], sem.at[slot])
+
+        def body(i, carry):
+            cols = pl.ds(pl.multiple_of(i * TILE, TILE), TILE)
+
+            @pl.when(i >= 2)
+            def _():
+                copy(i - 2).wait()
+
+            grad_tile[lax.rem(i, 2)] = dg(left[:, cols], right[...], ((0,), (0,))).astype(BF16)
+            copy(i).start()
+            return carry
+
+        lax.fori_loop(0, count, body, 0)
+        for i in range(max(0, count - 2), count):
+            copy(i).wait()
+
+    weight_grad(dy, act, g2, gs)
+    weight_grad(two, dpre, g1, gs)
+
+    def swap_out(kind, q):
+        r = near_rows(q)
+        return remote(sbuf.at[kind, r], mbuf.at[kind, r], ts.at[kind, q], tr.at[kind, q], at.sib)
+
+    for kind in range(2):
+        for q in range(tiles):
+            r = near_rows(q)
+            swap(kind, q).wait_send()
+            sbuf[kind, r] = dg(act[rows(3 - 2 * kind, q)], w2[...], ((1,), (1,)), BF16)
+            swap_out(kind, q).start()
+            value = dg(act[rows(2 - 2 * kind, q)], w2[...], ((1,), (1,)))
+            swap_out(kind, q).wait_recv()
+            value += mbuf[kind, r].astype(F32)
+            if kind == 0:
+                mlp_other[r] = value.astype(BF16)
+            else:
+                base[r] = hid[r] + value + b2[...]
+
+    def attn_copy(q):
+        r = near_rows(q)
+        return remote(out_low.at[r], d_attn.at[c, r], dos.at[q], dor.at[q], at.sib)
+
+    def attn_keep(q):
+        r = near_rows(q)
+        return pltpu.make_async_copy(out_low.at[r], d_attn.at[c, r], os.at[q])
+
+    sums = [jnp.zeros((1, tok.shape[1]), F32) for _ in range(4)]
+    for q in range(tiles):
+        r = near_rows(q)
+        y_copy(q).wait_recv()
+        grad = acc[r] + yin[r].astype(F32)
+        value = hid[r]
+        center = value - jnp.mean(value, -1, keepdims=True)
+        inverse = lax.rsqrt(jnp.mean(center * center, -1, keepdims=True) + NORM_EPS)
+        normal = center * inverse
+        out_grad = dy[rows(0, q)].astype(F32)
+        total = out_grad + norm_back(grad, normal, inverse, gain[...])
+        low = total.astype(BF16)
+        d_hid[r] = total
+        out_low[r] = low
+        attn_copy(q).start()
+        attn_keep(q).start()
+        for i, t in enumerate((low.astype(F32), grad * normal, grad, out_grad)):
+            sums[i] += jnp.sum(t, axis=0, keepdims=True)
+    for i in range(4):
+        vec[i : i + 1] = sums[i]
+    vec[4:5] = shift_sum
+    vec[5:8] = jnp.zeros((3, tok.shape[1]), F32)
+
+    part_copy.wait_send()
+    for q in range(tiles):
+        two_sib(q).wait_send()
+        two_peer(q).wait_send()
+        two_pass(q).wait_send()
+        y_copy(q).wait_send()
+        for kind in range(2):
+            swap_out(kind, q).wait_send()
+        attn_copy(q).wait_send()
+        attn_keep(q).wait()
+        there = d_attn.at[1 - c, near_rows(q)]
+        remote(there, there, dos.at[q], dor.at[q], at.sib).wait_recv()
+
+
+def feed(lines, part, tok, proj_bias, gain, shift, b1, b2, w1, w2, dy, dy_sib):
+    local, width = tok.shape
+    quarter = w1.shape[1]
+    tiles = local // TILE
+    anywhere = pl.BlockSpec(memory_space=pl.ANY)
+    vmem = pl.BlockSpec(memory_space=pltpu.VMEM)
+    dma = pltpu.SemaphoreType.DMA
+    slots = pltpu.VMEM((local, width), BF16)
+    shape = jax.ShapeDtypeStruct
+    return pl.pallas_call(
+        functools.partial(feed_kernel, lines),
+        in_specs=[vmem] * 7 + [anywhere] * 4,
+        out_specs=[anywhere, vmem, vmem, vmem, anywhere, anywhere, vmem],
+        out_shape=[
+            shape((2, local, width), BF16),
+            shape((local, width), F32),
+            shape((local, width), F32),
+            shape((local, width), BF16),
+            shape((width, quarter), BF16),
+            shape((width, quarter), BF16),
+            shape((8, width), F32),
+        ],
+        scratch_shapes=[
+            pltpu.VMEM((width, quarter), BF16),
+            pltpu.VMEM((width, quarter), BF16),
+            pltpu.VMEM((4 * local, width), BF16),
+            pltpu.VMEM((4 * local, width), BF16),
+            pltpu.VMEM((4 * local, quarter), BF16),
+            pltpu.VMEM((4 * local, quarter), BF16),
+            pltpu.VMEM((local, width), F32),
+            slots,
+            pltpu.VMEM((2, local, width), BF16),
+            pltpu.VMEM((2, local, width), BF16),
+            pltpu.VMEM((2, local, width), BF16),
+            slots,
+            slots,
+            pltpu.VMEM((local, width), F32),
+            pltpu.VMEM((8, 128), BF16),
+            pltpu.VMEM((2, TILE, quarter), BF16),
+            slots,
+            dma((6,)), dma, dma,
+            dma((3, tiles)), dma((3, tiles)),
+            dma((2, tiles)), dma((2, tiles)), dma((2, tiles)), dma((2, tiles)),
+            dma((tiles,)), dma((tiles,)), dma((tiles,)), dma((tiles,)), dma((tiles,)), dma((2,)),
+        ],
+        compiler_params=pltpu.CompilerParams(
+            collective_id=2, has_side_effects=True, vmem_limit_bytes=63 << 20
+        ),
+        name="feed",
+    )(part, tok, proj_bias[None], gain[None], shift[None], b1[None], b2[None], w1, w2, dy, dy_sib)
+
+
 def norm_stats(values):
     center = values - jnp.mean(values, -1, keepdims=True)
     spread = jnp.mean(center * center, -1, keepdims=True)
@@ -555,57 +1089,14 @@
         + bias_qkv[:, :, None]
     )
     low, mixed, mixed_f, lse = attend(qkv, cosine, sine, ids)
-    attn_part = dg(mixed, proj_full, ((0,), (1,))).reshape(2, local, width)
-    attn_own = pick(attn_part, c) + net.core(pick(attn_part, 1 - c))
-    hidden = inputs + attn_own + proj_bias
-
-    normal_two, inverse_two = norm_stats(hidden)
-    two_own = (normal_two * mlp_norm_gain + mlp_norm_bias).astype(BF16)
-    two_peer = net.across(two_own)
-    two = [
-        jnp.concatenate([two_own, net.core(two_own)]),
-        jnp.concatenate([two_peer, net.core(two_peer)]),
-    ]
-    dy_own = pick(grad_out, y)
-    dy = [jnp.concatenate([pick(grad_out, m), pick(grad_out_sib, m)]) for m in (y, 1 - y)]
-
-    acts, d_pres, d_twos = [], [], []
-    for part, dy_part in zip(two, dy):
-        pre = dg(part, fc1_full, ((1,), (0,))) + bias_fc1
-        sig = jax.nn.sigmoid(GELU * pre)
-        acts.append((pre * sig).astype(BF16))
-        d_act = dg(dy_part, fc2_full, ((1,), (0,)))
-        d_pre = (d_act * (sig + GELU * pre * sig * (1.0 - sig))).astype(BF16)
-        d_pres.append(d_pre)
-        d_twos.append(dg(d_pre, fc1_full, ((1,), (1,))))
-
-    def reduce_slots(parts):
-        own, other = parts
-        other = other[:local] + net.core(other[local:].astype(BF16)).astype(F32)
-        from_peer = net.across(other.astype(BF16)).astype(F32)
-        own = own[:local] + net.core(own[local:].astype(BF16)).astype(F32)
-        return own + from_peer
-
-    d_two = reduce_slots(d_twos)
-    mlp_out = reduce_slots([dg(a, fc2_full, ((1,), (1,))) for a in acts])
-    out_own = (hidden + mlp_out + fc2_bias).astype(BF16)
+    attn_part = dg(mixed, proj_full, ((0,), (1,)), BF16).reshape(2, local, width)
+    d_attn, d_hidden, base, mlp_other, grad_fc1_part, grad_fc2_part, sums_two = feed(
+        net.lines, attn_part, tok, proj_bias, mlp_norm_gain, mlp_norm_bias, bias_fc1, fc2_bias,
+        fc1_full, fc2_full, grad_out, grad_out_sib,
+    )
+    out_own = (base + net.across(mlp_other).astype(F32)).astype(BF16)
     block_output = both(out_own, net.across(out_own), y)
-
-    def weight_sum(lefts, rights):
-        total = sum(dg(l, r, ((0,), (0,))) for l, r in zip(lefts, rights))
-        return total.astype(BF16).reshape(net.lines, 2, rows, quarter)
-
-    def all_hidden(block):
-        return both(block, net.core(block), c)
-
-    grad_fc2 = all_hidden(net.scatter(weight_sum(dy, acts)))
-    grad_fc1 = all_hidden(net.scatter(weight_sum(two, d_pres)))
-    grad_fc1 = jnp.moveaxis(grad_fc1, 0, 1).reshape(rows, 2 * quarter)
-    grad_fc2 = jnp.moveaxis(grad_fc2, 1, 2).reshape(2 * quarter, rows)
-
-    d_hidden = dy_own.astype(F32) + norm_back(d_two, normal_two, inverse_two, mlp_norm_gain)
-    d_attn_own = d_hidden.astype(BF16)
-    d_attn = both(d_attn_own, net.core(d_attn_own), c).reshape(full, width)
+    d_attn = d_attn.reshape(full, width)
     grad_proj_part = dg(d_attn, mixed, ((0,), (1,)), BF16)
     d_mixed = dg(proj_full, d_attn, ((0,), (1,)), BF16)
     d_proj = attend_back(low, d_mixed, mixed_f, lse, cosine, sine, ids)
@@ -615,35 +1106,38 @@
     d_one = pick(d_one_part, c) + net.core(pick(d_one_part, 1 - c))
     grad_in = d_hidden + norm_back(d_one, normal_one, inverse_one, attn_norm_gain)
     grad_in = grad_in.astype(BF16)
-    input_grad = both(grad_in, net.across(grad_in), y).astype(F32)
-
-    proj_plane = net.scatter(grad_proj_part.reshape(net.lines, 2, rows, inner))
-    proj_sum = proj_plane + net.across(proj_plane.astype(BF16), off_diag).astype(F32)
-    qkv_pair = grad_qkv_part.astype(F32) + net.across(grad_qkv_part, off_diag).astype(F32)
-    qkv_pair = jnp.moveaxis(qkv_pair.astype(BF16).reshape(3, net.lines, 2, rows, inner), 0, 2)
-    qkv_sum = net.scatter(qkv_pair, on_diag)
-    attn_sum = jnp.concatenate([qkv_sum, proj_sum[None]])
-    attn_sum = mine_or(attn_sum, net.send(attn_sum, lambda s, c, y: (s, 1 - c, y), on_diag))
-    grad_qkv, grad_proj = attn_sum[:3], attn_sum[3].T
 
     sums = lambda t: jnp.sum(t.astype(F32), axis=0)
     qkv_shift = jnp.sum(d_proj.astype(F32), axis=2)
-    fc1_shift = sum(sums(d) for d in d_pres)
+    fc1_shift = sums_two[4]
     zero_qkv, zero_fc1 = jnp.zeros_like(qkv_shift), jnp.zeros_like(fc1_shift)
     small = jnp.concatenate(
         [
             sums(d_one * normal_one),
             sums(d_one),
-            sums(d_attn_own),
-            sums(d_two * normal_two),
-            sums(d_two),
-            sums(dy_own),
+            sums_two[0],
+            sums_two[1],
+            sums_two[2],
+            sums_two[3],
             jnp.where(c == 0, qkv_shift, zero_qkv).reshape(-1),
             jnp.where(c == 1, qkv_shift, zero_qkv).reshape(-1),
         ]
         + [jnp.where((y == i) & (c == j), fc1_shift, zero_fc1) for i in range(2) for j in range(2)]
     )
-    small = lax.psum(small, AXES)
+    blocks = (net.lines, 2, rows, inner)
+    attn_parts = jnp.concatenate(
+        [grad_qkv_part.reshape((3,) + blocks), grad_proj_part.reshape((1,) + blocks)]
+    )
+    fc_parts = jnp.stack([grad_fc1_part, grad_fc2_part]).reshape(2, net.lines, 2, rows, quarter)
+    attn_sum, fc_sum, grad_in_peer, small = settle(
+        net.lines, attn_parts, fc_parts, grad_in, small.reshape(-1, width)
+    )
+    small = small.reshape(-1)
+    input_grad = both(grad_in, grad_in_peer, y).astype(F32)
+    grad_qkv, grad_proj = attn_sum[:3], attn_sum[3].T
+    grad_fc1 = jnp.moveaxis(fc_sum[:, 0], 0, 1).reshape(rows, 2 * quarter)
+    grad_fc2 = jnp.moveaxis(fc_sum[:, 1], 1, 2).reshape(2 * quarter, rows)
+
     vec = lambda i: small[i * width : (i + 1) * width]
     at = 6 * width
     qkv_shifts = small[at : at + 6 * inner].reshape(2, 3, inner)

time: 722 us -> 601 us (0.83)
  Pallas kernels: 130 us -> 404 us
  waiting for transfers between devices: 267 us -> 61 us
  matrix products: 118 us -> 40.3 us
  starting transfers between devices: 56.5 us -> 15.3 us
  local copies, waits for them, and re-layouts: 66.4 us -> 41.1 us
  other arithmetic: 57.6 us -> 33.4 us
  between operations: 15.7 us -> 1.52 us
    pallas_call x0 -> x2, Pallas kernels: none -> 283 us  [the longest x1 181 us: settle(): pl.pallas_call(functools.partial(settle_kernel, lines, pieces, fc_cols),...]
    psum x1 -> x0, waiting for transfers between devices: 119 us -> none  [per_device(): small = lax.psum(small, AXES)]
    ppermute x42 -> x10, waiting for transfers between devices: 148 us -> 61 us  [send(): return lax.ppermute(value, AXES, pairs)]
    dot_general x15 -> x3, matrix products: 91.8 us -> 13.8 us  [dg(): lax.dot_general(left, right, (dims, ((), ())), preferred_element_type=F32)]
    ppermute x42 -> x10, starting transfers between devices: 56.4 us -> 15.3 us  [send(): return lax.ppermute(value, AXES, pairs)]
    convert_element_type x10 -> x2, other arithmetic: 21.1 us -> 6.52 us  [the longest x1 4.74 us: per_device(): input_grad = both(grad_in, grad_in_peer, y).astype(F32)]
    squeeze x5 -> x2, local copies, waits for them, and re-layouts: 12 us -> 2.42 us  [per_device(): pick = lambda t, i, d=0: lax.dynamic_index_in_dim(t, i, d, False)]
    pallas_call x1, Pallas kernels: 76.9 us -> 67.8 us  [collect(): pl.pallas_call(functools.partial(collect_kernel, lines, pieces), in_specs...]
  transfers between devices with their start and end apart: 43 -> 10, of which waited for: 14 -> 4; matrix products, arithmetic and copies ran while one was open for 31% -> 12% of each run, Pallas kernels for 7% -> 35%
where the time goes in v3:
time: 601 us; the launch traced here: 596 us
  Pallas kernels  404 us (67%)
  waiting for transfers between devices  61 us (10%)
  local copies, waits for them, and re-layouts  41.1 us (7%)
  matrix products  40.3 us (7%)
  other arithmetic  33.4 us (6%)
  starting transfers between devices  15.3 us (3%)
    pallas_call x1, Pallas kernels, settle(): pl.pallas_call(functools.partial(settle_kernel, lines, pieces, fc_cols),...  181 us
    pallas_call x1, Pallas kernels, feed(): pl.pallas_call(functools.partial(feed_kernel, lines), in_specs=[vmem] * 7...  102 us
    pallas_call x1, Pallas kernels, collect(): pl.pallas_call(functools.partial(collect_kernel, lines, pieces), in_specs...  67.8 us
    ppermute x10, waiting for transfers between devices, send(): return lax.ppermute(value, AXES, pairs)  61 us
    pallas_call x1, Pallas kernels, attend(): pl.pallas_call(attend_kernel, grid=(heads,), in_specs=[pl.BlockSpec((3, H...  27.1 us
    pallas_call x1, Pallas kernels, attend_back(): pl.pallas_call(attend_back_kernel, grid=(heads,), in_specs=[pl.BlockSpec(...  26 us
    ppermute x10, starting transfers between devices, send(): return lax.ppermute(value, AXES, pairs)  15.3 us
    dot_general x3, matrix products, dg(): lax.dot_general(left, right, (dims, ((), ())), preferred_element_type=F32)  13.8 us
  transfers between devices with their start and end apart: 10, of which 4 were waited for; matrix products, arithmetic and copies ran while one was open for 12% of the time, Pallas kernels for 35%

profile of v3, /device:TPU:0, one launch (start us, length us, event | category | flops | bytes accessed | tf_op | source)
XLA Modules:
  0.0 596.5 jit_solution(6166481721692224965)
XLA Ops:
  9.4 67.8 %collect.1 = (bf16[4,8,160,640]{3,2,1,0:T(8,128)(2,1)S(1)}, bf16[2,512,1280]{2,1,0:T(8,128)(2,1)S(1)}, bf16[2,512,1280]{2,1,0:T(8,128)(2,1)S(1)}, f32[3,640]{1,0:T(4,128)S(1)}) custom-call(bf16[4,160,640]{2,1,0:T(8,128)(2,1)S(1)} %pad_maximum_fusion.2.block, bf16[512,1280]{1,0:T(8,128)(2,1)S(1)} %get-tuple-element.74.tok, ...), custom_call_target="tpu_custom_call" | custom-call | tf_op jit(solution)/shard_map/collect/pallas_call | solution.py:387
  80.2 1.9 collective-permute-start
  82.1 2.1 collective-permute-start.1
  84.2 2.4 collective-permute-start.5
  86.6 2.8 slice.97
  91.6 11.1 %broadcast_add_fusion.x_ref = f32[3,640,1024]{2,1,0:T(8,128)} fusion(f32[3,640]{1,0:T(4,128)S(1)} %get-tuple-element.36, bf16[3,1280,640]{2,1,0:T(8,128)(2,1)} %bitcast.128, bf16[1024,1280,1]{1,0,2:T(8,128)(2,1)} %bitcast.117), kind=kOutput, calls=%fused_computation.7 | convolution fusion | flops 5035130880 | bytes 15408640 | tf_op jit(solution)/shard_map/cde,rd->cer/dot_general | solution.py:1088
  102.7 27.1 %attend.1 = (bf16[3,640,1024]{2,1,0:T(8,128)(2,1)}, bf16[640,1024]{1,0:T(8,128)(2,1)S(1)}, f32[640,1024]{1,0:T(8,128)S(1)}, f32[8,1,1024]{2,1,0:T(1,128)S(1)}) custom-call(f32[3,640,1024]{2,1,0:T(8,128)} %broadcast_add_fusion.x_ref, f32[40,1024]{1,0:T(8,128)S(1)} %get-tuple-element.80.cos_ref, f32[40,1024]{1,0:T(8,128)S(1)} %get-tuple-element.79.sin_ref, ...), custom_call_target="tpu_custom_call" | custom-call | flops 2684354560 | bytes 17039360 | tf_op jit(solution)/shard_map/attend/pallas_call | solution.py:78
  129.9 3.7 convolution_convert_fusion.1
  138.1 2.1 collective-permute-start.2
  140.3 1.9 collective-permute-start.6
  144.7 14.8 %collective-permute-done.2 = bf16[2,160,1280]{2,1,0:T(8,128)(2,1)S(1)} collective-permute-done((bf16[2,160,1280]{2,1,0:T(8,128)(2,1)}, bf16[2,160,1280]{2,1,0:T(8,128)(2,1)S(1)}, u32[]{:S(2)}, u32[]{:S(2)}) %collective-permute-start.2) | collective-permute-done | bytes 819232 | tf_op jit(solution)/shard_map/ppermute | solution.py:980
  160.8 16.3 %collective-permute-done.4 = bf16[2,160,1280]{2,1,0:T(8,128)(2,1)S(1)} collective-permute-done((bf16[2,160,1280]{2,1,0:T(8,128)(2,1)}, bf16[2,160,1280]{2,1,0:T(8,128)(2,1)S(1)}, u32[]{:S(2)}, u32[]{:S(2)}) %collective-permute-start.4) | collective-permute-done | bytes 819232 | tf_op jit(solution)/shard_map/ppermute | solution.py:980
  178.3 15.4 %collective-permute-done.6 = bf16[2,160,1280]{2,1,0:T(8,128)(2,1)S(1)} collective-permute-done((bf16[2,160,1280]{2,1,0:T(8,128)(2,1)}, bf16[2,160,1280]{2,1,0:T(8,128)(2,1)S(1)}, u32[]{:S(2)}, u32[]{:S(2)}) %collective-permute-start.6) | collective-permute-done | bytes 819232 | tf_op jit(solution)/shard_map/ppermute | solution.py:980
  193.8 3.1 fusion.25
  196.9 101.7 %feed.1 = (bf16[2,512,1280]{2,1,0:T(8,128)(2,1)}, f32[512,1280]{1,0:T(8,128)}, f32[512,1280]{1,0:T(8,128)}, bf16[512,1280]{1,0:T(8,128)(2,1)}, bf16[1280,1280]{1...) custom-call(bf16[2,512,1280]{2,1,0:T(8,128)(2,1)} %bitcast.135, bf16[512,1280]{1,0:T(8,128)(2,1)} %copy-done.2, ...), custom_call_target="tpu_custom_call" | custom-call | tf_op jit(solution)/shard_map/feed/pallas_call | solution.py:902
  298.6 4.7 convolution_convert_fusion.3.grad_ref
  303.4 26.0 %attend_back.1 = bf16[3,640,1024]{2,1,0:T(8,128)(2,1)} custom-call(bf16[3,640,1024]{2,1,0:T(8,128)(2,1)} %get-tuple-element.43.low_ref, bf16[640,1024]{1,0:T(8,128)(2,1)S(1)} %convolution_convert_fusion.3.grad_ref, f32[640,1024]{1,0:T(8,128)S(1)} %copy-done.10, f32[8,1,1024]{2,1,0:T(1,128)S(1)} %get-tuple-element.46.lse_ref, ...), custom_call_target="tpu_custom_call" | custom-call | flops 6710886400 | bytes 11796480 | tf_op jit(solution)/shard_map/attend_back/pallas_call | solution.py:151
  329.4 9.7 %convolution_convert_fusion = bf16[1280,3,640]{2,0,1:T(8,128)(2,1)} fusion(bf16[1024,1280,1]{1,0,2:T(8,128)(2,1)S(1)} %bitcast.118, bf16[3,640,1024]{2,1,0:T(8,128)(2,1)} %attend_back.1), kind=kOutput, calls=%fused_computation.3 | convolution fusion | flops 5035622400 | bytes 11468800 | tf_op jit(solution)/shard_map/cer,rd->cde/dot_general | solution.py:1103
  339.1 5.7 convolution_bitcast_fusion
  344.8 1.8 dynamic-slice_bitcast_fusion
  349.0 2.7 collective-permute-start.7
  351.8 5.3 convolution_convert_fusion.2
  357.1 5.6 pad_maximum_fusion.attn
  362.7 3.8 pad_maximum_fusion.1.fc
  366.5 14.5 %collective-permute-done.7 = bf16[512,1280]{1,0:T(8,128)(2,1)} collective-permute-done((bf16[512,1280]{1,0:T(8,128)(2,1)}, bf16[512,1280]{1,0:T(8,128)(2,1)}, u32[]{:S(2)}, u32[]{:S(2)}) %collective-permute-start.7) | collective-permute-done | bytes 1310752 | tf_op jit(solution)/shard_map/ppermute | solution.py:980
  382.8 1.8 collective-permute-start.8
  384.7 4.2 fusion.12
  389.7 4.7 fusion.11.grad_in
  394.4 181.3 %settle.1 = (f32[4,160,640]{2,1,0:T(8,128)}, f32[2,2,160,1280]{3,2,1,0:T(8,128)}, bf16[512,1280]{1,0:T(8,128)(2,1)}, f32[13,1280]{1,0:T(8,128)}) custom-call(bf16[4,4,2,160,640]{4,3,2,1,0:T(8,128)(2,1)} %pad_maximum_fusion.attn, bf16[2,4,2,160,1280]{4,3,2,1,0:T(8,128)(2,1)} %pad_maximum_fusion.1.fc, bf16[512,1280]{1,0:T(8,128)(2,1)} %fusion.11.grad_in, ...), custom_call_target="tpu_custom_call" | custom-call | tf_op jit(solution)/shard_map/settle/pallas_call | solution.py:657
  577.3 2.2 slice_bitcast_fusion
  588.1 4.7 fusion.14
  592.9 3.4 maximum_select_fusion
  (149 shorter events, 38.6 us)
Async XLA Ops:
  1.8 4.2 copy-start.21
  6.0 127.7 %copy-start.2 = (bf16[512,1280]{1,0:T(8,128)(2,1)}, bf16[512,1280]{1,0:T(8,128)(2,1)S(1)}, u32[]{:S(2)}) copy-start(bf16[512,1280]{1,0:T(8,128)(2,1)S(1)} %get-tuple-element.74.tok) | copy-start | bytes 3932164
  80.2 62.1 %collective-permute-start = (bf16[2,160,1280]{2,1,0:T(8,128)(2,1)S(1)}, bf16[2,160,1280]{2,1,0:T(8,128)(2,1)}, u32[]{:S(2)}, u32[]{:S(2)}) collective-permute-start(bf16[2,160,1280]{2,1,0:T(8,128)(2,1)S(1)} %pad_maximum_fusion.3), channel_id=1, source_target_pairs={{0,4},{1,5},{2,6},{3,7},{4,0},{5,1},{6,2},{7,3},{8,12},{9,13},{10,... | collective-permute-start | bytes 2457608 | tf_op jit(solution)/shard_map/ppermute | solution.py:980
  82.1 56.1 %collective-permute-start.1 = (bf16[2,160,1280]{2,1,0:T(8,128)(2,1)S(1)}, bf16[2,160,1280]{2,1,0:T(8,128)(2,1)}, u32[]{:S(2)}, u32[]{:S(2)}) collective-permute-start(bf16[2,160,1280]{2,1,0:T(8,128)(2,1)S(1)} %pad_maximum_fusion.3), channel_id=1, source_target_pairs={{0,8},{1,9},{2,10},{3,11},{4,12},{5,13},{6,14},{7,15},{8,16},{9,17... | collective-permute-start | bytes 2457608 | tf_op jit(solution)/shard_map/ppermute | solution.py:980
  84.2 56.0 %collective-permute-start.3 = (bf16[2,160,1280]{2,1,0:T(8,128)(2,1)S(1)}, bf16[2,160,1280]{2,1,0:T(8,128)(2,1)}, u32[]{:S(2)}, u32[]{:S(2)}) collective-permute-start(bf16[2,160,1280]{2,1,0:T(8,128)(2,1)S(1)} %pad_maximum_fusion.3), channel_id=1, source_target_pairs={{0,16},{1,17},{2,18},{3,19},{4,20},{5,21},{6,22},{7,23},{8,24},{9,... | collective-permute-start | bytes 2457608 | tf_op jit(solution)/shard_map/ppermute | solution.py:980
  84.2 56.1 %collective-permute-start.5 = (bf16[2,160,1280]{2,1,0:T(8,128)(2,1)S(1)}, bf16[2,160,1280]{2,1,0:T(8,128)(2,1)}, u32[]{:S(2)}, u32[]{:S(2)}) collective-permute-start(bf16[2,160,1280]{2,1,0:T(8,128)(2,1)S(1)} %pad_maximum_fusion.3), channel_id=1, source_target_pairs={{0,24},{1,25},{2,26},{3,27},{4,28},{5,29},{6,30},{7,31},{8,0},{9,1... | collective-permute-start | bytes 2457608 | tf_op jit(solution)/shard_map/ppermute | solution.py:980
  102.7 27.2 %copy-start.19 = (bf16[1,8,160,640]{3,2,1,0:T(8,128)(2,1)S(1)}, bf16[1,8,160,640]{3,2,1,0:T(8,128)(2,1)}, u32[]{:S(2)}) copy-start(bf16[1,8,160,640]{3,2,1,0:T(8,128)(2,1)} %slice.102) | copy-start | bytes 4915204
  129.9 4.4 copy-start.30
  129.9 5.1 copy-start.25
  129.9 5.7 copy-start.26
  129.9 6.3 %copy-start.27 = (f32[1280]{0:T(1024)S(1)}, f32[1280]{0:T(1024)}, u32[]{:S(2)}) copy-start(f32[1280]{0:T(1024)} %param.24) | copy-start | bytes 15364
  129.9 6.9 %copy-start.28 = (f32[1280]{0:T(1024)S(1)}, f32[1280]{0:T(1024)}, u32[]{:S(2)}) copy-start(f32[1280]{0:T(1024)} %param.28) | copy-start | bytes 15364
  138.1 21.4 %collective-permute-start.2 = (bf16[2,160,1280]{2,1,0:T(8,128)(2,1)}, bf16[2,160,1280]{2,1,0:T(8,128)(2,1)S(1)}, u32[]{:S(2)}, u32[]{:S(2)}) collective-permute-start(bf16[2,160,1280]{2,1,0:T(8,128)(2,1)} %collective-permute-done.1), channel_id=1, source_target_pairs={{0,4},{1,5},{2,6},{3,7},{4,0},{5,1},{6,2},{7,3},{8,12},{9,13},{10,... | collective-permute-start | bytes 2457608 | tf_op jit(solution)/shard_map/ppermute | solution.py:980
  140.2 36.8 %collective-permute-start.4 = (bf16[2,160,1280]{2,1,0:T(8,128)(2,1)}, bf16[2,160,1280]{2,1,0:T(8,128)(2,1)S(1)}, u32[]{:S(2)}, u32[]{:S(2)}) collective-permute-start(bf16[2,160,1280]{2,1,0:T(8,128)(2,1)} %collective-permute-done.3), channel_id=1, source_target_pairs={{0,4},{1,5},{2,6},{3,7},{4,0},{5,1},{6,2},{7,3},{8,12},{9,13},{10,... | collective-permute-start | bytes 2457608 | tf_op jit(solution)/shard_map/ppermute | solution.py:980
  140.3 53.4 %collective-permute-start.6 = (bf16[2,160,1280]{2,1,0:T(8,128)(2,1)}, bf16[2,160,1280]{2,1,0:T(8,128)(2,1)S(1)}, u32[]{:S(2)}, u32[]{:S(2)}) collective-permute-start(bf16[2,160,1280]{2,1,0:T(8,128)(2,1)} %collective-permute-done.5), channel_id=1, source_target_pairs={{0,4},{1,5},{2,6},{3,7},{4,0},{5,1},{6,2},{7,3},{8,12},{9,13},{10,... | collective-permute-start | bytes 2457608 | tf_op jit(solution)/shard_map/ppermute | solution.py:980
  298.6 4.7 copy-start.10
  303.4 26.1 %copy-start.8 = (bf16[2,512,1280]{2,1,0:T(8,128)(2,1)S(1)}, bf16[2,512,1280]{2,1,0:T(8,128)(2,1)}, u32[]{:S(2)}) copy-start(bf16[2,512,1280]{2,1,0:T(8,128)(2,1)} %copy-done.7) | copy-start | bytes 7864324
  303.4 35.7 %slice-start.4 = ((s8[4915200]{0:T(1024)(128)(4,1)}), s8[4194304]{0:T(1024)(128)(4,1)S(1)}, s32[]{:S(2)}) async-start(s8[4915200]{0:T(1024)(128)(4,1)} %bitcast.129), calls=%async_computation.4 | async-start | bytes 8388608
  329.4 9.7 %slice-start.5 = ((s8[4915200]{0:T(1024)(128)(4,1)}), s8[720896]{0:T(1024)(128)(4,1)S(1)}, s32[]{:S(2)}) async-start(s8[4915200]{0:T(1024)(128)(4,1)} %bitcast.129), calls=%async_computation.5 | async-start | bytes 1441792
  329.4 9.7 %copy-start.15 = (bf16[3,640,1024]{2,1,0:T(8,128)(2,1)S(1)}, bf16[3,640,1024]{2,1,0:T(8,128)(2,1)}, u32[]{:S(2)}) copy-start(bf16[3,640,1024]{2,1,0:T(8,128)(2,1)} %attend_back.1) | copy-start | bytes 11796484
  348.0 36.7 %collective-permute-start.9 = (f32[512,1280]{1,0:T(8,128)}, f32[512,1280]{1,0:T(8,128)}, u32[]{:S(2)}, u32[]{:S(2)}) collective-permute-start(f32[512,1280]{1,0:T(8,128)} %dynamic-slice_bitcast_fusion), channel_id=1, source_target_pairs={{0,2},{1,3},{2,0},{3,1},{4,6},{5,7},{6,4},{7,5},{8,10},{9,11},{10,... | collective-permute-start | bytes 7864328 | tf_op jit(solution)/shard_map/ppermute | solution.py:980
  349.0 32.1 %collective-permute-start.7 = (bf16[512,1280]{1,0:T(8,128)(2,1)}, bf16[512,1280]{1,0:T(8,128)(2,1)}, u32[]{:S(2)}, u32[]{:S(2)}) collective-permute-start(bf16[512,1280]{1,0:T(8,128)(2,1)} %get-tuple-element.41), channel_id=1, source_target_pairs={{0,1},{1,0},{2,3},{3,2},{4,5},{5,4},{6,7},{7,6},{8,9},{9,8},{10,11... | collective-permute-start | bytes 3932168 | tf_op jit(solution)/shard_map/ppermute | solution.py:980
  351.6 5.5 slice-start.2
  351.7 5.3 slice-start.3
  357.1 5.6 copy-start.16
  357.1 5.6 copy-start.17
  357.1 27.5 %slice-start = ((s8[5242880]{0:T(1024)(128)(4,1)}), s8[4194304]{0:T(1024)(128)(4,1)S(1)}, s32[]{:S(2)}) async-start(s8[5242880]{0:T(1024)(128)(4,1)} %bitcast.122), calls=%async_computation | async-start | bytes 8388608
  362.7 18.3 %copy-start.18 = (f32[512,1280]{1,0:T(8,128)S(1)}, f32[512,1280]{1,0:T(8,128)}, u32[]{:S(2)}) copy-start(f32[512,1280]{1,0:T(8,128)} %get-tuple-element.40) | copy-start | bytes 7864324
  362.7 21.9 %slice-start.1 = ((s8[5242880]{0:T(1024)(128)(4,1)}), s8[1048576]{0:T(1024)(128)(4,1)S(1)}, s32[]{:S(2)}) async-start(s8[5242880]{0:T(1024)(128)(4,1)} %bitcast.122), calls=%async_computation.1 | async-start | bytes 2097152
  382.8 6.1 %copy-start.23 = (f32[16640]{0:T(1024)S(1)}, f32[16640]{0:T(1024)}, u32[]{:S(2)}) copy-start(f32[16640]{0:T(1024)} %custom-call) | copy-start | bytes 199684
  382.8 210.0 %collective-permute-start.8 = (bf16[512,1280]{1,0:T(8,128)(2,1)S(1)}, bf16[512,1280]{1,0:T(8,128)(2,1)}, u32[]{:S(2)}, u32[]{:S(2)}) collective-permute-start(bf16[512,1280]{1,0:T(8,128)(2,1)S(1)} %add_convert_fusion), channel_id=1, source_target_pairs={{0,1},{1,0},{2,3},{3,2},{4,5},{5,4},{6,7},{7,6},{8,9},{9,8},{10,11... | collective-permute-start | bytes 3932168 | tf_op jit(solution)/shard_map/ppermute | solution.py:980
  580.8 7.3 %copy-start.13 = (bf16[512,1280]{1,0:T(8,128)(2,1)S(1)}, bf16[512,1280]{1,0:T(8,128)(2,1)}, u32[]{:S(2)}) copy-start(bf16[512,1280]{1,0:T(8,128)(2,1)} %fusion.11.grad_in) | copy-start | bytes 3932164
  (15 other events, 42.1 us)

commit v4 on v3

v4 whole, which is shorter than its diff:
```python
import functools
import math

import jax
import jax.numpy as jnp
from jax import lax
from jax.experimental import pallas as pl
from jax.experimental.pallas import tpu as pltpu
from jax.sharding import PartitionSpec as P

HDIM = 80
NORM_EPS = 1e-06
GELU = 1.702
ROPE_BASE = 10000.0
SCALE = 1.0 / math.sqrt(HDIM)
LOG2E = 1.0 / math.log(2.0)
NEG = -1e30
F32 = jnp.float32
BF16 = jnp.bfloat16
AXES = ("shard", "ctx", "tp")
QB = 256
AHEAD = 2
FIRST = 3
SLICE = 384
TILE = 256


def dg(left, right, dims, out=F32):
    return lax.dot_general(left, right, (dims, ((), ())), preferred_element_type=F32).astype(out)


def rope_rows(t, cosine, sine):
    half = t.shape[0] // 2
    first, second = t[:half], t[half:]
    return jnp.concatenate([first * cosine - second * sine, second * cosine + first * sine], axis=0)


def rope_rows_back(t, cosine, sine):
    half = t.shape[0] // 2
    first, second = t[:half], t[half:]
    return jnp.concatenate([first * cosine + second * sine, second * cosine - first * sine], axis=0)


def fill_bias(bias, idc_ref, idr_ref):
    @pl.when(pl.program_id(0) == 0)
    def _():
        bias[...] = jnp.where(idc_ref[...] == idr_ref[...], 0.0, NEG)


def at_step(h, action):
    pl.when(pl.program_id(0) == h)(action)


def spread(ticks, heads):
    plan = [[] for _ in range(heads)]
    for i, tick in enumerate(ticks):
        plan[min(i, heads - 1)].append(tick)
    return plan


def run_ticks(plan):
    for h, ticks in enumerate(plan):
        if ticks:
            at_step(h, lambda ticks=ticks: [tick() for tick in ticks] and None)


def attend_kernel(
    lines, heads, weights, normed, shift, cos_ref, sin_ref, idc_ref, idr_ref, w_own,
    low_ref, mixed_ref, outf_ref, lse_ref, part_ref, w_full,
    bias, proj_in, wv, rows_in, loads, own_sem, zs, zr, xs, xr,
):
    at = Place(lines)
    h = pl.program_id(0)
    gather = Gather(at, w_own, w_full, columns_of(w_own.shape[1]), own_sem, zs, zr, xs, xr)
    local = rows_in.shape[0] // 2
    copies = [
        pltpu.make_async_copy(weights, wv, loads.at[0]),
        pltpu.make_async_copy(normed.at[0], rows_in.at[pl.ds(0, local)], loads.at[1]),
        pltpu.make_async_copy(normed.at[1], rows_in.at[pl.ds(local, local)], loads.at[2]),
    ]

    @pl.when(h == 0)
    def _():
        for copy in copies:
            copy.start()
        at.greet()
        gather.start()
        for copy in copies:
            copy.wait()
        columns = shift[...].T
        for j in range(3):
            proj_in[j] = dg(wv[j], rows_in[...], ((0,), (1,))) + columns[:, j : j + 1]

    fill_bias(bias, idc_ref, idr_ref)
    cosine, sine = cos_ref[...], sin_ref[...]
    mine = pl.ds(pl.multiple_of(h * HDIM, HDIM), HDIM)
    query = rope_rows(proj_in[0, mine], cosine, sine).astype(BF16)
    key_f = rope_rows(proj_in[1, mine], cosine, sine)
    value = proj_in[2, mine].astype(BF16)
    low_ref[0] = query
    low_ref[1] = key_f.astype(BF16)
    low_ref[2] = value
    key_nat = key_f.T.astype(BF16)
    length = query.shape[1]
    factor = SCALE * LOG2E
    for start in range(0, length, QB):
        cols = slice(start, start + QB)
        logits = dg(key_nat, query[:, cols], ((1,), (0,))) + bias[:, cols]
        peak = jnp.max(logits, axis=0, keepdims=True)
        probs = jnp.exp2((logits - peak) * factor)
        total = jnp.sum(probs, axis=0, keepdims=True)
        mixed = dg(value, probs.astype(BF16), ((1,), (0,))) * (1.0 / total)
        mixed_ref[mine, cols] = mixed.astype(BF16)
        outf_ref[:, cols] = mixed
        lse_ref[0, :, cols] = peak * factor + jnp.log2(total)

    @pl.when(h == heads - 1)
    def _():
        def body(i, carry):
            r = pl.ds(pl.multiple_of(i * QB, QB), QB)
            part_ref[r] = dg(mixed_ref[:, r], wv[3], ((0,), (1,)), BF16)
            return carry

        lax.fori_loop(0, length // QB, body, 0)

    ticks = [functools.partial(gather.tick, i) for i in range(len(gather.pieces) + 1)]
    run_ticks(spread(ticks + [gather.drain], heads))


def attend(lines, weights, normed, shift, cosine, sine, ids, w_own):
    _, width, inner = weights.shape
    length = ids.shape[0]
    heads = inner // HDIM
    half = HDIM // 2
    head = lambda h: (0, h, 0)
    whole = lambda h: (0, 0)
    rows, quarter = w_own.shape
    anywhere = pl.BlockSpec(memory_space=pl.ANY)
    return pl.pallas_call(
        functools.partial(attend_kernel, lines, heads),
        grid=(heads,),
        in_specs=[
            anywhere,
            anywhere,
            pl.BlockSpec((8, inner), whole),
            pl.BlockSpec((half, length), whole),
            pl.BlockSpec((half, length), whole),
            pl.BlockSpec((length, 1), whole),
            pl.BlockSpec((1, length), whole),
            anywhere,
        ],
        out_specs=[
            pl.BlockSpec((3, HDIM, length), head),
            pl.BlockSpec((inner, length), whole),
            pl.BlockSpec((HDIM, length), lambda h: (h, 0)),
            pl.BlockSpec((1, 1, length), lambda h: (h, 0, 0)),
            pl.BlockSpec((length, width), whole),
            anywhere,
        ],
        out_shape=[
            jax.ShapeDtypeStruct((3, inner, length), BF16),
            jax.ShapeDtypeStruct((inner, length), BF16),
            jax.ShapeDtypeStruct((inner, length), F32),
            jax.ShapeDtypeStruct((heads, 1, length), F32),
            jax.ShapeDtypeStruct((length, width), BF16),
            jax.ShapeDtypeStruct((2 * lines * rows, quarter), BF16),
        ],
        scratch_shapes=[
            pltpu.VMEM((length, length), F32),
            pltpu.VMEM((3, inner, length), F32),
            pltpu.VMEM(weights.shape, BF16),
            pltpu.VMEM((length, width), BF16),
            pltpu.SemaphoreType.DMA((3,)),
        ]
        + gather_scratch(lines, quarter),
        compiler_params=pltpu.CompilerParams(
            collective_id=3, has_side_effects=True, vmem_limit_bytes=60 << 20
        ),
        cost_estimate=pl.CostEstimate(
            flops=4 * inner * length * length + 8 * inner * length * width,
            transcendentals=heads * length * length,
            bytes_accessed=26 * inner * length,
        ),
        name="attend",
    )(weights, normed, shift, cosine, sine, ids[:, None], ids[None, :], w_own)


def attend_back_kernel(
    lines, heads, low_ref, outf_ref, lse_ref, cos_ref, sin_ref, idc_ref, idr_ref,
    weights, normed, mixed, d_attn, w_grad, other, base,
    one_ref, qkv_grad, proj_grad, shift_ref, w_out, out_own, out_peer,
    bias, dq, dk, dv, d_mixed, d_proj, wv, rows_in, mixed_in, base_in, other_in, tile_buf, w_sum,
    loads, ys, yr, ts, *share_refs
):
    at = Place(lines)
    h = pl.program_id(0)
    share = Share(at, w_grad, w_sum, columns_of(w_grad.shape[1]), *share_refs)
    length, width = rows_in.shape
    local = length // 2

    def load_rows(source):
        return [
            pltpu.make_async_copy(source.at[i], rows_in.at[pl.ds(i * local, local)], loads.at[i])
            for i in range(2)
        ]

    mixed_copy = pltpu.make_async_copy(mixed, mixed_in, loads.at[2])
    weight_copy = pltpu.make_async_copy(weights, wv, loads.at[3])
    base_copy = pltpu.make_async_copy(base, base_in, loads.at[4])
    other_copy = remote(other, other_in, ys.at[0], yr.at[0], at.peer)
    out_copy = remote(out_own, out_peer, ys.at[1], yr.at[1], at.peer)

    @pl.when(h == 0)
    def _():
        for copy in load_rows(d_attn) + [mixed_copy, weight_copy, base_copy]:
            copy.start()
        at.greet()
        share.flow.start()
        other_copy.start()
        for copy in load_rows(d_attn) + [mixed_copy, weight_copy]:
            copy.wait()
        d_mixed[...] = dg(wv[3], rows_in[...], ((0,), (1,)), BF16)

        def body(i, carry):
            cols = pl.ds(pl.multiple_of(i * QB, QB), QB)
            proj_grad[cols] = dg(rows_in[:, cols], mixed_in[...], ((0,), (1,)), BF16)
            return carry

        lax.fori_loop(0, width // QB, body, 0)
        for copy in load_rows(normed):
            copy.start()

    fill_bias(bias, idc_ref, idr_ref)
    cosine, sine = cos_ref[...], sin_ref[...]
    mine = pl.ds(pl.multiple_of(h * HDIM, HDIM), HDIM)
    query, key = low_ref[0], low_ref[1]
    grad = d_mixed[mine]
    grad_f = grad.astype(F32)
    delta = jnp.sum(grad_f * outf_ref[...], axis=0, keepdims=True)
    nat = lambda t: t.astype(F32).T.astype(BF16)
    query_nat, key_nat, value_nat, grad_nat = nat(query), nat(key), nat(low_ref[2]), nat(grad)
    lse = lse_ref[0]
    factor = SCALE * LOG2E
    for start in range(0, length, QB):
        cols = slice(start, start + QB)
        logits = dg(key_nat, query[:, cols], ((1,), (0,)))
        probs = jnp.exp2(logits * factor + bias[:, cols] - lse[:, cols])
        d_probs = dg(value_nat, grad[:, cols], ((1,), (0,)))
        d_logits = (probs * (d_probs - delta[:, cols])).astype(BF16)
        part_v = dg(probs.astype(BF16), grad_nat[cols], ((1,), (0,)))
        part_k = dg(d_logits, query_nat[cols], ((1,), (0,)))
        dq[:, cols] = dg(key, d_logits, ((1,), (0,)))
        if start == 0:
            dv[...] = part_v
            dk[...] = part_k
        else:
            dv[...] += part_v
            dk[...] += part_k
    d_proj[0, mine] = rope_rows_back(dq[...] * SCALE, cosine, sine).astype(BF16)
    d_proj[1, mine] = rope_rows_back(dk[...].T * SCALE, cosine, sine).astype(BF16)
    d_proj[2, mine] = dv[...].T.astype(BF16)

    @pl.when(h == heads - 3)
    def _():
        other_copy.wait()
        base_copy.wait()
        out_own[...] = (base_in[...] + other_in[...].astype(F32)).astype(BF16)
        out_copy.start()

    ticks = [functools.partial(share.flow.tick, i) for i in range(len(share.pieces) + 1)]
    plan = spread(ticks, heads)
    run_ticks(plan[:-1])

    @pl.when(h == heads - 1)
    def _():
        for copy in load_rows(normed):
            copy.wait()
        one_rows = jnp.ones((8, length), BF16)

        def one_body(i, carry):
            r = pl.ds(pl.multiple_of(i * QB, QB), QB)
            total = dg(d_proj[0, :, r], wv[0], ((0,), (1,)))
            for j in range(1, 3):
                total += dg(d_proj[j, :, r], wv[j], ((0,), (1,)))
            one_ref[r] = total.astype(BF16)
            return carry

        lax.fori_loop(0, length // QB, one_body, 0)
        count = width // QB

        def copy_out(i):
            where = pl.ds(pl.multiple_of(lax.rem(i, count) * QB, QB), QB)
            slot = lax.rem(i, 2)
            return pltpu.make_async_copy(tile_buf.at[slot], qkv_grad.at[i // count, where], ts.at[slot])

        def grad_body(i, carry):
            cols = pl.ds(pl.multiple_of(lax.rem(i, count) * QB, QB), QB)

            @pl.when(i >= 2)
            def _():
                copy_out(i - 2).wait()

            tile_buf[lax.rem(i, 2)] = dg(rows_in[:, cols], d_proj[i // count], ((0,), (1,)), BF16)
            copy_out(i).start()
            return carry

        lax.fori_loop(0, 3 * count, grad_body, 0)
        for i in range(max(0, 3 * count - 2), 3 * count):
            copy_out(i).wait()
        for j in range(3):
            shift_ref[j] = dg(one_rows, d_proj[j], ((1,), (1,)))
        for tick in plan[-1]:
            tick()
        share.drain()
        w_out[...] = w_sum[...]
        out_copy.wait()


def attend_back(lines, low, outf, lse, cosine, sine, ids, weights, normed, mixed, d_attn, w_grad, other, base):
    _, inner, length = low.shape
    width = weights.shape[1]
    local = length // 2
    heads = inner // HDIM
    half = HDIM // 2
    w_rows, quarter = w_grad.shape
    rows = w_rows // (2 * lines)
    head = lambda h: (0, h, 0)
    whole = lambda h: (0, 0)
    cube = lambda h: (0, 0, 0)
    anywhere = pl.BlockSpec(memory_space=pl.ANY)
    dma = pltpu.SemaphoreType.DMA
    shape = jax.ShapeDtypeStruct
    return pl.pallas_call(
        functools.partial(attend_back_kernel, lines, heads),
        grid=(heads,),
        in_specs=[
            pl.BlockSpec((3, HDIM, length), head),
            pl.BlockSpec((HDIM, length), lambda h: (h, 0)),
            pl.BlockSpec((1, 1, length), lambda h: (h, 0, 0)),
            pl.BlockSpec((half, length), whole),
            pl.BlockSpec((half, length), whole),
            pl.BlockSpec((length, 1), whole),
            pl.BlockSpec((1, length), whole),
        ]
        + [anywhere] * 7,
        out_specs=[
            pl.BlockSpec((length, width), whole),
            anywhere,
            pl.BlockSpec((width, inner), whole),
            pl.BlockSpec((3, 8, inner), cube),
            pl.BlockSpec((2, rows, quarter), cube),
            pl.BlockSpec((local, width), whole),
            anywhere,
        ],
        out_shape=[
            shape((length, width), BF16),
            shape((3, width, inner), BF16),
            shape((width, inner), BF16),
            shape((3, 8, inner), F32),
            shape((2, rows, quarter), F32),
            shape((local, width), BF16),
            shape((local, width), BF16),
        ],
        scratch_shapes=[
            pltpu.VMEM((length, length), F32),
            pltpu.VMEM((HDIM, length), F32),
            pltpu.VMEM((length, HDIM), F32),
            pltpu.VMEM((length, HDIM), F32),
            pltpu.VMEM((inner, length), BF16),
            pltpu.VMEM((3, inner, length), BF16),
            pltpu.VMEM(weights.shape, BF16),
            pltpu.VMEM((length, width), BF16),
            pltpu.VMEM((inner, length), BF16),
            pltpu.VMEM((local, width), F32),
            pltpu.VMEM((local, width), BF16),
            pltpu.VMEM((2, QB, inner), BF16),
            pltpu.VMEM((2, rows, quarter), F32),
            dma((5,)), dma((2,)), dma((2,)), dma((2,)),
        ]
        + share_scratch(lines, rows, quarter),
        compiler_params=pltpu.CompilerParams(
            collective_id=4, has_side_effects=True, vmem_limit_bytes=63 << 20
        ),
        cost_estimate=pl.CostEstimate(
            flops=10 * inner * length * length + 20 * inner * length * width,
            transcendentals=heads * length * length,
            bytes_accessed=18 * inner * length,
        ),
        name="attend_back",
    )(low, outf, lse, cosine, sine, ids[:, None], ids[None, :], weights, normed, mixed, d_attn, w_grad, other, base)


def rope_tables(patch_row, patch_col):
    quarter = HDIM // 4
    frequency = ROPE_BASE ** (-2.0 * jnp.arange(quarter, dtype=F32) / (HDIM // 2))
    angles = jnp.concatenate(
        [
            frequency[:, None] * patch_row.astype(F32)[None, :],
            frequency[:, None] * patch_col.astype(F32)[None, :],
        ],
        axis=0,
    )
    return jnp.cos(angles), jnp.sin(angles)


MESH = pl.DeviceIdType.MESH


def remote(src, dst, send_sem, recv_sem, device):
    return pltpu.make_async_remote_copy(
        src_ref=src,
        dst_ref=dst,
        send_sem=send_sem,
        recv_sem=recv_sem,
        device_id=device,
        device_id_type=MESH,
    )


class Place:
    def __init__(self, lines):
        self.lines = lines
        self.s = lax.axis_index("shard")
        self.c = lax.axis_index("ctx")
        self.y = lax.axis_index("tp")
        self.line = self.s // 2
        self.side = lax.rem(self.s, 2)
        self.sib = (self.s, 1 - self.c, self.y)
        self.peer = (self.s, self.c, 1 - self.y)
        self.beside = (self.line * 2 + 1 - self.side, self.c, self.y)

    def ahead(self, k):
        return (lax.rem(self.line + k, self.lines) * 2 + self.side, self.c, self.y)

    def source(self, k):
        return lax.rem(self.line + self.lines - k, self.lines) * 2

    def greet(self):
        barrier = pltpu.get_barrier_semaphore()
        others = [self.sib, self.peer, self.beside] + [self.ahead(k) for k in range(1, self.lines)]
        for other in others:
            pl.semaphore_signal(barrier, inc=1, device_id=other, device_id_type=MESH)
        pl.semaphore_wait(barrier, len(others))


def norm_rows(values):
    center = values - jnp.mean(values, -1, keepdims=True)
    spread = jnp.mean(center * center, -1, keepdims=True)
    return center * lax.rsqrt(spread + NORM_EPS)


def collect_kernel(
    lines, pieces, block, tok, gain, shift, dy, qb,
    out, normed, dy_sib, qb_out,
    norm_buf, own_sem, zs, zr, xs, xr, ys, yr, ms, mr,
):
    at = Place(lines)
    diag = at.c == at.y

    def part(p, s):
        j, first, count, _ = pieces[p]
        rows = block.shape[1]
        return out.at[j, pl.ds(pl.multiple_of(s * rows, rows), rows), pl.ds(first, count)]

    def own(p):
        j, first, count, _ = pieces[p]
        return block.at[j, :, pl.ds(first, count)]

    def z_copy(p, k, src):
        return remote(src, part(p, at.s), zs.at[p, k], zr.at[p, k], at.ahead(k))

    def x_copy(p, k, src):
        return remote(src, part(p, at.source(k) + at.side), xs.at[p, k], xr.at[p, k], at.beside)

    def y_copy(p, i, src, s):
        return remote(src, part(p, s), ys.at[p, i], yr.at[p, i], at.peer)

    def near(k):
        return at.source(k) + at.side

    def far(k):
        return at.source(k) + 1 - at.side

    def z_wait(p, k):
        z_copy(p, k, part(p, near(k))).wait_recv()

    def x_wait(p, k):
        x_copy(p, k, part(p, far(k))).wait_recv()

    def y_wait(p, i, s):
        y_copy(p, i, part(p, s), s).wait_recv()

    late = [p for p in range(len(pieces)) if pieces[p][3]]
    early = [p for p in range(len(pieces)) if not pieces[p][3]]
    order = late + early
    at.greet()

    own_rows = pl.ds(pl.multiple_of(at.s * block.shape[1], block.shape[1]), block.shape[1])
    own_copy = pltpu.make_async_copy(block, out.at[:, own_rows], own_sem.at[0])
    bias_copy = pltpu.make_async_copy(qb, qb_out, own_sem.at[1])

    @pl.when(diag)
    def _():
        own_copy.start()
        bias_copy.start()
        remote(qb, qb_out, ms.at[0], mr.at[0], at.peer).start()
        for p in early:
            y_copy(p, 0, own(p), at.s).start()
        for p in order[:AHEAD]:
            for k in range(1, lines):
                z_copy(p, k, own(p)).start()

    dy_copy = remote(dy, dy_sib, ms.at[1], mr.at[1], at.sib)
    dy_copy.start()
    norm_buf[...] = (norm_rows(tok[...].astype(F32)) * gain[...] + shift[...]).astype(BF16)
    norm_copy = remote(norm_buf, normed.at[at.c], ms.at[2], mr.at[2], at.sib)
    norm_copy.start()
    norm_keep = pltpu.make_async_copy(norm_buf, normed.at[at.c], own_sem.at[2])
    norm_keep.start()

    @pl.when(diag)
    def _():
        for step in range(len(order) + 1):
            if step < len(order):
                p = order[step]
                if step + AHEAD < len(order):
                    for k in range(1, lines):
                        z_copy(order[step + AHEAD], k, own(order[step + AHEAD])).start()
                x_copy(p, 0, own(p)).start()
                if p in late:
                    y_copy(p, 0, own(p), at.s).start()
                for k in range(1, lines):
                    z_wait(p, k)
                    x_copy(p, k, part(p, near(k))).start()
                    if p in late:
                        y_copy(p, k, part(p, near(k)), near(k)).start()
            if step > 0:
                p = order[step - 1]
                for k in range(lines):
                    x_wait(p, k)
                    if p in late:
                        y_copy(p, lines + k, part(p, far(k)), far(k)).start()
        own_copy.wait()
        bias_copy.wait()
        remote(qb, qb_out, ms.at[0], mr.at[0], at.peer).wait_send()
        for p in order:
            for k in range(1, lines):
                z_copy(p, k, own(p)).wait_send()
            for k in range(lines):
                x_copy(p, k, part(p, near(k))).wait_send()
            y_copy(p, 0, own(p), at.s).wait_send()
            if p in late:
                for k in range(1, lines):
                    y_copy(p, k, part(p, near(k)), near(k)).wait_send()
                for k in range(lines):
                    y_copy(p, lines + k, part(p, far(k)), far(k)).wait_send()

    @pl.when(jnp.logical_not(diag))
    def _():
        for p in early:
            y_wait(p, 0, at.s)
            for k in range(1, lines):
                z_copy(p, k, part(p, at.s)).start()
            x_copy(p, 0, part(p, at.s)).start()
        for step in range(len(early) + 1):
            if step < len(early):
                p = early[step]
                for k in range(1, lines):
                    z_wait(p, k)
                    x_copy(p, k, part(p, near(k))).start()
            if step > 0:
                for k in range(lines):
                    x_wait(early[step - 1], k)
        for p in early:
            for k in range(1, lines):
                z_copy(p, k, part(p, at.s)).wait_send()
            for k in range(lines):
                x_copy(p, k, part(p, near(k))).wait_send()
        remote(qb, qb_out, ms.at[0], mr.at[0], at.peer).wait_recv()
        for p in late:
            for k in range(lines):
                y_wait(p, k, near(k))
                y_wait(p, lines + k, far(k))

    dy_copy.wait()
    norm_copy.wait_send()
    remote(norm_buf, normed.at[1 - at.c], ms.at[2], mr.at[2], at.sib).wait_recv()
    norm_keep.wait()


def collect(lines, block, tok, gain, shift, dy, qb):
    groups, rows, inner = block.shape
    local, width = tok.shape
    cut = (inner * 3 // 5) // 128 * 128
    pieces = [(j, f, n, i < 5) for i, (j, f, n) in enumerate((j, f, n) for j in range(4) for f, n in ((0, cut), (cut, inner - cut)))]
    n = len(pieces)
    anywhere = pl.BlockSpec(memory_space=pl.ANY)
    vmem = pl.BlockSpec(memory_space=pltpu.VMEM)
    dma = pltpu.SemaphoreType.DMA
    return pl.pallas_call(
        functools.partial(collect_kernel, lines, pieces),
        in_specs=[anywhere, vmem, vmem, vmem, anywhere, anywhere],
        out_specs=[anywhere] * 4,
        out_shape=[
            jax.ShapeDtypeStruct((groups, 2 * lines * rows, inner), BF16),
            jax.ShapeDtypeStruct((2, local, width), BF16),
            jax.ShapeDtypeStruct(dy.shape, BF16),
            jax.ShapeDtypeStruct(qb.shape, F32),
        ],
        scratch_shapes=[
            pltpu.VMEM((local, width), BF16),
            dma((3,)),
            dma((n, lines)),
            dma((n, lines)),
            dma((n, lines)),
            dma((n, lines)),
            dma((n, 2 * lines)),
            dma((n, 2 * lines)),
            dma((3,)),
            dma((3,)),
        ],
        compiler_params=pltpu.CompilerParams(
            collective_id=0, has_side_effects=True, vmem_limit_bytes=24 << 20
        ),
        name="collect",
    )(block, tok, gain[None], shift[None], dy, qb)


class Gather:
    def __init__(self, at, own, full, pieces, own_sem, zs, zr, xs, xr):
        self.at, self.own, self.full, self.pieces = at, own, full, pieces
        self.own_sem, self.zs, self.zr, self.xs, self.xr = own_sem, zs, zr, xs, xr
        self.rows = own.shape[0]

    def part(self, p, s):
        start, count = self.pieces[p]
        return self.full.at[pl.ds(pl.multiple_of(s * self.rows, self.rows), self.rows), pl.ds(start, count)]

    def z_copy(self, p, k):
        start, count = self.pieces[p]
        src = self.own.at[:, pl.ds(start, count)]
        return remote(src, self.part(p, self.at.s), self.zs.at[p, k], self.zr.at[p, k], self.at.ahead(k))

    def x_copy(self, p, k):
        start, count = self.pieces[p]
        there = self.part(p, self.at.source(k) + self.at.side)
        src = self.own.at[:, pl.ds(start, count)] if k == 0 else there
        return remote(src, there, self.xs.at[p, k], self.xr.at[p, k], self.at.beside)

    def z_wait(self, p, k):
        there = self.part(p, self.at.source(k) + self.at.side)
        remote(there, there, self.zs.at[p, k], self.zr.at[p, k], self.at.ahead(k)).wait_recv()

    def x_wait(self, p, k):
        there = self.part(p, self.at.source(k) + 1 - self.at.side)
        remote(there, there, self.xs.at[p, k], self.xr.at[p, k], self.at.beside).wait_recv()

    def keep(self):
        there = self.full.at[pl.ds(pl.multiple_of(self.at.s * self.rows, self.rows), self.rows)]
        return pltpu.make_async_copy(self.own, there, self.own_sem)

    def begin(self, p):
        if p < len(self.pieces):
            for k in range(1, self.at.lines):
                self.z_copy(p, k).start()

    def start(self):
        self.keep().start()
        for p in range(AHEAD):
            self.begin(p)

    def tick(self, p):
        if p < len(self.pieces):
            self.begin(p + AHEAD)
            self.x_copy(p, 0).start()
            for k in range(1, self.at.lines):
                self.z_wait(p, k)
                self.x_copy(p, k).start()
        if 0 < p <= len(self.pieces):
            for k in range(self.at.lines):
                self.x_wait(p - 1, k)
        if p == len(self.pieces):
            self.keep().wait()

    def drain(self):
        for p in range(len(self.pieces)):
            for k in range(self.at.lines):
                self.x_copy(p, k).wait_send()
                if k > 0:
                    self.z_copy(p, k).wait_send()


class Scatter:
    def __init__(self, at, block, mine, xbuf, zin, xs, xr, zs, zr, load=None):
        self.at, self.block, self.mine, self.xbuf, self.zin = at, block, mine, xbuf, zin
        self.xs, self.xr, self.zs, self.zr, self.load = xs, xr, zs, zr, load

    def x_copy(self, row):
        src = self.block(row, 1 - self.at.side)
        return remote(src, self.xbuf.at[row], self.xs.at[row], self.xr.at[row], self.at.beside)

    def load_copy(self, row):
        return pltpu.make_async_copy(self.block(row, self.at.side), self.mine.at[row], self.load.at[row])

    def z_copy(self, k):
        row = lax.rem(self.at.line + k, self.at.lines)
        return remote(self.mine.at[row], self.zin.at[k], self.zs.at[k], self.zr.at[k], self.at.ahead(k))

    def start(self):
        for row in range(self.at.lines):
            self.x_copy(row).start()
            if self.load is not None:
                self.load_copy(row).start()

    def middle(self):
        for row in range(self.at.lines):
            self.x_copy(row).wait_recv()
            if self.load is not None:
                self.load_copy(row).wait()
                here = self.mine[row]
            else:
                here = self.block(row, self.at.side)[...]
            self.mine[row] = (here.astype(F32) + self.xbuf[row].astype(F32)).astype(BF16)
        for k in range(1, self.at.lines):
            self.z_copy(k).start()

    def finish(self):
        total = self.mine[self.at.line].astype(F32)
        for k in range(1, self.at.lines):
            self.z_copy(k).wait_recv()
            total += self.zin[k].astype(F32)
        return total

    def drain(self):
        for row in range(self.at.lines):
            self.x_copy(row).wait_send()
        for k in range(1, self.at.lines):
            self.z_copy(k).wait_send()


class Flow:
    def __init__(self, units, begin, done):
        self.units, self.begin, self.done = units, begin, done

    def start(self):
        for i in range(min(AHEAD, len(self.units))):
            self.begin(i)

    def tick(self, i):
        count = len(self.units)
        if i < count:
            self.units[i].middle()
            if i + AHEAD < count:
                self.begin(i + AHEAD)
        if 0 < i <= count:
            self.done(i - 1, self.units[i - 1].finish())

    def run(self):
        self.start()
        for i in range(len(self.units) + 1):
            self.tick(i)


class Share:
    def __init__(self, at, grad, out, pieces, mine, xbuf, zin, xs, xr, zs, zr, load, cs, cr):
        rows = out.shape[1]
        self.at, self.out, self.pieces, self.cs, self.cr = at, out, pieces, cs, cr

        def unit(i):
            start, count = pieces[i]

            def block(line, side):
                first = pl.multiple_of((2 * line + side) * rows, rows)
                return grad.at[pl.ds(first, rows), pl.ds(start, count)]

            cut = lambda ref: ref.at[:, :, pl.ds(start, count)]
            return Scatter(
                at, block, cut(mine), cut(xbuf), cut(zin), xs.at[i], xr.at[i], zs.at[i], zr.at[i], load.at[i]
            )

        units = [unit(i) for i in range(len(pieces))]
        self.flow = Flow(units, lambda i: units[i].start(), self.done)

    def share(self, i, core):
        start, count = self.pieces[i]
        here = self.out.at[core, :, pl.ds(start, count)]
        return remote(here, here, self.cs.at[i], self.cr.at[i], self.at.sib)

    def done(self, i, total):
        start, count = self.pieces[i]
        self.out[self.at.c, :, start : start + count] = total
        self.share(i, self.at.c).start()

    def drain(self):
        for i, unit in enumerate(self.flow.units):
            unit.drain()
            self.share(i, self.at.c).wait_send()
            self.share(i, 1 - self.at.c).wait_recv()


def columns_of(quarter):
    return [(start, 256) for start in range(0, quarter, 256)]


def share_scratch(lines, rows, quarter):
    n = len(columns_of(quarter))
    dma = pltpu.SemaphoreType.DMA
    slab = pltpu.VMEM((lines, rows, quarter), BF16)
    return [slab] * 3 + [dma((n, lines))] * 5 + [dma((n,))] * 2


def gather_scratch(lines, quarter):
    n = len(columns_of(quarter))
    dma = pltpu.SemaphoreType.DMA
    return [dma] + [dma((n, lines))] * 4


def settle_kernel(
    lines, pieces, qkv, proj, d_one, d_hid, tok, gain, vec,
    attn_out, grad_own, grad_peer, vec_out,
    here, mine, ax, ai, ay, al, one_in, vown, vbuf, vin,
    hs, axs, axr, azs, azr, ays, ayr, cs, cr, vs, vr, os, orr, ms, mr,
):
    at = Place(lines)
    diag = at.c == at.y
    first = [p for p in range(len(pieces)) if pieces[p][3]]
    last = [p for p in range(len(pieces)) if not pieces[p][3]]

    def cut(ref, p):
        _, start, count, _ = pieces[p]
        return ref.at[..., pl.ds(start, count)]

    def source(p):
        j = pieces[p][0]
        return cut(proj if j == 3 else qkv.at[j], p)

    def local_part(p):
        return cut(here.at[pieces[p][0]], p)

    class Direct(Scatter):
        def __init__(self, p):
            j = pieces[p][0]
            super().__init__(
                at, lambda line, side: local_part(p).at[line, side],
                cut(mine.at[j], p), cut(ax.at[j], p), cut(ai.at[j], p),
                axs.at[p], axr.at[p], azs.at[p], azr.at[p],
            )
            self.p = p

        def x_copy(self, row):
            src = source(self.p).at[row, 1 - at.side]
            return remote(src, self.xbuf.at[row], self.xs.at[row], self.xr.at[row], at.beside)

    def summed(p):
        j = pieces[p][0]
        return Scatter(
            at, lambda line, side: cut(ay.at[j, line, side], p),
            cut(mine.at[j], p), cut(ax.at[j], p), cut(ai.at[j], p),
            axs.at[p], axr.at[p], azs.at[p], azr.at[p],
        )

    def pair_copy(p, half):
        side = (1 - at.side, at.side)[half]
        there = cut(ay.at[pieces[p][0], :, side], p)
        return remote(source(p).at[:, side], there, ays.at[p, half], ayr.at[p, half], at.peer)

    def last_copy(p):
        j = pieces[p][0]
        return remote(cut(al.at[j, 0], p), cut(al.at[j, 1], p), ays.at[p, 0], ayr.at[p, 0], at.peer)

    def attn_share(p):
        there = cut(attn_out.at[pieces[p][0]], p)
        return remote(there, there, cs.at[p], cr.at[p], at.sib)

    order = last + first
    diag_units = [Direct(p) for p in last] + [summed(p) for p in first]
    off_units = [Direct(p) for p in last]

    def diag_begin(i):
        p = order[i]
        if p in first:
            j, start, count, _ = pieces[p]
            for half in range(2):
                pair_copy(p, half).wait_recv()
            for row in range(lines):
                for side in range(2):
                    both = local_part(p)[row, side].astype(F32) + cut(ay.at[j, row, side], p)[...].astype(F32)
                    ay[j, row, side, :, start : start + count] = both.astype(BF16)
        diag_units[i].start()

    def diag_done(i, total):
        p = order[i]
        j, start, count, _ = pieces[p]
        if p in last:
            last_copy(p).wait_recv()
            total = total + cut(al.at[j, 1], p)[...].astype(F32)
        attn_out[j, :, start : start + count] = total
        attn_share(p).start()

    def off_done(i, total):
        j, start, count, _ = pieces[last[i]]
        al[j, 0, :, start : start + count] = total.astype(BF16)
        last_copy(last[i]).start()

    diag_flow = Flow(diag_units, diag_begin, diag_done)
    off_flow = Flow(off_units, lambda i: off_units[i].start(), off_done)

    def ticks(begin, end):
        @pl.when(diag)
        def _():
            for i in range(begin, end):
                diag_flow.tick(i)

        @pl.when(jnp.logical_not(diag))
        def _():
            for i in range(begin, end):
                off_flow.tick(i)

    loads = [
        pltpu.make_async_copy(qkv, here.at[pl.ds(0, 3)], hs.at[0]),
        pltpu.make_async_copy(proj, here.at[3], hs.at[1]),
    ]
    for load in loads:
        load.start()
    at.greet()
    one_copy = remote(d_one.at[1 - at.c], one_in, os, orr, at.sib)
    one_copy.start()

    @pl.when(diag)
    def _():
        for i in range(min(AHEAD, len(last))):
            diag_units[i].start()

    @pl.when(jnp.logical_not(diag))
    def _():
        for p in first:
            for half in range(2):
                pair_copy(p, half).start()
        off_flow.start()

    one_copy.wait_recv()
    local = tok.shape[0]
    tile = TILE
    grad_copies = []
    sums = [jnp.zeros((1, tok.shape[1]), F32) for _ in range(2)]
    for q in range(local // tile):
        r = pl.ds(q * tile, tile)
        value = tok[r].astype(F32)
        center = value - jnp.mean(value, -1, keepdims=True)
        inverse = lax.rsqrt(jnp.mean(center * center, -1, keepdims=True) + NORM_EPS)
        normal = center * inverse
        grad = d_one[at.c, r].astype(F32) + one_in[r].astype(F32)
        grad_own[r] = (d_hid[r] + norm_back(grad, normal, inverse, gain[...])).astype(BF16)
        copy = remote(grad_own.at[r], grad_peer.at[r], ms.at[q], mr.at[q], at.peer)
        grad_copies.append(copy)
        for i, t in enumerate((grad * normal, grad)):
            sums[i] += jnp.sum(t, axis=0, keepdims=True)
    vown[...] = vec[...]
    for i in range(2):
        vown[i : i + 1] = sums[i]

    def small_copy(stage, device):
        src = vown if stage == 0 else vbuf.at[stage - 1]
        return remote(src, vin.at[stage], vs.at[stage], vr.at[stage], device)

    steps = [at.sib, at.peer, at.beside]

    def small_start(stage):
        small_copy(stage, steps[stage]).start()

    def small_add(stage):
        small_copy(stage, steps[stage]).wait_recv()
        before = vown[...] if stage == 0 else vbuf[stage - 1]
        vbuf[stage] = before + vin[stage]

    def line_copy(k):
        return remote(vbuf.at[2], vin.at[3 + at.line], vs.at[2 + k], vr.at[2 + k], at.ahead(k))

    def line_wait(k):
        there = vin.at[3 + at.source(k) // 2]
        remote(vbuf.at[2], there, vs.at[2 + k], vr.at[2 + k], at.ahead(k)).wait_recv()

    small_start(0)
    for load in loads:
        load.wait()
    total_ticks = len(order) + 1
    marks = [total_ticks * i // 5 for i in range(1, 5)]

    @pl.when(diag)
    def _():
        for i in range(len(last), min(AHEAD, len(order))):
            diag_begin(i)

    ticks(0, marks[0])
    for copy in grad_copies:
        copy.start()
    small_add(0)
    small_start(1)
    ticks(marks[0], marks[1])
    small_add(1)
    small_start(2)
    ticks(marks[1], marks[2])
    small_add(2)
    for k in range(1, lines):
        line_copy(k).start()
    vin[3 + at.line] = vbuf[2]
    ticks(marks[2], total_ticks)
    for k in range(1, lines):
        line_wait(k)
    total = vin[3]
    for row in range(1, lines):
        total = total + vin[3 + row]
    vec_out[...] = total

    @pl.when(diag)
    def _():
        for unit in diag_units:
            unit.drain()
        for p in order:
            attn_share(p).wait_send()

    @pl.when(jnp.logical_not(diag))
    def _():
        for unit in off_units:
            unit.drain()
        for p in last:
            last_copy(p).wait_send()
        for p in first:
            for half in range(2):
                pair_copy(p, half).wait_send()
        for p in order:
            attn_share(p).wait_recv()

    for stage in range(3):
        small_copy(stage, steps[stage]).wait_send()
    for k in range(1, lines):
        line_copy(k).wait_send()
    one_copy.wait_send()
    for copy in grad_copies:
        copy.wait()


def settle(lines, qkv, proj, d_one, d_hid, tok, gain, vec):
    _, _, _, rows, inner = qkv.shape
    local, width = tok.shape
    pieces = settle_pieces(inner)
    n = len(pieces)
    tiles = local // TILE
    anywhere = pl.BlockSpec(memory_space=pl.ANY)
    vmem = pl.BlockSpec(memory_space=pltpu.VMEM)
    dma = pltpu.SemaphoreType.DMA
    stage = (4, lines, rows, inner)
    return pl.pallas_call(
        functools.partial(settle_kernel, lines, pieces),
        in_specs=[anywhere] * 2 + [vmem] * 5,
        out_specs=[vmem, vmem, anywhere, vmem],
        out_shape=[
            jax.ShapeDtypeStruct((4, rows, inner), F32),
            jax.ShapeDtypeStruct((local, width), BF16),
            jax.ShapeDtypeStruct((local, width), BF16),
            jax.ShapeDtypeStruct(vec.shape, F32),
        ],
        scratch_shapes=[
            pltpu.VMEM((4, lines, 2, rows, inner), BF16),
            pltpu.VMEM(stage, BF16),
            pltpu.VMEM(stage, BF16),
            pltpu.VMEM(stage, BF16),
            pltpu.VMEM((4, lines, 2, rows, inner), BF16),
            pltpu.VMEM((4, 2, rows, inner), BF16),
            pltpu.VMEM((local, width), BF16),
            pltpu.VMEM(vec.shape, F32),
            pltpu.VMEM((3,) + vec.shape, F32),
            pltpu.VMEM((3 + lines,) + vec.shape, F32),
            dma((2,)),
            dma((n, lines)), dma((n, lines)), dma((n, lines)), dma((n, lines)), dma((n, 2)), dma((n, 2)),
            dma((n,)), dma((n,)), dma((2 + lines,)), dma((2 + lines,)),
            dma, dma, dma((tiles,)), dma((tiles,)),
        ],
        compiler_params=pltpu.CompilerParams(
            collective_id=1, has_side_effects=True, vmem_limit_bytes=60 << 20
        ),
        name="settle",
    )(qkv, proj, d_one, d_hid, tok, gain[None], vec)


def settle_pieces(inner):
    cuts = [(f, min(SLICE, inner - f)) for f in range(0, inner, SLICE)]
    every = [(j, f, n) for j in (3, 0, 1, 2) for f, n in cuts]
    return [(j, f, n, i >= len(every) - FIRST) for i, (j, f, n) in enumerate(every)]


def feed_kernel(
    lines, part, tok, proj_bias, gain, shift, b1, b2, w1_in, w2_own, dy_in, dy_sib,
    d_attn, d_hid, base, mlp_other, g1, g2, g2_out, vec,
    w1, w2, two, dy, act, dpre, hid, sbuf, rbuf, mbuf, ybuf, yin, acc, grad_tile, wide_tile,
    loads, ps, pr, ns, nr, ss, sr, ts, tr, ys, yr, os, dos, dor, gs, outs, keeps,
    own_sem, zs, zr, xs, xr, *share_refs,
):
    at = Place(lines)
    c, y = at.c, at.y
    local = hid.shape[0]
    tiles = local // TILE
    pieces = columns_of(w1.shape[1])
    gather = Gather(at, w2_own, w2, pieces, own_sem, zs, zr, xs, xr)
    share = Share(at, g2, g2_out, pieces, *share_refs)
    gather_ticks = [functools.partial(gather.tick, i) for i in range(len(pieces) + 1)]
    share_ticks = [functools.partial(share.flow.tick, i) for i in range(len(pieces) + 1)]

    def advance(ticks, count=1):
        for _ in range(count):
            if ticks:
                ticks.pop(0)()

    def rows(g, q):
        return pl.ds((g * tiles + q) * TILE, TILE)

    def group(g):
        return pl.ds(g * local, local)

    def near_rows(q):
        return pl.ds(q * TILE, TILE)

    copies = [
        pltpu.make_async_copy(tok, ybuf, loads.at[0]),
        pltpu.make_async_copy(part.at[c], yin, loads.at[1]),
        pltpu.make_async_copy(w1_in, w1, loads.at[2]),
        pltpu.make_async_copy(dy_in.at[y], dy.at[group(0)], loads.at[3]),
        pltpu.make_async_copy(dy_sib.at[y], dy.at[group(1)], loads.at[4]),
        pltpu.make_async_copy(dy_in.at[1 - y], dy.at[group(2)], loads.at[5]),
        pltpu.make_async_copy(dy_sib.at[1 - y], dy.at[group(3)], loads.at[6]),
    ]
    for copy in copies:
        copy.start()
    at.greet()
    part_copy = remote(part.at[1 - c], rbuf.at[0], ps, pr, at.sib)
    part_copy.start()
    gather.start()

    def two_sib(q):
        return remote(two.at[rows(0, q)], two.at[rows(1, q)], ns.at[0, q], nr.at[0, q], at.sib)

    def two_peer(q):
        return remote(two.at[rows(0, q)], two.at[rows(2, q)], ns.at[1, q], nr.at[1, q], at.peer)

    def two_pass(q):
        return remote(two.at[rows(2, q)], two.at[rows(3, q)], ns.at[2, q], nr.at[2, q], at.sib)

    copies[0].wait()
    copies[1].wait()
    part_copy.wait_recv()
    for q in range(tiles):
        r = near_rows(q)
        value = ybuf[r].astype(F32) + yin[r].astype(F32) + rbuf[0, r].astype(F32) + proj_bias[...]
        hid[r] = value
        two[rows(0, q)] = (norm_rows(value) * gain[...] + shift[...]).astype(BF16)
        two_peer(q).start()
        two_sib(q).start()

    def first_layer(start, count):
        def body(i, carry):
            r = pl.ds(pl.multiple_of((start + i) * TILE, TILE), TILE)
            pre = dg(two[r], w1[...], ((1,), (0,))) + b1[...]
            sig = jax.nn.sigmoid(GELU * pre)
            act[r] = (pre * sig).astype(BF16)
            dpre[r] = (sig + GELU * pre * sig * (1.0 - sig)).astype(BF16)
            return carry

        lax.fori_loop(0, count, body, 0)

    copies[2].wait()
    first_layer(0, tiles)
    advance(gather_ticks)
    for q in range(tiles):
        two_sib(q).wait_recv()
    first_layer(tiles, tiles)
    advance(gather_ticks)
    for q in range(tiles):
        two_peer(q).wait_recv()
        two_pass(q).start()
        first_layer(2 * tiles + q, 1)
        advance(gather_ticks)
    for q in range(tiles):
        two_pass(q).wait_recv()
    first_layer(3 * tiles, tiles)
    for copy in copies[3:]:
        copy.wait()

    def weight_grad(left, right, out):
        count = out.shape[0] // TILE

        def copy(i):
            slot = lax.rem(i, 2)
            where = pl.ds(pl.multiple_of(i * TILE, TILE), TILE)
            return pltpu.make_async_copy(grad_tile.at[slot], out.at[where], gs.at[slot])

        def body(i, carry):
            cols = pl.ds(pl.multiple_of(i * TILE, TILE), TILE)

            @pl.when(i >= 2)
            def _():
                copy(i - 2).wait()

            grad_tile[lax.rem(i, 2)] = dg(left[:, cols], right[...], ((0,), (0,))).astype(BF16)
            copy(i).start()
            return carry

        lax.fori_loop(0, count, body, 0)
        for i in range(max(0, count - 2), count):
            copy(i).wait()

    weight_grad(dy, act, g2)
    advance(gather_ticks, len(gather_ticks))
    share.flow.start()

    shift_sum = jnp.zeros((1, b1.shape[1]), F32)

    def to_norm(g, q):
        r = rows(g, q)
        low = (dg(dy[r], w2[...], ((1,), (0,))) * dpre[r].astype(F32)).astype(BF16)
        dpre[r] = low
        return dg(low, w1[...], ((1,), (1,))), jnp.sum(low.astype(F32), axis=0, keepdims=True)

    def swap(kind, q):
        r = near_rows(q)
        return remote(sbuf.at[kind, r], rbuf.at[kind, r], ss.at[kind, q], sr.at[kind, q], at.sib)

    def y_copy(q):
        r = near_rows(q)
        return remote(ybuf.at[r], yin.at[r], ys.at[q], yr.at[q], at.peer)

    for kind in range(2):
        for q in range(tiles):
            r = near_rows(q)
            value, total = to_norm(3 - 2 * kind, q)
            sbuf[kind, r] = value.astype(BF16)
            shift_sum += total
            swap(kind, q).start()
            value, total = to_norm(2 - 2 * kind, q)
            shift_sum += total
            swap(kind, q).wait_recv()
            value += rbuf[kind, r].astype(F32)
            if kind == 0:
                ybuf[r] = value.astype(BF16)
                y_copy(q).start()
            else:
                acc[r] = value
                advance(share_ticks)

    weight_grad(two, dpre, g1)
    advance(share_ticks)

    def swap_out(kind, q):
        r = near_rows(q)
        return remote(sbuf.at[kind, r], mbuf.at[kind, r], ts.at[kind, q], tr.at[kind, q], at.sib)

    def other_out(q):
        r = near_rows(q)
        return pltpu.make_async_copy(mbuf.at[0, r], mlp_other.at[r], outs.at[q])

    def base_out(q):
        return pltpu.make_async_copy(wide_tile.at[q % 2], base.at[near_rows(q)], keeps.at[q])

    for kind in range(2):
        for q in range(tiles):
            r = near_rows(q)
            swap(kind, q).wait_send()
            sbuf[kind, r] = dg(act[rows(3 - 2 * kind, q)], w2[...], ((1,), (1,)), BF16)
            swap_out(kind, q).start()
            value = dg(act[rows(2 - 2 * kind, q)], w2[...], ((1,), (1,)))
            swap_out(kind, q).wait_recv()
            value += mbuf[kind, r].astype(F32)
            if kind == 0:
                mbuf[0, r] = value.astype(BF16)
                other_out(q).start()
            else:
                if q >= 2:
                    base_out(q - 2).wait()
                wide_tile[q % 2] = hid[r] + value + b2[...]
                base_out(q).start()
        advance(share_ticks)

    def attn_copy(q):
        r = near_rows(q)
        return remote(ybuf.at[r], d_attn.at[c, r], dos.at[q], dor.at[q], at.sib)

    def attn_keep(q):
        r = near_rows(q)
        return pltpu.make_async_copy(ybuf.at[r], d_attn.at[c, r], os.at[q])

    def hid_keep(q):
        r = near_rows(q)
        return pltpu.make_async_copy(acc.at[r], d_hid.at[r], os.at[tiles + q])

    sums = [jnp.zeros((1, hid.shape[1]), F32) for _ in range(4)]
    for q in range(tiles):
        r = near_rows(q)
        y_copy(q).wait()
        grad = acc[r] + yin[r].astype(F32)
        value = hid[r]
        center = value - jnp.mean(value, -1, keepdims=True)
        inverse = lax.rsqrt(jnp.mean(center * center, -1, keepdims=True) + NORM_EPS)
        normal = center * inverse
        out_grad = dy[rows(0, q)].astype(F32)
        total = out_grad + norm_back(grad, normal, inverse, gain[...])
        low = total.astype(BF16)
        ybuf[r] = low
        attn_copy(q).start()
        attn_keep(q).start()
        acc[r] = total
        hid_keep(q).start()
        for i, t in enumerate((low.astype(F32), grad * normal, grad, out_grad)):
            sums[i] += jnp.sum(t, axis=0, keepdims=True)
    for i in range(4):
        vec[i : i + 1] = sums[i]
    vec[4:5] = shift_sum
    vec[5:8] = jnp.zeros((3, hid.shape[1]), F32)

    advance(share_ticks, len(share_ticks))
    share.drain()
    gather.drain()
    part_copy.wait_send()
    for q in range(tiles):
        two_sib(q).wait_send()
        two_peer(q).wait_send()
        two_pass(q).wait_send()
        other_out(q).wait()
        if q >= tiles - 2:
            base_out(q).wait()
        for kind in range(2):
            swap_out(kind, q).wait_send()
        attn_copy(q).wait_send()
        attn_keep(q).wait()
        hid_keep(q).wait()
        there = d_attn.at[1 - c, near_rows(q)]
        remote(there, there, dos.at[q], dor.at[q], at.sib).wait_recv()


def feed(lines, part, tok, proj_bias, gain, shift, b1, b2, w1, w2_own, dy, dy_sib):
    local, width = tok.shape
    rows, quarter = w2_own.shape
    tiles = local // TILE
    anywhere = pl.BlockSpec(memory_space=pl.ANY)
    vmem = pl.BlockSpec(memory_space=pltpu.VMEM)
    dma = pltpu.SemaphoreType.DMA
    slots = pltpu.VMEM((local, width), BF16)
    shape = jax.ShapeDtypeStruct
    return pl.pallas_call(
        functools.partial(feed_kernel, lines),
        in_specs=[anywhere] * 2 + [vmem] * 5 + [anywhere] * 4,
        out_specs=[anywhere] * 6 + [vmem] * 2,
        out_shape=[
            shape((2, local, width), BF16),
            shape((local, width), F32),
            shape((local, width), F32),
            shape((local, width), BF16),
            shape((width, quarter), BF16),
            shape((width, quarter), BF16),
            shape((2, rows, quarter), F32),
            shape((8, width), F32),
        ],
        scratch_shapes=[
            pltpu.VMEM((width, quarter), BF16),
            pltpu.VMEM((width, quarter), BF16),
            pltpu.VMEM((4 * local, width), BF16),
            pltpu.VMEM((4 * local, width), BF16),
            pltpu.VMEM((4 * local, quarter), BF16),
            pltpu.VMEM((4 * local, quarter), BF16),
            pltpu.VMEM((local, width), F32),
            pltpu.VMEM((2, local, width), BF16),
            pltpu.VMEM((2, local, width), BF16),
            pltpu.VMEM((2, local, width), BF16),
            slots,
            slots,
            pltpu.VMEM((local, width), F32),
            pltpu.VMEM((2, TILE, quarter), BF16),
            pltpu.VMEM((2, TILE, width), F32),
            dma((7,)), dma, dma,
            dma((3, tiles)), dma((3, tiles)),
            dma((2, tiles)), dma((2, tiles)), dma((2, tiles)), dma((2, tiles)),
            dma((tiles,)), dma((tiles,)), dma((2 * tiles,)), dma((tiles,)), dma((tiles,)), dma((2,)),
            dma((tiles,)), dma((tiles,)),
        ]
        + gather_scratch(lines, quarter)
        + share_scratch(lines, rows, quarter),
        compiler_params=pltpu.CompilerParams(
            collective_id=2, has_side_effects=True, vmem_limit_bytes=63 << 20
        ),
        name="feed",
    )(part, tok, proj_bias[None], gain[None], shift[None], b1[None], b2[None], w1, w2_own, dy, dy_sib)


def norm_back(grad_out, normal, inverse, gain):
    scaled = grad_out * gain
    return inverse * (
        scaled
        - jnp.mean(scaled, -1, keepdims=True)
        - normal * jnp.mean(scaled * normal, -1, keepdims=True)
    )


class Links:
    def __init__(self, shards):
        self.shards = shards
        self.lines = shards // 2
        self.s = lax.axis_index("shard")
        self.c = lax.axis_index("ctx")
        self.y = lax.axis_index("tp")
        self.line = self.s // 2
        self.side = self.s % 2
        self.diag = self.c == self.y

    def send(self, value, target, where=lambda c, y: True):
        flat = lambda s, c, y: (s * 2 + c) * 2 + y
        pairs = []
        for s in range(self.shards):
            for c in range(2):
                for y in range(2):
                    if where(c, y):
                        pairs.append((flat(s, c, y), flat(*target(s, c, y))))
        return lax.ppermute(value, AXES, pairs)

    def across(self, value, where=lambda c, y: True):
        return self.send(value, lambda s, c, y: (s, c, 1 - y), where)


def per_device(
    tokens,
    patch_meta,
    attn_norm_gain,
    attn_norm_bias,
    qkv_weight,
    qkv_bias,
    proj_weight,
    proj_bias,
    mlp_norm_gain,
    mlp_norm_bias,
    fc1_weight,
    fc1_bias,
    fc2_weight,
    fc2_bias,
    cotangent,
    *,
    shards,
):
    net = Links(shards)
    c, y = net.c, net.y
    local = tokens.shape[2]
    width = tokens.shape[3]
    full = patch_meta.shape[3]
    inner = qkv_weight.shape[2]
    rows = width // shards
    quarter = fc1_weight.shape[1] // 2
    pick = lambda t, i, d=0: lax.dynamic_index_in_dim(t, i, d, False)
    mine_or = lambda own, other: jnp.where(net.diag, own, other)

    def both(own, other, index):
        return jnp.where(index == 0, jnp.stack([own, other]), jnp.stack([other, own]))

    attn_block = jnp.concatenate([qkv_weight, proj_weight.T[None]], axis=0)
    grad_out = cotangent.reshape(2, local, width)
    tok = pick(tokens, y).reshape(local, width)
    attn_full, normed, grad_out_sib, bias_qkv = collect(
        net.lines, attn_block, tok, attn_norm_gain, attn_norm_bias, grad_out, qkv_bias
    )
    fc1_block = lax.dynamic_slice_in_dim(fc1_weight, c * quarter, quarter, 1)
    fc2_block = lax.dynamic_slice_in_dim(fc2_weight, c * quarter, quarter, 0).T
    bias_fc1 = lax.dynamic_slice_in_dim(fc1_bias, c * quarter, quarter, 0)

    meta = pick(patch_meta, y, 1).reshape(3, full)
    ids = meta[0]
    cosine, sine = rope_tables(meta[1], meta[2])
    shift = jnp.pad(bias_qkv, ((0, 5), (0, 0)))
    low, mixed, mixed_f, lse, attn_part, fc1_full = attend(
        net.lines, attn_full, normed, shift, cosine, sine, ids, fc1_block
    )
    attn_part = attn_part.reshape(2, local, width)
    d_attn, d_hidden, base, mlp_other, grad_fc1_part, _, fc2_sum, sums_two = feed(
        net.lines, attn_part, tok, proj_bias, mlp_norm_gain, mlp_norm_bias, bias_fc1, fc2_bias,
        fc1_full, fc2_block, grad_out, grad_out_sib,
    )
    d_one_part, grad_qkv_part, grad_proj_part, qkv_shift, fc1_sum, out_own, out_peer = attend_back(
        net.lines, low, mixed_f, lse, cosine, sine, ids, attn_full, normed, mixed, d_attn,
        grad_fc1_part, mlp_other, base,
    )
    d_one_part = d_one_part.reshape(2, local, width)
    qkv_shift = qkv_shift[:, 0]
    block_output = both(out_own, out_peer, y)

    fc1_shift = sums_two[4]
    zero_qkv, zero_fc1 = jnp.zeros_like(qkv_shift), jnp.zeros_like(fc1_shift)
    small = jnp.concatenate(
        [
            jnp.zeros((2 * width,), F32),
            sums_two[0],
            sums_two[1],
            sums_two[2],
            sums_two[3],
            jnp.where(c == 0, qkv_shift, zero_qkv).reshape(-1),
            jnp.where(c == 1, qkv_shift, zero_qkv).reshape(-1),
        ]
        + [jnp.where((y == i) & (c == j), fc1_shift, zero_fc1) for i in range(2) for j in range(2)]
    )
    blocks = (net.lines, 2, rows, inner)
    attn_sum, grad_in, grad_in_peer, small = settle(
        net.lines, grad_qkv_part.reshape((3,) + blocks), grad_proj_part.reshape(blocks), d_one_part,
        d_hidden, tok, attn_norm_gain, small.reshape(-1, width),
    )
    small = small.reshape(-1)
    input_grad = both(grad_in, grad_in_peer, y).astype(F32)
    grad_qkv, grad_proj = attn_sum[:3], attn_sum[3].T
    grad_fc1 = jnp.moveaxis(fc1_sum, 0, 1).reshape(rows, 2 * quarter)
    grad_fc2 = jnp.moveaxis(fc2_sum, 1, 2).reshape(2 * quarter, rows)

    vec = lambda i: small[i * width : (i + 1) * width]
    at = 6 * width
    qkv_shifts = small[at : at + 6 * inner].reshape(2, 3, inner)
    fc1_shifts = small[at + 6 * inner :].reshape(2, 2 * quarter)
    out_shape = tokens.shape
    return (
        block_output.reshape(out_shape),
        input_grad.reshape(out_shape),
        vec(0),
        vec(1),
        grad_qkv,
        pick(qkv_shifts, y),
        grad_proj,
        vec(2),
        vec(3),
        vec(4),
        grad_fc1,
        pick(fc1_shifts, y),
        grad_fc2,
        vec(5),
    )


def solution(mesh):
    slots = P(None, "shard", "ctx", None)
    placed = (
        slots,
        P(None, None, "shard", None),
        P(),
        P(),
        P(None, "shard", "tp"),
        P(None, "tp"),
        P("tp", "shard"),
        P(),
        P(),
        P(),
        P("shard", "tp"),
        P("tp"),
        P("tp", "shard"),
        P(),
        slots,
    )
    return jax.shard_map(
        functools.partial(per_device, shards=mesh.shape["shard"]),
        mesh=mesh,
        in_specs=placed,
        out_specs=(
            slots,
            slots,
            P(),
            P(),
            P(None, "shard", "tp"),
            P(None, "tp"),
            P("tp", "shard"),
            P(),
            P(),
            P(),
            P("shard", "tp"),
            P("tp"),
            P("tp", "shard"),
            P(),
        ),
        check_vma=False,
    )
```

time: 601 us -> 485 us (0.81)
  waiting for transfers between devices: 61 us -> 0 us
  matrix products: 40.3 us -> 0 us
  Pallas kernels: 404 us -> 441 us
  other arithmetic: 33.4 us -> 13.8 us
  local copies, waits for them, and re-layouts: 41.1 us -> 25 us
  starting transfers between devices: 15.3 us -> 0 us
    ppermute x10 -> x0, waiting for transfers between devices: 61 us -> none  [send(): return lax.ppermute(value, AXES, pairs)]
    dot_general x6 -> x0, matrix products: 40.3 us -> none  [the longest x3 13.8 us: dg(): lax.dot_general(left, right, (dims, ((), ())), preferred_element_type=F32)]
    pallas_call x4, Pallas kernels: 336 us -> 373 us  [the longest x1 125 us: feed(): pl.pallas_call(functools.partial(feed_kernel, lines), in_specs=[anywhere]...]
    ppermute x10 -> x0, starting transfers between devices: 15.3 us -> none  [send(): return lax.ppermute(value, AXES, pairs)]
    slice x3 -> x0, local copies, waits for them, and re-layouts: 7.18 us -> none  [the longest x1 3.11 us: per_device(): fc_full[:, i].reshape(width, quarter)]
    reduce_sum x4 -> x0, other arithmetic: 6.84 us -> none  [the longest x1 4.19 us: per_device(): sums = lambda t: jnp.sum(t.astype(F32), axis=0)]
    convert_element_type x2 -> x0, other arithmetic: 6.45 us -> none  [the longest x1 4.67 us: per_device(): grad_in = grad_in.astype(BF16)]
  transfers between devices with their start and end apart: 10 -> 0, of which waited for: 4 -> 0; matrix products, arithmetic and copies ran while one was open for 12% -> 0% of each run, Pallas kernels for 35% -> 0%
where the time goes in v4:
time: 485 us; the launch traced here: 481 us
  Pallas kernels  441 us (91%)
  local copies, waits for them, and re-layouts  25 us (5%)
  other arithmetic  13.8 us (3%)
    pallas_call x1, Pallas kernels, feed(): pl.pallas_call(functools.partial(feed_kernel, lines), in_specs=[anywhere]...  125 us
    pallas_call x1, Pallas kernels, settle(): pl.pallas_call(functools.partial(settle_kernel, lines, pieces), in_specs=...  105 us
    pallas_call x1, Pallas kernels, attend_back(): pl.pallas_call(functools.partial(attend_back_kernel, lines, heads), grid=...  79.7 us
    pallas_call x1, Pallas kernels, collect(): pl.pallas_call(functools.partial(collect_kernel, lines, pieces), in_specs...  67.7 us
    pallas_call x1, Pallas kernels, attend(): pl.pallas_call(functools.partial(attend_kernel, lines, heads), grid=(head...  64.1 us

profile of v4, /device:TPU:0, one launch (start us, length us, event | category | flops | bytes accessed | tf_op | source)
XLA Modules:
  0.0 481.4 jit_solution(13518149490933479476)
XLA Ops:
  0.7 1.3 pad_maximum_fusion.block
  2.0 1.6 dynamic-slice_bitcast_fusion.tok
  4.2 67.7 %collect.1 = (bf16[4,1280,640]{2,1,0:T(8,128)(2,1)S(1)}, bf16[2,512,1280]{2,1,0:T(8,128)(2,1)S(1)}, bf16[2,512,1280]{2,1,0:T(8,128)(2,1)S(1)}, f32[3,640]{1,0:T(4,128)S(1)}) custom-call(bf16[4,160,640]{2,1,0:T(8,128)(2,1)S(1)} %pad_maximum_fusion.block, bf16[512,1280]{1,0:T(8,128)(2,1)S(1)} %dynamic-slice_bitcast_fusion.tok, ...), custom_call_target="tpu_custom_call" | custom-call | tf_op jit(solution)/shard_map/collect/pallas_call | solution.py:600
  71.9 1.0 copy-done.2
  72.9 1.5 copy-done.4
  74.4 2.7 copy-done.7
  77.2 1.5 copy-done.8
  78.7 0.6 pad.4.shift
  79.3 0.6 fusion.9
  80.0 1.3 fusion.1
  81.3 1.0 copy.29.idc_ref
  82.3 0.8 constant_dynamic-slice_fusion.w_own
  83.1 64.1 %attend.1 = (bf16[3,640,1024]{2,1,0:T(8,128)(2,1)}, bf16[640,1024]{1,0:T(8,128)(2,1)}, f32[640,1024]{1,0:T(8,128)}, f32[8,1,1024]{2,1,0:T(1,128)}, bf16[1024,128...) custom-call(bf16[4,1280,640]{2,1,0:T(8,128)(2,1)} %copy-done.7, bf16[2,512,1280]{2,1,0:T(8,128)(2,1)} %copy-done.8, ...), custom_call_target="tpu_custom_call" | custom-call | flops 9395240960 | bytes 17039360 | tf_op jit(solution)/shard_map/attend/pallas_call | solution.py:139
  147.2 0.6 broadcast_in_dim.41.proj_bias
  147.8 0.6 broadcast_in_dim.42.gain
  148.4 0.6 broadcast_in_dim.43.shift
  149.1 0.6 broadcast_in_dim.44.b1
  150.3 0.8 dynamic-slice_bitcast_fusion.1.w2_own
  151.1 124.9 %feed.1 = (bf16[2,512,1280]{2,1,0:T(8,128)(2,1)}, f32[512,1280]{1,0:T(8,128)}, f32[512,1280]{1,0:T(8,128)}, bf16[512,1280]{1,0:T(8,128)(2,1)}, bf16[1280,1280]{1...) custom-call(bf16[2,512,1280]{2,1,0:T(8,128)(2,1)} %bitcast.38, ...), custom_call_target="tpu_custom_call" | custom-call | tf_op jit(solution)/shard_map/feed/pallas_call | solution.py:1347
  276.0 79.7 %attend_back.1 = (bf16[1024,1280]{1,0:T(8,128)(2,1)}, bf16[3,1280,640]{2,1,0:T(8,128)(2,1)}, bf16[1280,640]{1,0:T(8,128)(2,1)}, f32[3,8,640]{2,1,0:T(8,128)}, f3...) custom-call(bf16[3,640,1024]{2,1,0:T(8,128)(2,1)} %get-tuple-element.45.low_ref, ...), custom_call_target="tpu_custom_call" | custom-call | flops 23488102400 | bytes 11796480 | tf_op jit(solution)/shard_map/attend_back/pallas_call | solution.py:333
  355.7 4.0 maximum_select_fusion
  360.0 0.9 fusion.4
  361.0 0.6 reshape.249.vec
  361.6 104.8 %settle.1 = (f32[4,160,640]{2,1,0:T(8,128)}, bf16[512,1280]{1,0:T(8,128)(2,1)}, bf16[512,1280]{1,0:T(8,128)(2,1)}, f32[13,1280]{1,0:T(8,128)}) custom-call(bf16[3,4,2,160,640]{4,3,2,1,0:T(8,128)(2,1)} %bitcast.36, bf16[4,2,160,640]{3,2,1,0:T(8,128)(2,1)} %bitcast.39, bf16[2,512,1280]{2,1,0:T(8,128)(2,1)} %bitcast.37, f32[512,1280]{1,0:T(8,128)} %get-tuple-element.61.d_hid, ...), custom_call_target="tpu_custom_call" | custom-call | tf_op jit(solution)/shard_map/settle/pallas_call | solution.py:1053
  466.4 5.5 %fusion = f32[2,1,512,1280]{3,2,1,0:T(8,128)} fusion(bf16[1,1,512,1280]{3,2,1,0:T(8,128)(2,1)} %bitcast.47, bf16[1,1,512,1280]{3,2,1,0:T(8,128)(2,1)} %bitcast.46, pred[]{:T(512)S(6)} %eq.8), kind=kLoop, calls=%fused_computation.2 | loop fusion | flops 5242880 | bytes 7864321 | tf_op jit(solution)/shard_map/convert_element_type | solution.py:1509
  471.9 0.7 slice_reduce_fusion
  472.5 1.1 slice.96
  473.7 0.6 dynamic-slice_bitcast_fusion.2
  474.3 1.8 slice_bitcast_fusion
  476.1 2.9 copy.33
  479.0 0.6 dynamic-slice_reduce_fusion
  479.6 1.4 copy.34
  (65 shorter events, 1.6 us)
Async XLA Ops:
  0.6 81.7 %copy-start = (bf16[160,2560]{1,0:T(8,128)(2,1)S(1)}, bf16[160,2560]{1,0:T(8,128)(2,1)}, u32[]{:S(2)}) copy-start(bf16[160,2560]{1,0:T(8,128)(2,1)} %param.25) | copy-start | bytes 2457604
  0.7 2.9 copy-start.14
  0.7 3.0 copy-start.15
  0.7 3.0 copy-start.6
  2.0 2.1 copy-start.3
  3.6 75.7 %copy-start.20 = (s32[3,2,1,1024]{3,2,1,0:T(1,128)S(1)}, s32[3,2,1,1024]{3,2,1,0:T(1,128)}, u32[]{:S(2)}) copy-start(s32[3,2,1,1024]{3,2,1,0:T(1,128)} %param.16) | copy-start | bytes 73732
  3.6 77.7 %copy-start.5 = (f32[1,1280]{1,0:T(1,128)}, f32[1,1280]{1,0:T(1,128)S(1)}, u32[]{:S(2)}) copy-start(f32[1,1280]{1,0:T(1,128)S(1)} %broadcast_in_dim.39.gain) | copy-start | bytes 15364
  71.9 1.1 copy-start.2
  72.9 1.5 copy-start.4
  74.4 2.8 copy-start.7
  77.2 1.5 copy-start.8
  83.1 64.1 %copy-start.16 = (f32[1280]{0:T(1024)S(1)}, f32[1280]{0:T(1024)}, u32[]{:S(2)}) copy-start(f32[1280]{0:T(1024)} %param.22) | copy-start | bytes 15364
  83.1 64.7 %copy-start.17 = (f32[1280]{0:T(1024)S(1)}, f32[1280]{0:T(1024)}, u32[]{:S(2)}) copy-start(f32[1280]{0:T(1024)} %param.23) | copy-start | bytes 15364
  83.1 65.3 %copy-start.18 = (f32[1280]{0:T(1024)S(1)}, f32[1280]{0:T(1024)}, u32[]{:S(2)}) copy-start(f32[1280]{0:T(1024)} %param.24) | copy-start | bytes 15364
  83.1 65.9 %copy-start.21 = (f32[2560]{0:T(1024)S(1)}, f32[2560]{0:T(1024)}, u32[]{:S(2)}) copy-start(f32[2560]{0:T(1024)} %param.26) | copy-start | bytes 30724
  83.1 66.6 %copy-start.19 = (f32[1280]{0:T(1024)S(1)}, f32[1280]{0:T(1024)}, u32[]{:S(2)}) copy-start(f32[1280]{0:T(1024)} %param.28) | copy-start | bytes 15364
  83.1 67.2 %copy-start.11 = (bf16[2560,160]{0,1:T(8,128)(2,1)S(1)}, bf16[2560,160]{0,1:T(8,128)(2,1)}, u32[]{:S(2)}) copy-start(bf16[2560,160]{0,1:T(8,128)(2,1)} %param.27) | copy-start | bytes 2457604
  355.7 4.1 copy-start.13
  466.4 5.5 %copy-start.12 = (f32[13,1280]{1,0:T(8,128)S(1)}, f32[13,1280]{1,0:T(8,128)}, u32[]{:S(2)}) copy-start(f32[13,1280]{1,0:T(8,128)} %get-tuple-element.66) | copy-start | bytes 199684
  466.4 6.1 %copy-start.10 = (f32[4,160,640]{2,1,0:T(8,128)S(1)}, f32[4,160,640]{2,1,0:T(8,128)}, u32[]{:S(2)}) copy-start(f32[4,160,640]{2,1,0:T(8,128)} %get-tuple-element.67) | copy-start | bytes 4915204
  473.7 6.0 %copy-start.9 = (f32[2,160,1280]{2,1,0:T(8,128)S(1)}, f32[2,160,1280]{2,1,0:T(8,128)}, u32[]{:S(2)}) copy-start(f32[2,160,1280]{2,1,0:T(8,128)} %get-tuple-element.69) | copy-start | bytes 4915204
  476.1 4.9 %copy-start.1 = (bf16[160,2560]{1,0:T(8,128)(2,1)S(1)}, bf16[160,2560]{1,0:T(8,128)(2,1)}, u32[]{:S(2)}) copy-start(bf16[160,2560]{1,0:T(8,128)(2,1)} %param.25) | copy-start | bytes 2457604

commit v5 on v4

--- a/solution.py
+++ b/solution.py
@@ -20,7 +20,8 @@
 AXES = ("shard", "ctx", "tp")
 QB = 256
 AHEAD = 2
-FIRST = 3
+KEPT = 3
+FIRST = 4
 SLICE = 384
 TILE = 256
 
@@ -48,20 +49,22 @@
 
 
 def at_step(h, action):
-    pl.when(pl.program_id(0) == h)(action)
+    @pl.when(pl.program_id(0) == h)
+    def _():
+        action()
 
 
 def spread(ticks, heads):
     plan = [[] for _ in range(heads)]
     for i, tick in enumerate(ticks):
-        plan[min(i, heads - 1)].append(tick)
+        plan[i * (heads - 1) // max(1, len(ticks) - 1)].append(tick)
     return plan
 
 
 def run_ticks(plan):
     for h, ticks in enumerate(plan):
         if ticks:
-            at_step(h, lambda ticks=ticks: [tick() for tick in ticks] and None)
+            at_step(h, lambda ticks=ticks: [tick() for tick in ticks])
 
 
 def attend_kernel(
@@ -114,6 +117,9 @@
         outf_ref[:, cols] = mixed
         lse_ref[0, :, cols] = peak * factor + jnp.log2(total)
 
+    ticks = [functools.partial(gather.tick, i) for i in range(len(gather.pieces))]
+    run_ticks(spread(ticks, heads))
+
     @pl.when(h == heads - 1)
     def _():
         def body(i, carry):
@@ -122,9 +128,8 @@
             return carry
 
         lax.fori_loop(0, length // QB, body, 0)
-
-    ticks = [functools.partial(gather.tick, i) for i in range(len(gather.pieces) + 1)]
-    run_ticks(spread(ticks + [gather.drain], heads))
+        gather.finish()
+        gather.drain()
 
 
 def attend(lines, weights, normed, shift, cosine, sine, ids, w_own):
@@ -174,7 +179,7 @@
         ]
         + gather_scratch(lines, quarter),
         compiler_params=pltpu.CompilerParams(
-            collective_id=3, has_side_effects=True, vmem_limit_bytes=60 << 20
+            collective_id=3, has_side_effects=True, vmem_limit_bytes=63 << 20
         ),
         cost_estimate=pl.CostEstimate(
             flops=4 * inner * length * length + 8 * inner * length * width,
@@ -187,14 +192,16 @@
 
 def attend_back_kernel(
     lines, heads, low_ref, outf_ref, lse_ref, cos_ref, sin_ref, idc_ref, idr_ref,
-    weights, normed, mixed, d_attn, w_grad, other, base,
+    weights, normed, mixed, d_attn, w_grad, w_grad_two, other, base,
     one_ref, qkv_grad, proj_grad, shift_ref, w_out, out_own, out_peer,
     bias, dq, dk, dv, d_mixed, d_proj, wv, rows_in, mixed_in, base_in, other_in, tile_buf, w_sum,
     loads, ys, yr, ts, *share_refs
 ):
     at = Place(lines)
     h = pl.program_id(0)
-    share = Share(at, w_grad, w_sum, columns_of(w_grad.shape[1]), *share_refs)
+    slices = [(w_grad,) + piece for piece in columns_of(w_grad.shape[1])]
+    slices = [(w_grad_two,) + piece for piece in columns_of(w_grad.shape[1])[KEPT:]] + slices
+    share = Share(at, slices, w_sum, *share_refs)
     length, width = rows_in.shape
     local = length // 2
 
@@ -207,8 +214,14 @@
     mixed_copy = pltpu.make_async_copy(mixed, mixed_in, loads.at[2])
     weight_copy = pltpu.make_async_copy(weights, wv, loads.at[3])
     base_copy = pltpu.make_async_copy(base, base_in, loads.at[4])
-    other_copy = remote(other, other_in, ys.at[0], yr.at[0], at.peer)
-    out_copy = remote(out_own, out_peer, ys.at[1], yr.at[1], at.peer)
+    chunk = local // 2
+    chunks = [pl.ds(q * chunk, chunk) for q in range(2)]
+    other_copies = [
+        remote(other.at[r], other_in.at[r], ys.at[0, q], yr.at[0, q], at.peer) for q, r in enumerate(chunks)
+    ]
+    out_copies = [
+        remote(out_own.at[r], out_peer.at[r], ys.at[1, q], yr.at[1, q], at.peer) for q, r in enumerate(chunks)
+    ]
 
     @pl.when(h == 0)
     def _():
@@ -216,7 +229,7 @@
             copy.start()
         at.greet()
         share.flow.start()
-        other_copy.start()
+        other_copies[0].start()
         for copy in load_rows(d_attn) + [mixed_copy, weight_copy]:
             copy.wait()
         d_mixed[...] = dg(wv[3], rows_in[...], ((0,), (1,)), BF16)
@@ -227,6 +240,7 @@
             return carry
 
         lax.fori_loop(0, width // QB, body, 0)
+        other_copies[1].start()
         for copy in load_rows(normed):
             copy.start()
 
@@ -260,16 +274,26 @@
     d_proj[1, mine] = rope_rows_back(dk[...].T * SCALE, cosine, sine).astype(BF16)
     d_proj[2, mine] = dv[...].T.astype(BF16)
 
-    @pl.when(h == heads - 3)
+    def out_rows(q):
+        r = chunks[q]
+        other_copies[q].wait()
+        out_own[r] = (base_in[r] + other_in[r].astype(F32)).astype(BF16)
+        out_copies[q].start()
+
+    @pl.when(h == 1)
     def _():
-        other_copy.wait()
         base_copy.wait()
-        out_own[...] = (base_in[...] + other_in[...].astype(F32)).astype(BF16)
-        out_copy.start()
-
-    ticks = [functools.partial(share.flow.tick, i) for i in range(len(share.pieces) + 1)]
-    plan = spread(ticks, heads)
-    run_ticks(plan[:-1])
+        out_rows(0)
+
+    @pl.when(h == heads // 2)
+    def _():
+        out_rows(1)
+
+    ticks = share.flow.ticks()
+    early = min(len(ticks), heads // 2 + 1)
+    for i in range(early):
+        at_step(max(0, 2 * i - 1), ticks[i])
+    ticks = ticks[early:]
 
     @pl.when(h == heads - 1)
     def _():
@@ -286,6 +310,8 @@
             return carry
 
         lax.fori_loop(0, length // QB, one_body, 0)
+        for tick in ticks[:1]:
+            tick()
         count = width // QB
 
         def copy_out(i):
@@ -309,14 +335,16 @@
             copy_out(i).wait()
         for j in range(3):
             shift_ref[j] = dg(one_rows, d_proj[j], ((1,), (1,)))
-        for tick in plan[-1]:
+        for tick in ticks[1:]:
             tick()
         share.drain()
         w_out[...] = w_sum[...]
-        out_copy.wait()
-
-
-def attend_back(lines, low, outf, lse, cosine, sine, ids, weights, normed, mixed, d_attn, w_grad, other, base):
+        for copy in out_copies:
+            copy.wait()
+
+
+def attend_back(lines, low, outf, lse, cosine, sine, ids, *arrays):
+    weights, w_grad = arrays[0], arrays[4]
     _, inner, length = low.shape
     width = weights.shape[1]
     local = length // 2
@@ -324,6 +352,8 @@
     half = HDIM // 2
     w_rows, quarter = w_grad.shape
     rows = w_rows // (2 * lines)
+    pieces = columns_of(quarter)[KEPT:] + columns_of(quarter)
+    columns = sum(count for _, count in pieces)
     head = lambda h: (0, h, 0)
     whole = lambda h: (0, 0)
     cube = lambda h: (0, 0, 0)
@@ -342,13 +372,13 @@
             pl.BlockSpec((length, 1), whole),
             pl.BlockSpec((1, length), whole),
         ]
-        + [anywhere] * 7,
+        + [anywhere] * 8,
         out_specs=[
             pl.BlockSpec((length, width), whole),
             anywhere,
             pl.BlockSpec((width, inner), whole),
             pl.BlockSpec((3, 8, inner), cube),
-            pl.BlockSpec((2, rows, quarter), cube),
+            pl.BlockSpec((2, rows, columns), cube),
             pl.BlockSpec((local, width), whole),
             anywhere,
         ],
@@ -357,7 +387,7 @@
             shape((3, width, inner), BF16),
             shape((width, inner), BF16),
             shape((3, 8, inner), F32),
-            shape((2, rows, quarter), F32),
+            shape((2, rows, columns), F32),
             shape((local, width), BF16),
             shape((local, width), BF16),
         ],
@@ -374,10 +404,10 @@
             pltpu.VMEM((local, width), F32),
             pltpu.VMEM((local, width), BF16),
             pltpu.VMEM((2, QB, inner), BF16),
-            pltpu.VMEM((2, rows, quarter), F32),
-            dma((5,)), dma((2,)), dma((2,)), dma((2,)),
+            pltpu.VMEM((2, rows, columns), F32),
+            dma((5,)), dma((2, 2)), dma((2, 2)), dma((2,)),
         ]
-        + share_scratch(lines, rows, quarter),
+        + share_scratch(lines, rows, pieces),
         compiler_params=pltpu.CompilerParams(
             collective_id=4, has_side_effects=True, vmem_limit_bytes=63 << 20
         ),
@@ -387,7 +417,7 @@
             bytes_accessed=18 * inner * length,
         ),
         name="attend_back",
-    )(low, outf, lse, cosine, sine, ids[:, None], ids[None, :], weights, normed, mixed, d_attn, w_grad, other, base)
+    )(low, outf, lse, cosine, sine, ids[:, None], ids[None, :], *arrays)
 
 
 def rope_tables(patch_row, patch_col):
@@ -620,7 +650,7 @@
             dma((3,)),
         ],
         compiler_params=pltpu.CompilerParams(
-            collective_id=0, has_side_effects=True, vmem_limit_bytes=24 << 20
+            collective_id=0, has_side_effects=True, vmem_limit_bytes=63 << 20
         ),
         name="collect",
     )(block, tok, gain[None], shift[None], dy, qb)
@@ -668,19 +698,20 @@
         self.keep().start()
         for p in range(AHEAD):
             self.begin(p)
+        for p in range(len(self.pieces)):
+            self.x_copy(p, 0).start()
 
     def tick(self, p):
-        if p < len(self.pieces):
-            self.begin(p + AHEAD)
-            self.x_copy(p, 0).start()
-            for k in range(1, self.at.lines):
-                self.z_wait(p, k)
-                self.x_copy(p, k).start()
-        if 0 < p <= len(self.pieces):
+        self.begin(p + AHEAD)
+        for k in range(1, self.at.lines):
+            self.z_wait(p, k)
+            self.x_copy(p, k).start()
+
+    def finish(self):
+        for p in range(len(self.pieces)):
             for k in range(self.at.lines):
-                self.x_wait(p - 1, k)
-        if p == len(self.pieces):
-            self.keep().wait()
+                self.x_wait(p, k)
+        self.keep().wait()
 
     def drain(self):
         for p in range(len(self.pieces)):
@@ -739,8 +770,8 @@
 
 
 class Flow:
-    def __init__(self, units, begin, done):
-        self.units, self.begin, self.done = units, begin, done
+    def __init__(self, units, begin, done, lag=1):
+        self.units, self.begin, self.done, self.lag = units, begin, done, lag
 
     def start(self):
         for i in range(min(AHEAD, len(self.units))):
@@ -752,42 +783,41 @@
             self.units[i].middle()
             if i + AHEAD < count:
                 self.begin(i + AHEAD)
-        if 0 < i <= count:
-            self.done(i - 1, self.units[i - 1].finish())
-
-    def run(self):
-        self.start()
-        for i in range(len(self.units) + 1):
-            self.tick(i)
+        if 0 <= i - self.lag < count:
+            self.done(i - self.lag, self.units[i - self.lag].finish())
+
+    def ticks(self):
+        return [functools.partial(self.tick, i) for i in range(len(self.units) + self.lag)]
 
 
 class Share:
-    def __init__(self, at, grad, out, pieces, mine, xbuf, zin, xs, xr, zs, zr, load, cs, cr):
+    def __init__(self, at, slices, out, mine, xbuf, zin, xs, xr, zs, zr, load, cs, cr):
         rows = out.shape[1]
-        self.at, self.out, self.pieces, self.cs, self.cr = at, out, pieces, cs, cr
-
-        def unit(i):
-            start, count = pieces[i]
-
-            def block(line, side):
+        self.at, self.out, self.cs, self.cr = at, out, cs, cr
+        self.places, units, total = [], [], 0
+        for i, (grad, start, count) in enumerate(slices):
+
+            def block(line, side, grad=grad, start=start, count=count):
                 first = pl.multiple_of((2 * line + side) * rows, rows)
                 return grad.at[pl.ds(first, rows), pl.ds(start, count)]
 
-            cut = lambda ref: ref.at[:, :, pl.ds(start, count)]
-            return Scatter(
-                at, block, cut(mine), cut(xbuf), cut(zin), xs.at[i], xr.at[i], zs.at[i], zr.at[i], load.at[i]
+            cut = lambda ref: ref.at[:, :, pl.ds(total, count)]
+            units.append(
+                Scatter(
+                    at, block, cut(mine), cut(xbuf), cut(zin), xs.at[i], xr.at[i], zs.at[i], zr.at[i], load.at[i]
+                )
             )
-
-        units = [unit(i) for i in range(len(pieces))]
-        self.flow = Flow(units, lambda i: units[i].start(), self.done)
+            self.places.append((total, count))
+            total += count
+        self.flow = Flow(units, lambda i: units[i].start(), self.done, lag=2)
 
     def share(self, i, core):
-        start, count = self.pieces[i]
+        start, count = self.places[i]
         here = self.out.at[core, :, pl.ds(start, count)]
         return remote(here, here, self.cs.at[i], self.cr.at[i], self.at.sib)
 
     def done(self, i, total):
-        start, count = self.pieces[i]
+        start, count = self.places[i]
         self.out[self.at.c, :, start : start + count] = total
         self.share(i, self.at.c).start()
 
@@ -802,10 +832,10 @@
     return [(start, 256) for start in range(0, quarter, 256)]
 
 
-def share_scratch(lines, rows, quarter):
-    n = len(columns_of(quarter))
+def share_scratch(lines, rows, pieces):
+    n = len(pieces)
     dma = pltpu.SemaphoreType.DMA
-    slab = pltpu.VMEM((lines, rows, quarter), BF16)
+    slab = pltpu.VMEM((lines, rows, sum(count for _, count in pieces)), BF16)
     return [slab] * 3 + [dma((n, lines))] * 5 + [dma((n,))] * 2
 
 
@@ -891,11 +921,9 @@
     def diag_done(i, total):
         p = order[i]
         j, start, count, _ = pieces[p]
-        if p in last:
-            last_copy(p).wait_recv()
-            total = total + cut(al.at[j, 1], p)[...].astype(F32)
         attn_out[j, :, start : start + count] = total
-        attn_share(p).start()
+        if p in first:
+            attn_share(p).start()
 
     def off_done(i, total):
         j, start, count, _ = pieces[last[i]]
@@ -940,7 +968,7 @@
 
     one_copy.wait_recv()
     local = tok.shape[0]
-    tile = TILE
+    tile = TILE // 2
     grad_copies = []
     sums = [jnp.zeros((1, tok.shape[1]), F32) for _ in range(2)]
     for q in range(local // tile):
@@ -984,27 +1012,29 @@
     for load in loads:
         load.wait()
     total_ticks = len(order) + 1
-    marks = [total_ticks * i // 5 for i in range(1, 5)]
+    small_add(0)
+    small_start(1)
+    for i in range(total_ticks):
+        ticks(i, i + 1)
+        if i >= 1 and grad_copies[i - 1 : i]:
+            grad_copies[i - 1].start()
+        if i == total_ticks // 2:
+            small_add(1)
+            small_start(2)
+        if i == total_ticks - 2:
+            small_add(2)
+            for k in range(1, lines):
+                line_copy(k).start()
+            vin[3 + at.line] = vbuf[2]
 
     @pl.when(diag)
     def _():
-        for i in range(len(last), min(AHEAD, len(order))):
-            diag_begin(i)
-
-    ticks(0, marks[0])
-    for copy in grad_copies:
-        copy.start()
-    small_add(0)
-    small_start(1)
-    ticks(marks[0], marks[1])
-    small_add(1)
-    small_start(2)
-    ticks(marks[1], marks[2])
-    small_add(2)
-    for k in range(1, lines):
-        line_copy(k).start()
-    vin[3 + at.line] = vbuf[2]
-    ticks(marks[2], total_ticks)
+        for p in last:
+            j, start, count, _ = pieces[p]
+            last_copy(p).wait_recv()
+            attn_out[j, :, start : start + count] += cut(al.at[j, 1], p)[...].astype(F32)
+            attn_share(p).start()
+
     for k in range(1, lines):
         line_wait(k)
     total = vin[3]
@@ -1045,7 +1075,7 @@
     local, width = tok.shape
     pieces = settle_pieces(inner)
     n = len(pieces)
-    tiles = local // TILE
+    tiles = local // TILE * 2
     anywhere = pl.BlockSpec(memory_space=pl.ANY)
     vmem = pl.BlockSpec(memory_space=pltpu.VMEM)
     dma = pltpu.SemaphoreType.DMA
@@ -1077,7 +1107,7 @@
             dma, dma, dma((tiles,)), dma((tiles,)),
         ],
         compiler_params=pltpu.CompilerParams(
-            collective_id=1, has_side_effects=True, vmem_limit_bytes=60 << 20
+            collective_id=1, has_side_effects=True, vmem_limit_bytes=63 << 20
         ),
         name="settle",
     )(qkv, proj, d_one, d_hid, tok, gain[None], vec)
@@ -1102,9 +1132,9 @@
     tiles = local // TILE
     pieces = columns_of(w1.shape[1])
     gather = Gather(at, w2_own, w2, pieces, own_sem, zs, zr, xs, xr)
-    share = Share(at, g2, g2_out, pieces, *share_refs)
-    gather_ticks = [functools.partial(gather.tick, i) for i in range(len(pieces) + 1)]
-    share_ticks = [functools.partial(share.flow.tick, i) for i in range(len(pieces) + 1)]
+    share = Share(at, [(g2,) + piece for piece in pieces[:KEPT]], g2_out, *share_refs)
+    gather_ticks = [functools.partial(gather.tick, i) for i in range(len(pieces))]
+    share_ticks = share.flow.ticks()
 
     def advance(ticks, count=1):
         for _ in range(count):
@@ -1208,8 +1238,9 @@
         for i in range(max(0, count - 2), count):
             copy(i).wait()
 
+    advance(gather_ticks, len(gather_ticks))
     weight_grad(dy, act, g2)
-    advance(gather_ticks, len(gather_ticks))
+    gather.finish()
     share.flow.start()
 
     shift_sum = jnp.zeros((1, b1.shape[1]), F32)
@@ -1338,6 +1369,7 @@
 def feed(lines, part, tok, proj_bias, gain, shift, b1, b2, w1, w2_own, dy, dy_sib):
     local, width = tok.shape
     rows, quarter = w2_own.shape
+    kept = columns_of(quarter)[:KEPT]
     tiles = local // TILE
     anywhere = pl.BlockSpec(memory_space=pl.ANY)
     vmem = pl.BlockSpec(memory_space=pltpu.VMEM)
@@ -1355,7 +1387,7 @@
             shape((local, width), BF16),
             shape((width, quarter), BF16),
             shape((width, quarter), BF16),
-            shape((2, rows, quarter), F32),
+            shape((2, rows, sum(n for _, n in kept)), F32),
             shape((8, width), F32),
         ],
         scratch_shapes=[
@@ -1381,7 +1413,7 @@
             dma((tiles,)), dma((tiles,)),
         ]
         + gather_scratch(lines, quarter)
-        + share_scratch(lines, rows, quarter),
+        + share_scratch(lines, rows, kept),
         compiler_params=pltpu.CompilerParams(
             collective_id=2, has_side_effects=True, vmem_limit_bytes=63 << 20
         ),
@@ -1474,14 +1506,17 @@
         net.lines, attn_full, normed, shift, cosine, sine, ids, fc1_block
     )
     attn_part = attn_part.reshape(2, local, width)
-    d_attn, d_hidden, base, mlp_other, grad_fc1_part, _, fc2_sum, sums_two = feed(
+    d_attn, d_hidden, base, mlp_other, grad_fc1_part, grad_fc2_part, fc2_sum, sums_two = feed(
         net.lines, attn_part, tok, proj_bias, mlp_norm_gain, mlp_norm_bias, bias_fc1, fc2_bias,
         fc1_full, fc2_block, grad_out, grad_out_sib,
     )
     d_one_part, grad_qkv_part, grad_proj_part, qkv_shift, fc1_sum, out_own, out_peer = attend_back(
         net.lines, low, mixed_f, lse, cosine, sine, ids, attn_full, normed, mixed, d_attn,
-        grad_fc1_part, mlp_other, base,
+        grad_fc1_part, grad_fc2_part, mlp_other, base,
     )
+    late = fc1_sum.shape[2] - quarter
+    fc2_sum = jnp.concatenate([fc2_sum, fc1_sum[:, :, :late]], axis=2)
+    fc1_sum = fc1_sum[:, :, late:]
     d_one_part = d_one_part.reshape(2, local, width)
     qkv_shift = qkv_shift[:, 0]
     block_output = both(out_own, out_peer, y)

time: 485 us -> 431 us (0.89)
  Pallas kernels: 441 us -> 392 us
  local copies, waits for them, and re-layouts: 25 us -> 20.1 us
    pallas_call x1, Pallas kernels: 105 us -> 85.3 us  [settle(): pl.pallas_call(functools.partial(settle_kernel, lines, pieces), in_specs=...]
    pallas_call x1, Pallas kernels: 125 us -> 108 us  [feed(): pl.pallas_call(functools.partial(feed_kernel, lines), in_specs=[anywhere]...]
    pallas_call x1, Pallas kernels: 64.1 us -> 53.3 us  [attend(): pl.pallas_call(functools.partial(attend_kernel, lines, heads), grid=(head...]
    unnamed x54 -> x47, local copies, waits for them, and re-layouts: 7.42 us -> 1.1 us
where the time goes in v5:
time: 431 us; the launch traced here: 427 us
  Pallas kernels  392 us (91%)
  local copies, waits for them, and re-layouts  20.1 us (5%)
  other arithmetic  13.3 us (3%)
    pallas_call x1, Pallas kernels, feed(): pl.pallas_call(functools.partial(feed_kernel, lines), in_specs=[anywhere]...  108 us
    pallas_call x1, Pallas kernels, settle(): pl.pallas_call(functools.partial(settle_kernel, lines, pieces), in_specs=...  85.3 us
    pallas_call x1, Pallas kernels, attend_back(): pl.pallas_call(functools.partial(attend_back_kernel, lines, heads), grid=...  76.3 us
    pallas_call x1, Pallas kernels, collect(): pl.pallas_call(functools.partial(collect_kernel, lines, pieces), in_specs...  69.6 us
    pallas_call x1, Pallas kernels, attend(): pl.pallas_call(functools.partial(attend_kernel, lines, heads), grid=(head...  53.3 us

profile of v5, /device:TPU:0, one launch (start us, length us, event | category | flops | bytes accessed | tf_op | source)
XLA Modules:
  0.0 427.2 jit_solution(5015065796530485356)
XLA Ops:
  0.7 1.4 fusion.9
  2.3 1.3 fusion.1
  3.6 2.5 dynamic-slice_bitcast_fusion.tok
  6.0 0.6 broadcast_in_dim.39.gain
  6.6 1.0 pad_maximum_fusion.block
  7.6 0.6 broadcast_in_dim.40.shift
  8.2 69.6 %collect.1 = (bf16[4,1280,640]{2,1,0:T(8,128)(2,1)}, bf16[2,512,1280]{2,1,0:T(8,128)(2,1)}, bf16[2,512,1280]{2,1,0:T(8,128)(2,1)}, f32[3,640]{1,0:T(4,128)}) custom-call(bf16[4,160,640]{2,1,0:T(8,128)(2,1)} %pad_maximum_fusion.block, bf16[512,1280]{1,0:T(8,128)(2,1)} %dynamic-slice_bitcast_fusion.tok, f32[1,1280]{1,0:T(1,128)} %broadcast_in_dim.39.gain, ...), custom_call_target="tpu_custom_call" | custom-call | tf_op jit(solution)/shard_map/collect/pallas_call | solution.py:630
  77.8 1.3 pad.4.shift
  79.1 1.0 copy.29.idc_ref
  80.2 0.8 constant_dynamic-slice_fusion.w_own
  81.0 53.3 %attend.1 = (bf16[3,640,1024]{2,1,0:T(8,128)(2,1)}, bf16[640,1024]{1,0:T(8,128)(2,1)}, f32[640,1024]{1,0:T(8,128)}, f32[8,1,1024]{2,1,0:T(1,128)}, bf16[1024,128...) custom-call(bf16[4,1280,640]{2,1,0:T(8,128)(2,1)} %get-tuple-element.43.weights, ...), custom_call_target="tpu_custom_call" | custom-call | flops 9395240960 | bytes 17039360 | tf_op jit(solution)/shard_map/attend/pallas_call | solution.py:144
  134.3 0.8 dynamic-slice_bitcast_fusion.1.w2_own
  135.2 0.6 broadcast_in_dim.44.b1
  135.8 0.6 broadcast_in_dim.41.proj_bias
  136.4 0.6 broadcast_in_dim.42.gain
  138.2 108.0 %feed.1 = (bf16[2,512,1280]{2,1,0:T(8,128)(2,1)}, f32[512,1280]{1,0:T(8,128)}, f32[512,1280]{1,0:T(8,128)}, bf16[512,1280]{1,0:T(8,128)(2,1)}, bf16[1280,1280]{1...) custom-call(bf16[2,512,1280]{2,1,0:T(8,128)(2,1)} %bitcast.40, ...), custom_call_target="tpu_custom_call" | custom-call | tf_op jit(solution)/shard_map/feed/pallas_call | solution.py:1379
  246.1 76.3 %attend_back.1 = (bf16[1024,1280]{1,0:T(8,128)(2,1)}, bf16[3,1280,640]{2,1,0:T(8,128)(2,1)}, bf16[1280,640]{1,0:T(8,128)(2,1)}, f32[3,8,640]{2,1,0:T(8,128)}, f3...) custom-call(bf16[3,640,1024]{2,1,0:T(8,128)(2,1)} %get-tuple-element.46.low_ref, ...), custom_call_target="tpu_custom_call" | custom-call | flops 23488102400 | bytes 11796480 | tf_op jit(solution)/shard_map/attend_back/pallas_call | solution.py:363
  322.4 1.1 slice.113
  323.6 1.3 maximum_bitcast_fusion
  324.9 1.3 copy.34
  326.4 0.9 fusion.4
  327.4 0.6 reshape.249.vec
  328.1 85.3 %settle.1 = (f32[4,160,640]{2,1,0:T(8,128)}, bf16[512,1280]{1,0:T(8,128)(2,1)}, bf16[512,1280]{1,0:T(8,128)(2,1)}, f32[13,1280]{1,0:T(8,128)}) custom-call(bf16[3,4,2,160,640]{4,3,2,1,0:T(8,128)(2,1)} %bitcast.38, bf16[4,2,160,640]{3,2,1,0:T(8,128)(2,1)} %bitcast.41, bf16[2,512,1280]{2,1,0:T(8,128)(2,1)} %bitcast.39, f32[512,1280]{1,0:T(8,128)} %get-tuple-element.63.d_hid, ...), custom_call_target="tpu_custom_call" | custom-call | tf_op jit(solution)/shard_map/settle/pallas_call | solution.py:1083
  413.4 5.4 %fusion = f32[2,1,512,1280]{3,2,1,0:T(8,128)} fusion(bf16[1,1,512,1280]{3,2,1,0:T(8,128)(2,1)} %bitcast.47, bf16[1,1,512,1280]{3,2,1,0:T(8,128)(2,1)} %bitcast.46, pred[]{:T(512)S(6)} %eq.8), kind=kLoop, calls=%fused_computation.2 | loop fusion | flops 5242880 | bytes 7864321 | tf_op jit(solution)/shard_map/convert_element_type | solution.py:1544
  418.9 1.1 slice.102
  420.0 0.8 slice_bitcast_fusion.1
  420.8 0.6 dynamic-slice_reduce_fusion
  421.5 0.6 dynamic-slice_bitcast_fusion.2
  422.1 0.7 slice_reduce_fusion
  422.9 1.3 copy.33
  424.3 0.7 copy-done.5
  425.1 1.7 maximum_select_fusion
  (60 shorter events, 1.9 us)
Async XLA Ops:
  0.6 79.5 %copy-start = (bf16[160,2560]{1,0:T(8,128)(2,1)S(1)}, bf16[160,2560]{1,0:T(8,128)(2,1)}, u32[]{:S(2)}) copy-start(bf16[160,2560]{1,0:T(8,128)(2,1)} %param.25) | copy-start | bytes 2457604
  0.7 5.4 %copy-start.11 = (f32[1280]{0:T(1024)S(1)}, f32[1280]{0:T(1024)}, u32[]{:S(2)}) copy-start(f32[1280]{0:T(1024)} %param.17) | copy-start | bytes 15364
  0.7 5.9 %copy-start.7 = (bf16[640,160]{0,1:T(8,128)(2,1)S(1)}, bf16[640,160]{0,1:T(8,128)(2,1)}, u32[]{:S(2)}) copy-start(bf16[640,160]{0,1:T(8,128)(2,1)} %param.21) | copy-start | bytes 614404
  0.7 5.9 %copy-start.6 = (bf16[3,160,640]{2,1,0:T(8,128)(2,1)S(1)}, bf16[3,160,640]{2,1,0:T(8,128)(2,1)}, u32[]{:S(2)}) copy-start(bf16[3,160,640]{2,1,0:T(8,128)(2,1)} %param.19) | copy-start | bytes 1843204
  0.7 6.9 %copy-start.12 = (f32[1280]{0:T(1024)S(1)}, f32[1280]{0:T(1024)}, u32[]{:S(2)}) copy-start(f32[1280]{0:T(1024)} %param.18) | copy-start | bytes 15364
  81.0 53.3 %copy-start.8 = (bf16[2560,160]{0,1:T(8,128)(2,1)S(1)}, bf16[2560,160]{0,1:T(8,128)(2,1)}, u32[]{:S(2)}) copy-start(bf16[2560,160]{0,1:T(8,128)(2,1)} %param.27) | copy-start | bytes 2457604
  81.0 54.1 %copy-start.17 = (f32[2560]{0:T(1024)S(1)}, f32[2560]{0:T(1024)}, u32[]{:S(2)}) copy-start(f32[2560]{0:T(1024)} %param.26) | copy-start | bytes 30724
  81.0 54.8 %copy-start.13 = (f32[1280]{0:T(1024)S(1)}, f32[1280]{0:T(1024)}, u32[]{:S(2)}) copy-start(f32[1280]{0:T(1024)} %param.22) | copy-start | bytes 15364
  81.0 55.4 %copy-start.14 = (f32[1280]{0:T(1024)S(1)}, f32[1280]{0:T(1024)}, u32[]{:S(2)}) copy-start(f32[1280]{0:T(1024)} %param.23) | copy-start | bytes 15364
  81.0 56.0 %copy-start.15 = (f32[1280]{0:T(1024)S(1)}, f32[1280]{0:T(1024)}, u32[]{:S(2)}) copy-start(f32[1280]{0:T(1024)} %param.24) | copy-start | bytes 15364
  81.0 56.6 %copy-start.16 = (f32[1280]{0:T(1024)S(1)}, f32[1280]{0:T(1024)}, u32[]{:S(2)}) copy-start(f32[1280]{0:T(1024)} %param.28) | copy-start | bytes 15364
  323.6 2.7 copy-start.10
  413.4 5.5 %copy-start.3 = (f32[4,160,640]{2,1,0:T(8,128)S(1)}, f32[4,160,640]{2,1,0:T(8,128)}, u32[]{:S(2)}) copy-start(f32[4,160,640]{2,1,0:T(8,128)} %get-tuple-element.69) | copy-start | bytes 4915204
  418.9 1.9 copy-start.9
  418.9 3.9 copy-start.2
  422.8 1.6 copy-start.4
  422.8 2.3 copy-start.5
  424.2 2.5 copy-start.1

commit v6 on v5

--- a/solution.py
+++ b/solution.py
@@ -18,8 +18,9 @@
 F32 = jnp.float32
 BF16 = jnp.bfloat16
 AXES = ("shard", "ctx", "tp")
-QB = 256
+QB = 512
 AHEAD = 2
+LEAD = 1
 KEPT = 3
 FIRST = 4
 SLICE = 384
@@ -123,11 +124,11 @@
     @pl.when(h == heads - 1)
     def _():
         def body(i, carry):
-            r = pl.ds(pl.multiple_of(i * QB, QB), QB)
+            r = pl.ds(pl.multiple_of(i * TILE, TILE), TILE)
             part_ref[r] = dg(mixed_ref[:, r], wv[3], ((0,), (1,)), BF16)
             return carry
 
-        lax.fori_loop(0, length // QB, body, 0)
+        lax.fori_loop(0, length // TILE, body, 0)
         gather.finish()
         gather.drain()
 
@@ -193,9 +194,9 @@
 def attend_back_kernel(
     lines, heads, low_ref, outf_ref, lse_ref, cos_ref, sin_ref, idc_ref, idr_ref,
     weights, normed, mixed, d_attn, w_grad, w_grad_two, other, base,
-    one_ref, qkv_grad, proj_grad, shift_ref, w_out, out_own, out_peer,
-    bias, dq, dk, dv, d_mixed, d_proj, wv, rows_in, mixed_in, base_in, other_in, tile_buf, w_sum,
-    loads, ys, yr, ts, *share_refs
+    one_ref, qkv_grad, proj_grad, shift_ref, w_out, out_full,
+    bias, dq, dk, dv, d_mixed, d_proj, wv, rows_in, mixed_in, base_in, other_in, out_low, tile_buf, w_sum,
+    loads, ys, yr, ks, ts, *share_refs
 ):
     at = Place(lines)
     h = pl.program_id(0)
@@ -214,13 +215,17 @@
     mixed_copy = pltpu.make_async_copy(mixed, mixed_in, loads.at[2])
     weight_copy = pltpu.make_async_copy(weights, wv, loads.at[3])
     base_copy = pltpu.make_async_copy(base, base_in, loads.at[4])
-    chunk = local // 2
-    chunks = [pl.ds(q * chunk, chunk) for q in range(2)]
+    chunk = local // 4
+    chunks = [pl.ds(q * chunk, chunk) for q in range(4)]
     other_copies = [
         remote(other.at[r], other_in.at[r], ys.at[0, q], yr.at[0, q], at.peer) for q, r in enumerate(chunks)
     ]
     out_copies = [
-        remote(out_own.at[r], out_peer.at[r], ys.at[1, q], yr.at[1, q], at.peer) for q, r in enumerate(chunks)
+        remote(out_low.at[r], out_full.at[at.y, r], ys.at[1, q], yr.at[1, q], at.peer)
+        for q, r in enumerate(chunks)
+    ]
+    out_keeps = [
+        pltpu.make_async_copy(out_low.at[r], out_full.at[at.y, r], ks.at[q]) for q, r in enumerate(chunks)
     ]
 
     @pl.when(h == 0)
@@ -229,18 +234,18 @@
             copy.start()
         at.greet()
         share.flow.start()
-        other_copies[0].start()
+        for copy in other_copies:
+            copy.start()
         for copy in load_rows(d_attn) + [mixed_copy, weight_copy]:
             copy.wait()
         d_mixed[...] = dg(wv[3], rows_in[...], ((0,), (1,)), BF16)
 
         def body(i, carry):
-            cols = pl.ds(pl.multiple_of(i * QB, QB), QB)
+            cols = pl.ds(pl.multiple_of(i * TILE, TILE), TILE)
             proj_grad[cols] = dg(rows_in[:, cols], mixed_in[...], ((0,), (1,)), BF16)
             return carry
 
-        lax.fori_loop(0, width // QB, body, 0)
-        other_copies[1].start()
+        lax.fori_loop(0, width // TILE, body, 0)
         for copy in load_rows(normed):
             copy.start()
 
@@ -276,18 +281,15 @@
 
     def out_rows(q):
         r = chunks[q]
+        if q == 0:
+            base_copy.wait()
         other_copies[q].wait()
-        out_own[r] = (base_in[r] + other_in[r].astype(F32)).astype(BF16)
+        out_low[r] = (base_in[r] + other_in[r].astype(F32)).astype(BF16)
         out_copies[q].start()
-
-    @pl.when(h == 1)
-    def _():
-        base_copy.wait()
-        out_rows(0)
-
-    @pl.when(h == heads // 2)
-    def _():
-        out_rows(1)
+        out_keeps[q].start()
+
+    for q, step in enumerate((0, 1, 3, 5)):
+        at_step(step, functools.partial(out_rows, q))
 
     ticks = share.flow.ticks()
     early = min(len(ticks), heads // 2 + 1)
@@ -302,25 +304,25 @@
         one_rows = jnp.ones((8, length), BF16)
 
         def one_body(i, carry):
-            r = pl.ds(pl.multiple_of(i * QB, QB), QB)
+            r = pl.ds(pl.multiple_of(i * TILE, TILE), TILE)
             total = dg(d_proj[0, :, r], wv[0], ((0,), (1,)))
             for j in range(1, 3):
                 total += dg(d_proj[j, :, r], wv[j], ((0,), (1,)))
             one_ref[r] = total.astype(BF16)
             return carry
 
-        lax.fori_loop(0, length // QB, one_body, 0)
+        lax.fori_loop(0, length // TILE, one_body, 0)
         for tick in ticks[:1]:
             tick()
-        count = width // QB
+        count = width // TILE
 
         def copy_out(i):
-            where = pl.ds(pl.multiple_of(lax.rem(i, count) * QB, QB), QB)
+            where = pl.ds(pl.multiple_of(lax.rem(i, count) * TILE, TILE), TILE)
             slot = lax.rem(i, 2)
             return pltpu.make_async_copy(tile_buf.at[slot], qkv_grad.at[i // count, where], ts.at[slot])
 
         def grad_body(i, carry):
-            cols = pl.ds(pl.multiple_of(lax.rem(i, count) * QB, QB), QB)
+            cols = pl.ds(pl.multiple_of(lax.rem(i, count) * TILE, TILE), TILE)
 
             @pl.when(i >= 2)
             def _():
@@ -339,8 +341,11 @@
             tick()
         share.drain()
         w_out[...] = w_sum[...]
-        for copy in out_copies:
-            copy.wait()
+        for q, r in enumerate(chunks):
+            out_copies[q].wait_send()
+            there = out_full.at[1 - at.y, r]
+            remote(there, there, ys.at[1, q], yr.at[1, q], at.peer).wait_recv()
+            out_keeps[q].wait()
 
 
 def attend_back(lines, low, outf, lse, cosine, sine, ids, *arrays):
@@ -379,7 +384,6 @@
             pl.BlockSpec((width, inner), whole),
             pl.BlockSpec((3, 8, inner), cube),
             pl.BlockSpec((2, rows, columns), cube),
-            pl.BlockSpec((local, width), whole),
             anywhere,
         ],
         out_shape=[
@@ -388,8 +392,7 @@
             shape((width, inner), BF16),
             shape((3, 8, inner), F32),
             shape((2, rows, columns), F32),
-            shape((local, width), BF16),
-            shape((local, width), BF16),
+            shape((2, local, width), BF16),
         ],
         scratch_shapes=[
             pltpu.VMEM((length, length), F32),
@@ -403,9 +406,10 @@
             pltpu.VMEM((inner, length), BF16),
             pltpu.VMEM((local, width), F32),
             pltpu.VMEM((local, width), BF16),
-            pltpu.VMEM((2, QB, inner), BF16),
+            pltpu.VMEM((local, width), BF16),
+            pltpu.VMEM((2, TILE, inner), BF16),
             pltpu.VMEM((2, rows, columns), F32),
-            dma((5,)), dma((2, 2)), dma((2, 2)), dma((2,)),
+            dma((5,)), dma((2, 4)), dma((2, 4)), dma((4,)), dma((2,)),
         ]
         + share_scratch(lines, rows, pieces),
         compiler_params=pltpu.CompilerParams(
@@ -536,7 +540,7 @@
         remote(qb, qb_out, ms.at[0], mr.at[0], at.peer).start()
         for p in early:
             y_copy(p, 0, own(p), at.s).start()
-        for p in order[:AHEAD]:
+        for p in order[:LEAD]:
             for k in range(1, lines):
                 z_copy(p, k, own(p)).start()
 
@@ -553,9 +557,9 @@
         for step in range(len(order) + 1):
             if step < len(order):
                 p = order[step]
-                if step + AHEAD < len(order):
+                if step + LEAD < len(order):
                     for k in range(1, lines):
-                        z_copy(order[step + AHEAD], k, own(order[step + AHEAD])).start()
+                        z_copy(order[step + LEAD], k, own(order[step + LEAD])).start()
                 x_copy(p, 0, own(p)).start()
                 if p in late:
                     y_copy(p, 0, own(p), at.s).start()
@@ -847,9 +851,9 @@
 
 def settle_kernel(
     lines, pieces, qkv, proj, d_one, d_hid, tok, gain, vec,
-    attn_out, grad_own, grad_peer, vec_out,
-    here, mine, ax, ai, ay, al, one_in, vown, vbuf, vin,
-    hs, axs, axr, azs, azr, ays, ayr, cs, cr, vs, vr, os, orr, ms, mr,
+    attn_out, grad_full, vec_out,
+    grad_own, here, mine, ax, ai, ay, al, one_in, vown, vbuf, vin,
+    hs, axs, axr, azs, azr, ays, ayr, cs, cr, vs, vr, os, orr, ms, mr, ks,
 ):
     at = Place(lines)
     diag = at.c == at.y
@@ -969,7 +973,7 @@
     one_copy.wait_recv()
     local = tok.shape[0]
     tile = TILE // 2
-    grad_copies = []
+    grad_copies, grad_keeps = [], []
     sums = [jnp.zeros((1, tok.shape[1]), F32) for _ in range(2)]
     for q in range(local // tile):
         r = pl.ds(q * tile, tile)
@@ -979,7 +983,10 @@
         normal = center * inverse
         grad = d_one[at.c, r].astype(F32) + one_in[r].astype(F32)
         grad_own[r] = (d_hid[r] + norm_back(grad, normal, inverse, gain[...])).astype(BF16)
-        copy = remote(grad_own.at[r], grad_peer.at[r], ms.at[q], mr.at[q], at.peer)
+        copy = remote(grad_own.at[r], grad_full.at[at.y, r], ms.at[q], mr.at[q], at.peer)
+        keep = pltpu.make_async_copy(grad_own.at[r], grad_full.at[at.y, r], ks.at[q])
+        keep.start()
+        grad_keeps.append(keep)
         grad_copies.append(copy)
         for i, t in enumerate((grad * normal, grad)):
             sums[i] += jnp.sum(t, axis=0, keepdims=True)
@@ -1066,8 +1073,11 @@
     for k in range(1, lines):
         line_copy(k).wait_send()
     one_copy.wait_send()
-    for copy in grad_copies:
-        copy.wait()
+    for q, copy in enumerate(grad_copies):
+        copy.wait_send()
+        there = grad_full.at[1 - at.y, pl.ds(q * tile, tile)]
+        remote(there, there, ms.at[q], mr.at[q], at.peer).wait_recv()
+        grad_keeps[q].wait()
 
 
 def settle(lines, qkv, proj, d_one, d_hid, tok, gain, vec):
@@ -1083,14 +1093,14 @@
     return pl.pallas_call(
         functools.partial(settle_kernel, lines, pieces),
         in_specs=[anywhere] * 2 + [vmem] * 5,
-        out_specs=[vmem, vmem, anywhere, vmem],
+        out_specs=[vmem, anywhere, vmem],
         out_shape=[
             jax.ShapeDtypeStruct((4, rows, inner), F32),
-            jax.ShapeDtypeStruct((local, width), BF16),
-            jax.ShapeDtypeStruct((local, width), BF16),
+            jax.ShapeDtypeStruct((2, local, width), BF16),
             jax.ShapeDtypeStruct(vec.shape, F32),
         ],
         scratch_shapes=[
+            pltpu.VMEM((local, width), BF16),
             pltpu.VMEM((4, lines, 2, rows, inner), BF16),
             pltpu.VMEM(stage, BF16),
             pltpu.VMEM(stage, BF16),
@@ -1104,7 +1114,7 @@
             dma((2,)),
             dma((n, lines)), dma((n, lines)), dma((n, lines)), dma((n, lines)), dma((n, 2)), dma((n, 2)),
             dma((n,)), dma((n,)), dma((2 + lines,)), dma((2 + lines,)),
-            dma, dma, dma((tiles,)), dma((tiles,)),
+            dma, dma, dma((tiles,)), dma((tiles,)), dma((tiles,)),
         ],
         compiler_params=pltpu.CompilerParams(
             collective_id=1, has_side_effects=True, vmem_limit_bytes=63 << 20
@@ -1120,13 +1130,14 @@
 
 
 def feed_kernel(
-    lines, part, tok, proj_bias, gain, shift, b1, b2, w1_in, w2_own, dy_in, dy_sib,
+    lines, part, tok, params, w1_in, w2_own, dy_in, dy_sib,
     d_attn, d_hid, base, mlp_other, g1, g2, g2_out, vec,
     w1, w2, two, dy, act, dpre, hid, sbuf, rbuf, mbuf, ybuf, yin, acc, grad_tile, wide_tile,
     loads, ps, pr, ns, nr, ss, sr, ts, tr, ys, yr, os, dos, dor, gs, outs, keeps,
     own_sem, zs, zr, xs, xr, *share_refs,
 ):
     at = Place(lines)
+    proj_bias, gain, shift, b1, b2 = [params.at[pl.ds(i, 1)] for i in range(5)]
     c, y = at.c, at.y
     local = hid.shape[0]
     tiles = local // TILE
@@ -1366,7 +1377,7 @@
         remote(there, there, dos.at[q], dor.at[q], at.sib).wait_recv()
 
 
-def feed(lines, part, tok, proj_bias, gain, shift, b1, b2, w1, w2_own, dy, dy_sib):
+def feed(lines, part, tok, params, w1, w2_own, dy, dy_sib):
     local, width = tok.shape
     rows, quarter = w2_own.shape
     kept = columns_of(quarter)[:KEPT]
@@ -1378,7 +1389,7 @@
     shape = jax.ShapeDtypeStruct
     return pl.pallas_call(
         functools.partial(feed_kernel, lines),
-        in_specs=[anywhere] * 2 + [vmem] * 5 + [anywhere] * 4,
+        in_specs=[anywhere] * 2 + [vmem] + [anywhere] * 4,
         out_specs=[anywhere] * 6 + [vmem] * 2,
         out_shape=[
             shape((2, local, width), BF16),
@@ -1418,7 +1429,7 @@
             collective_id=2, has_side_effects=True, vmem_limit_bytes=63 << 20
         ),
         name="feed",
-    )(part, tok, proj_bias[None], gain[None], shift[None], b1[None], b2[None], w1, w2_own, dy, dy_sib)
+    )(part, tok, params, w1, w2_own, dy, dy_sib)
 
 
 def norm_back(grad_out, normal, inverse, gain):
@@ -1506,11 +1517,11 @@
         net.lines, attn_full, normed, shift, cosine, sine, ids, fc1_block
     )
     attn_part = attn_part.reshape(2, local, width)
+    params = jnp.stack([proj_bias, mlp_norm_gain, mlp_norm_bias, bias_fc1, fc2_bias])
     d_attn, d_hidden, base, mlp_other, grad_fc1_part, grad_fc2_part, fc2_sum, sums_two = feed(
-        net.lines, attn_part, tok, proj_bias, mlp_norm_gain, mlp_norm_bias, bias_fc1, fc2_bias,
-        fc1_full, fc2_block, grad_out, grad_out_sib,
+        net.lines, attn_part, tok, params, fc1_full, fc2_block, grad_out, grad_out_sib,
     )
-    d_one_part, grad_qkv_part, grad_proj_part, qkv_shift, fc1_sum, out_own, out_peer = attend_back(
+    d_one_part, grad_qkv_part, grad_proj_part, qkv_shift, fc1_sum, block_output = attend_back(
         net.lines, low, mixed_f, lse, cosine, sine, ids, attn_full, normed, mixed, d_attn,
         grad_fc1_part, grad_fc2_part, mlp_other, base,
     )
@@ -1519,7 +1530,6 @@
     fc1_sum = fc1_sum[:, :, late:]
     d_one_part = d_one_part.reshape(2, local, width)
     qkv_shift = qkv_shift[:, 0]
-    block_output = both(out_own, out_peer, y)
 
     fc1_shift = sums_two[4]
     zero_qkv, zero_fc1 = jnp.zeros_like(qkv_shift), jnp.zeros_like(fc1_shift)
@@ -1536,12 +1546,12 @@
         + [jnp.where((y == i) & (c == j), fc1_shift, zero_fc1) for i in range(2) for j in range(2)]
     )
     blocks = (net.lines, 2, rows, inner)
-    attn_sum, grad_in, grad_in_peer, small = settle(
+    attn_sum, input_grad, small = settle(
         net.lines, grad_qkv_part.reshape((3,) + blocks), grad_proj_part.reshape(blocks), d_one_part,
         d_hidden, tok, attn_norm_gain, small.reshape(-1, width),
     )
     small = small.reshape(-1)
-    input_grad = both(grad_in, grad_in_peer, y).astype(F32)
+    input_grad = input_grad.astype(F32)
     grad_qkv, grad_proj = attn_sum[:3], attn_sum[3].T
     grad_fc1 = jnp.moveaxis(fc1_sum, 0, 1).reshape(rows, 2 * quarter)
     grad_fc2 = jnp.moveaxis(fc2_sum, 1, 2).reshape(2 * quarter, rows)

time: 431 us -> 419 us (0.972)
  Pallas kernels: 392 us -> 384 us
    convert_element_type x1 -> x0, other arithmetic: 5.45 us -> none  [per_device(): input_grad = both(grad_in, grad_in_peer, y).astype(F32)]
    unnamed x2 -> x3, other arithmetic: 1.32 us -> 5.93 us
where the time goes in v6:
time: 419 us; the launch traced here: 416 us
  Pallas kernels  384 us (92%)
  local copies, waits for them, and re-layouts  19.3 us (5%)
  other arithmetic  10.7 us (3%)
    pallas_call x1, Pallas kernels, feed(): pl.pallas_call(functools.partial(feed_kernel, lines), in_specs=[anywhere]...  106 us
    pallas_call x1, Pallas kernels, settle(): pl.pallas_call(functools.partial(settle_kernel, lines, pieces), in_specs=...  83.8 us
    pallas_call x1, Pallas kernels, attend_back(): pl.pallas_call(functools.partial(attend_back_kernel, lines, heads), grid=...  74.1 us
    pallas_call x1, Pallas kernels, collect(): pl.pallas_call(functools.partial(collect_kernel, lines, pieces), in_specs...  69.6 us
    pallas_call x1, Pallas kernels, attend(): pl.pallas_call(functools.partial(attend_kernel, lines, heads), grid=(head...  51.2 us

profile of v6, /device:TPU:0, one launch (start us, length us, event | category | flops | bytes accessed | tf_op | source)
XLA Modules:
  0.0 415.7 jit_solution(15053319242273883562)
XLA Ops:
  0.7 1.4 fusion.8
  2.3 1.3 fusion
  3.6 2.5 dynamic-slice_bitcast_fusion.tok
  6.0 0.6 broadcast_in_dim.24.gain
  6.6 1.0 pad_maximum_fusion.block
  7.6 0.6 broadcast_in_dim.25.shift
  8.2 69.6 %collect.1 = (bf16[4,1280,640]{2,1,0:T(8,128)(2,1)}, bf16[2,512,1280]{2,1,0:T(8,128)(2,1)}, bf16[2,512,1280]{2,1,0:T(8,128)(2,1)}, f32[3,640]{1,0:T(4,128)}) custom-call(bf16[4,160,640]{2,1,0:T(8,128)(2,1)} %pad_maximum_fusion.block, bf16[512,1280]{1,0:T(8,128)(2,1)} %dynamic-slice_bitcast_fusion.tok, f32[1,1280]{1,0:T(1,128)} %broadcast_in_dim.24.gain, ...), custom_call_target="tpu_custom_call" | custom-call | tf_op jit(solution)/shard_map/collect/pallas_call | solution.py:634
  77.9 1.3 pad.4.shift
  79.2 1.0 copy.31.idc_ref
  80.2 0.8 constant_dynamic-slice_fusion.w_own
  81.0 51.2 %attend.1 = (bf16[3,640,1024]{2,1,0:T(8,128)(2,1)}, bf16[640,1024]{1,0:T(8,128)(2,1)}, f32[640,1024]{1,0:T(8,128)}, f32[8,1,1024]{2,1,0:T(1,128)}, bf16[1024,128...) custom-call(bf16[4,1280,640]{2,1,0:T(8,128)(2,1)} %get-tuple-element.41.weights, ...), custom_call_target="tpu_custom_call" | custom-call | flops 9395240960 | bytes 17039360 | tf_op jit(solution)/shard_map/attend/pallas_call | solution.py:145
  132.2 0.8 dynamic-slice_bitcast_fusion.1.w2_own
  133.1 0.7 stack.23.params
  133.8 105.6 %feed.1 = (bf16[2,512,1280]{2,1,0:T(8,128)(2,1)}, f32[512,1280]{1,0:T(8,128)}, f32[512,1280]{1,0:T(8,128)}, bf16[512,1280]{1,0:T(8,128)(2,1)}, bf16[1280,1280]{1...) custom-call(bf16[2,512,1280]{2,1,0:T(8,128)(2,1)} %bitcast.46, ...), custom_call_target="tpu_custom_call" | custom-call | tf_op jit(solution)/shard_map/feed/pallas_call | solution.py:1390
  239.4 74.1 %attend_back.1 = (bf16[1024,1280]{1,0:T(8,128)(2,1)}, bf16[3,1280,640]{2,1,0:T(8,128)(2,1)}, bf16[1280,640]{1,0:T(8,128)(2,1)}, f32[3,8,640]{2,1,0:T(8,128)}, f3...) custom-call(bf16[3,640,1024]{2,1,0:T(8,128)(2,1)} %get-tuple-element.44.low_ref, ...), custom_call_target="tpu_custom_call" | custom-call | flops 23488102400 | bytes 11796480 | tf_op jit(solution)/shard_map/attend_back/pallas_call | solution.py:368
  313.4 1.1 slice.113
  314.6 1.3 maximum_bitcast_fusion
  315.9 1.3 copy.38
  317.2 0.1 fusion.7
  317.4 0.9 fusion.3
  318.4 0.6 reshape.136.vec
  319.1 83.8 %settle.1 = (f32[4,160,640]{2,1,0:T(8,128)}, bf16[2,512,1280]{2,1,0:T(8,128)(2,1)}, f32[13,1280]{1,0:T(8,128)}) custom-call(bf16[3,4,2,160,640]{4,3,2,1,0:T(8,128)(2,1)} %bitcast.43, bf16[4,2,160,640]{3,2,1,0:T(8,128)(2,1)} %bitcast.47, bf16[2,512,1280]{2,1,0:T(8,128)(2,1)} %bitcast.45, f32[512,1280]{1,0:T(8,128)} %get-tuple-element.60.d_hid, ...), custom_call_target="tpu_custom_call" | custom-call | tf_op jit(solution)/shard_map/settle/pallas_call | solution.py:1093
  402.9 4.6 %bitcast_convert_fusion = f32[2,1,512,1280]{3,2,1,0:T(8,128)} fusion(bf16[2,512,1280]{2,1,0:T(8,128)(2,1)} %get-tuple-element.63), kind=kLoop, calls=%fused_computation | loop fusion | flops 1310720 | bytes 7864320
  407.5 1.1 slice.102
  408.6 0.8 slice_bitcast_fusion.1
  409.5 0.6 dynamic-slice_reduce_fusion
  410.1 0.6 dynamic-slice_bitcast_fusion.2
  410.7 0.7 slice_reduce_fusion
  411.4 0.1 slice_bitcast_fusion
  411.5 1.3 copy.37
  412.9 0.9 copy-done.2
  413.8 1.5 copy.51
  (59 shorter events, 0.4 us)
Async XLA Ops:
  0.6 79.5 %copy-start = (bf16[160,2560]{1,0:T(8,128)(2,1)S(1)}, bf16[160,2560]{1,0:T(8,128)(2,1)}, u32[]{:S(2)}) copy-start(bf16[160,2560]{1,0:T(8,128)(2,1)} %param.25) | copy-start | bytes 2457604
  0.7 5.4 %copy-start.10 = (f32[1280]{0:T(1024)S(1)}, f32[1280]{0:T(1024)}, u32[]{:S(2)}) copy-start(f32[1280]{0:T(1024)} %param.17) | copy-start | bytes 15364
  0.7 5.9 %copy-start.6 = (bf16[640,160]{0,1:T(8,128)(2,1)S(1)}, bf16[640,160]{0,1:T(8,128)(2,1)}, u32[]{:S(2)}) copy-start(bf16[640,160]{0,1:T(8,128)(2,1)} %param.21) | copy-start | bytes 614404
  0.7 5.9 %copy-start.5 = (bf16[3,160,640]{2,1,0:T(8,128)(2,1)S(1)}, bf16[3,160,640]{2,1,0:T(8,128)(2,1)}, u32[]{:S(2)}) copy-start(bf16[3,160,640]{2,1,0:T(8,128)(2,1)} %param.19) | copy-start | bytes 1843204
  0.7 6.9 %copy-start.11 = (f32[1280]{0:T(1024)S(1)}, f32[1280]{0:T(1024)}, u32[]{:S(2)}) copy-start(f32[1280]{0:T(1024)} %param.18) | copy-start | bytes 15364
  81.0 51.2 %copy-start.7 = (bf16[2560,160]{0,1:T(8,128)(2,1)S(1)}, bf16[2560,160]{0,1:T(8,128)(2,1)}, u32[]{:S(2)}) copy-start(bf16[2560,160]{0,1:T(8,128)(2,1)} %param.27) | copy-start | bytes 2457604
  81.0 52.0 %copy-start.16 = (f32[2560]{0:T(1024)S(1)}, f32[2560]{0:T(1024)}, u32[]{:S(2)}) copy-start(f32[2560]{0:T(1024)} %param.26) | copy-start | bytes 30724
  81.0 52.1 %copy-start.12 = (f32[1280]{0:T(1024)S(1)}, f32[1280]{0:T(1024)}, u32[]{:S(2)}) copy-start(f32[1280]{0:T(1024)} %param.22) | copy-start | bytes 15364
  81.0 52.1 %copy-start.13 = (f32[1280]{0:T(1024)S(1)}, f32[1280]{0:T(1024)}, u32[]{:S(2)}) copy-start(f32[1280]{0:T(1024)} %param.23) | copy-start | bytes 15364
  81.0 52.1 %copy-start.14 = (f32[1280]{0:T(1024)S(1)}, f32[1280]{0:T(1024)}, u32[]{:S(2)}) copy-start(f32[1280]{0:T(1024)} %param.24) | copy-start | bytes 15364
  81.0 52.1 %copy-start.15 = (f32[1280]{0:T(1024)S(1)}, f32[1280]{0:T(1024)}, u32[]{:S(2)}) copy-start(f32[1280]{0:T(1024)} %param.28) | copy-start | bytes 15364
  314.6 2.7 copy-start.9
  402.9 4.6 %copy-start.4 = (f32[4,160,640]{2,1,0:T(8,128)S(1)}, f32[4,160,640]{2,1,0:T(8,128)}, u32[]{:S(2)}) copy-start(f32[4,160,640]{2,1,0:T(8,128)} %get-tuple-element.65) | copy-start | bytes 4915204
  407.5 1.9 copy-start.8
  407.5 3.9 copy-start.3
  411.4 2.3 copy-start.2
  412.9 2.4 copy-start.1

commit v7 on v6

--- a/solution.py
+++ b/solution.py
@@ -21,7 +21,7 @@
 QB = 512
 AHEAD = 2
 LEAD = 1
-KEPT = 3
+KEPT = 4
 FIRST = 4
 SLICE = 384
 TILE = 256
@@ -543,6 +543,10 @@
         for p in order[:LEAD]:
             for k in range(1, lines):
                 z_copy(p, k, own(p)).start()
+        for p in order:
+            x_copy(p, 0, own(p)).start()
+            if p in late:
+                y_copy(p, 0, own(p), at.s).start()
 
     dy_copy = remote(dy, dy_sib, ms.at[1], mr.at[1], at.sib)
     dy_copy.start()
@@ -560,9 +564,6 @@
                 if step + LEAD < len(order):
                     for k in range(1, lines):
                         z_copy(order[step + LEAD], k, own(order[step + LEAD])).start()
-                x_copy(p, 0, own(p)).start()
-                if p in late:
-                    y_copy(p, 0, own(p), at.s).start()
                 for k in range(1, lines):
                     z_wait(p, k)
                     x_copy(p, k, part(p, near(k))).start()

time: 419 us -> 407 us (0.971)
  Pallas kernels: 384 us -> 372 us
    pallas_call x1, Pallas kernels: 74.1 us -> 65.4 us  [attend_back(): pl.pallas_call(functools.partial(attend_back_kernel, lines, heads), grid=...]
where the time goes in v7:
time: 407 us; the launch traced here: 404 us
  Pallas kernels  372 us (91%)
  local copies, waits for them, and re-layouts  19.1 us (5%)
  other arithmetic  10.9 us (3%)
    pallas_call x1, Pallas kernels, feed(): pl.pallas_call(functools.partial(feed_kernel, lines), in_specs=[anywhere]...  109 us
    pallas_call x1, Pallas kernels, settle(): pl.pallas_call(functools.partial(settle_kernel, lines, pieces), in_specs=...  81.8 us
    pallas_call x1, Pallas kernels, collect(): pl.pallas_call(functools.partial(collect_kernel, lines, pieces), in_specs...  66.1 us
    pallas_call x1, Pallas kernels, attend_back(): pl.pallas_call(functools.partial(attend_back_kernel, lines, heads), grid=...  65.4 us
    pallas_call x1, Pallas kernels, attend(): pl.pallas_call(functools.partial(attend_kernel, lines, heads), grid=(head...  49.5 us

profile of v7, /device:TPU:0, one launch (start us, length us, event | category | flops | bytes accessed | tf_op | source)
XLA Modules:
  0.0 403.8 jit_solution(18403736732360191215)
XLA Ops:
  0.7 1.4 fusion.8
  2.3 1.3 fusion
  3.6 2.5 dynamic-slice_bitcast_fusion.tok
  6.0 0.6 broadcast_in_dim.24.gain
  6.6 1.0 pad_maximum_fusion.block
  7.6 0.6 broadcast_in_dim.25.shift
  8.2 66.1 %collect.1 = (bf16[4,1280,640]{2,1,0:T(8,128)(2,1)}, bf16[2,512,1280]{2,1,0:T(8,128)(2,1)}, bf16[2,512,1280]{2,1,0:T(8,128)(2,1)}, f32[3,640]{1,0:T(4,128)}) custom-call(bf16[4,160,640]{2,1,0:T(8,128)(2,1)} %pad_maximum_fusion.block, bf16[512,1280]{1,0:T(8,128)(2,1)} %dynamic-slice_bitcast_fusion.tok, f32[1,1280]{1,0:T(1,128)} %broadcast_in_dim.24.gain, ...), custom_call_target="tpu_custom_call" | custom-call | tf_op jit(solution)/shard_map/collect/pallas_call | solution.py:635
  74.3 1.3 pad.4.shift
  75.7 1.0 copy.31.idc_ref
  76.7 0.8 constant_dynamic-slice_fusion.w_own
  77.5 49.5 %attend.1 = (bf16[3,640,1024]{2,1,0:T(8,128)(2,1)}, bf16[640,1024]{1,0:T(8,128)(2,1)}, f32[640,1024]{1,0:T(8,128)}, f32[8,1,1024]{2,1,0:T(1,128)}, bf16[1024,128...) custom-call(bf16[4,1280,640]{2,1,0:T(8,128)(2,1)} %get-tuple-element.41.weights, ...), custom_call_target="tpu_custom_call" | custom-call | flops 9395240960 | bytes 17039360 | tf_op jit(solution)/shard_map/attend/pallas_call | solution.py:145
  127.0 0.8 dynamic-slice_bitcast_fusion.1.w2_own
  128.0 0.7 stack.23.params
  128.7 109.5 %feed.1 = (bf16[2,512,1280]{2,1,0:T(8,128)(2,1)}, f32[512,1280]{1,0:T(8,128)}, f32[512,1280]{1,0:T(8,128)}, bf16[512,1280]{1,0:T(8,128)(2,1)}, bf16[1280,1280]{1...) custom-call(bf16[2,512,1280]{2,1,0:T(8,128)(2,1)} %bitcast.46, ...), custom_call_target="tpu_custom_call" | custom-call | tf_op jit(solution)/shard_map/feed/pallas_call | solution.py:1391
  238.1 65.4 %attend_back.1 = (bf16[1024,1280]{1,0:T(8,128)(2,1)}, bf16[3,1280,640]{2,1,0:T(8,128)(2,1)}, bf16[1280,640]{1,0:T(8,128)(2,1)}, f32[3,8,640]{2,1,0:T(8,128)}, f3...) custom-call(bf16[3,640,1024]{2,1,0:T(8,128)(2,1)} %get-tuple-element.44.low_ref, ...), custom_call_target="tpu_custom_call" | custom-call | flops 23488102400 | bytes 11796480 | tf_op jit(solution)/shard_map/attend_back/pallas_call | solution.py:368
  303.5 1.0 slice.113
  304.5 1.4 maximum_bitcast_fusion
  306.0 1.3 copy.38
  307.3 0.1 fusion.7
  307.5 0.9 fusion.3
  308.5 0.6 reshape.136.vec
  309.1 81.8 %settle.1 = (f32[4,160,640]{2,1,0:T(8,128)}, bf16[2,512,1280]{2,1,0:T(8,128)(2,1)}, f32[13,1280]{1,0:T(8,128)}) custom-call(bf16[3,4,2,160,640]{4,3,2,1,0:T(8,128)(2,1)} %bitcast.43, bf16[4,2,160,640]{3,2,1,0:T(8,128)(2,1)} %bitcast.47, bf16[2,512,1280]{2,1,0:T(8,128)(2,1)} %bitcast.45, f32[512,1280]{1,0:T(8,128)} %get-tuple-element.60.d_hid, ...), custom_call_target="tpu_custom_call" | custom-call | tf_op jit(solution)/shard_map/settle/pallas_call | solution.py:1094
  391.0 4.6 %bitcast_convert_fusion = f32[2,1,512,1280]{3,2,1,0:T(8,128)} fusion(bf16[2,512,1280]{2,1,0:T(8,128)(2,1)} %get-tuple-element.63), kind=kLoop, calls=%fused_computation | loop fusion | flops 1310720 | bytes 7864320
  395.6 1.1 slice.102
  396.7 0.8 slice_bitcast_fusion.1
  397.5 0.6 dynamic-slice_reduce_fusion
  398.2 0.6 dynamic-slice_bitcast_fusion.2
  398.8 0.7 slice_reduce_fusion
  399.5 0.1 slice_bitcast_fusion
  399.6 1.3 copy.37
  400.9 0.9 copy-done.2
  401.8 1.5 copy.51
  (59 shorter events, 0.4 us)
Async XLA Ops:
  0.6 76.0 %copy-start = (bf16[160,2560]{1,0:T(8,128)(2,1)S(1)}, bf16[160,2560]{1,0:T(8,128)(2,1)}, u32[]{:S(2)}) copy-start(bf16[160,2560]{1,0:T(8,128)(2,1)} %param.25) | copy-start | bytes 2457604
  0.7 5.4 %copy-start.10 = (f32[1280]{0:T(1024)S(1)}, f32[1280]{0:T(1024)}, u32[]{:S(2)}) copy-start(f32[1280]{0:T(1024)} %param.17) | copy-start | bytes 15364
  0.7 5.9 %copy-start.6 = (bf16[640,160]{0,1:T(8,128)(2,1)S(1)}, bf16[640,160]{0,1:T(8,128)(2,1)}, u32[]{:S(2)}) copy-start(bf16[640,160]{0,1:T(8,128)(2,1)} %param.21) | copy-start | bytes 614404
  0.7 5.9 %copy-start.5 = (bf16[3,160,640]{2,1,0:T(8,128)(2,1)S(1)}, bf16[3,160,640]{2,1,0:T(8,128)(2,1)}, u32[]{:S(2)}) copy-start(bf16[3,160,640]{2,1,0:T(8,128)(2,1)} %param.19) | copy-start | bytes 1843204
  0.7 6.9 %copy-start.11 = (f32[1280]{0:T(1024)S(1)}, f32[1280]{0:T(1024)}, u32[]{:S(2)}) copy-start(f32[1280]{0:T(1024)} %param.18) | copy-start | bytes 15364
  77.5 49.6 %copy-start.7 = (bf16[2560,160]{0,1:T(8,128)(2,1)S(1)}, bf16[2560,160]{0,1:T(8,128)(2,1)}, u32[]{:S(2)}) copy-start(bf16[2560,160]{0,1:T(8,128)(2,1)} %param.27) | copy-start | bytes 2457604
  77.5 50.4 %copy-start.16 = (f32[2560]{0:T(1024)S(1)}, f32[2560]{0:T(1024)}, u32[]{:S(2)}) copy-start(f32[2560]{0:T(1024)} %param.26) | copy-start | bytes 30724
  77.5 50.5 %copy-start.12 = (f32[1280]{0:T(1024)S(1)}, f32[1280]{0:T(1024)}, u32[]{:S(2)}) copy-start(f32[1280]{0:T(1024)} %param.22) | copy-start | bytes 15364
  77.5 50.5 %copy-start.13 = (f32[1280]{0:T(1024)S(1)}, f32[1280]{0:T(1024)}, u32[]{:S(2)}) copy-start(f32[1280]{0:T(1024)} %param.23) | copy-start | bytes 15364
  77.5 50.5 %copy-start.14 = (f32[1280]{0:T(1024)S(1)}, f32[1280]{0:T(1024)}, u32[]{:S(2)}) copy-start(f32[1280]{0:T(1024)} %param.24) | copy-start | bytes 15364
  77.5 50.5 %copy-start.15 = (f32[1280]{0:T(1024)S(1)}, f32[1280]{0:T(1024)}, u32[]{:S(2)}) copy-start(f32[1280]{0:T(1024)} %param.28) | copy-start | bytes 15364
  304.5 2.8 copy-start.9
  391.0 4.6 %copy-start.4 = (f32[4,160,640]{2,1,0:T(8,128)S(1)}, f32[4,160,640]{2,1,0:T(8,128)}, u32[]{:S(2)}) copy-start(f32[4,160,640]{2,1,0:T(8,128)} %get-tuple-element.65) | copy-start | bytes 4915204
  395.6 1.9 copy-start.8
  395.6 3.9 copy-start.3
  399.5 2.3 copy-start.2
  400.9 2.4 copy-start.1
